TPU v7x, 32 devices: a whole 2x2x4 slice. The times are simulated.
32 devices in a mesh: rep: 2 (over x), seq: 2 (over y), ctx: 8 (over z, core).
Axes of the slice: x: 2, y: 2, z: 4, core: 2. Of those that a mesh axis runs over, the one named last changes fastest.
Arguments:
- tokens: bfloat16 [4, 1024, 768], P(('rep', 'seq'), 'ctx'), may hold values from -6 to 6
- segments: int32 [4, 1024], P(('rep', 'seq')), may hold values from 0 to 7, never falling along the last dimension, each value on 1 to 768 neighbouring positions
- joined_weight: bfloat16 [768, 2304], P(('seq', 'ctx')), may hold values from -0.21875 to 0.21875
- query_bias: bfloat16 [768], P(('seq', 'ctx')), may hold values from -3 to 3
- value_bias: bfloat16 [768], P(('seq', 'ctx')), may hold values from -0.59765625 to 0.59765625
- output_weight: bfloat16 [768, 768], P(('seq', 'ctx')), may hold values from -0.875 to 0.875
- output_bias: bfloat16 [768], P(('seq', 'ctx')), may hold values from -2 to 2
- first_gain: bfloat16 [768], P(('seq', 'ctx')), may hold values from 0.5 to 1.5
- first_shift: bfloat16 [768], P(('seq', 'ctx')), may hold values from -2 to 2
- widen_weight: bfloat16 [768, 6144], P(('seq', 'ctx')), may hold values from -0.21875 to 0.21875
- widen_bias: bfloat16 [6144], P(('seq', 'ctx')), may hold values from -2 to 2
- narrow_weight: bfloat16 [3072, 768], P(('seq', 'ctx')), may hold values from -0.15625 to 0.15625
- narrow_bias: bfloat16 [768], P(('seq', 'ctx')), may hold values from -2 to 2
- final_gain: bfloat16 [768], P(('seq', 'ctx')), may hold values from 0.5 to 1.5
- final_shift: bfloat16 [768], P(('seq', 'ctx')), may hold values from -2 to 2
- cotangent: bfloat16 [4, 1024, 768], P(('rep', 'seq'), 'ctx'), may hold values from -6 to 6
Outputs:
- layer_output: bfloat16 [4, 1024, 768], P(('rep', 'seq'), 'ctx')
- tokens_grad: float32 [4, 1024, 768], P(('rep', 'seq'), 'ctx')
- joined_weight_grad: float32 [768, 2304], P(('seq', 'ctx'))
- query_bias_grad: float32 [768], P(('seq', 'ctx'))
- value_bias_grad: float32 [768], P(('seq', 'ctx'))
- output_weight_grad: float32 [768, 768], P(('seq', 'ctx'))
- output_bias_grad: float32 [768], P(('seq', 'ctx'))
- first_gain_grad: float32 [768], P(('seq', 'ctx'))
- first_shift_grad: float32 [768], P(('seq', 'ctx'))
- widen_weight_grad: float32 [768, 6144], P(('seq', 'ctx'))
- widen_bias_grad: float32 [6144], P(('seq', 'ctx'))
- narrow_weight_grad: float32 [3072, 768], P(('seq', 'ctx'))
- narrow_bias_grad: float32 [768], P(('seq', 'ctx'))
- final_gain_grad: float32 [768], P(('seq', 'ctx'))
- final_shift_grad: float32 [768], P(('seq', 'ctx'))
Inputs may be any that keep to these rules, and one draw needn't show every extreme that they name: `segments`: in each sequence the document ids never fall, each of the 8 documents holds 1 to 768 tokens, and one holds exactly 768.
All inputs are finite; a program needn't handle non-finite values.
Results may differ from a plain program's by a relative error of at most 0.03.
Values may be sent and summed in bfloat16 or wider, within the bound.
No kernel may reach another device: no remote copies, remote signals or barrier semaphores. Data moves between devices by JAX's collectives and lax.ppermute only.
A program may use at most 256 MiB of HBM per device.

v0:
```python
import math

import jax
import jax.numpy as jnp
from jax import lax
from jax.sharding import PartitionSpec as P

HEAD_DIM = 64


def normalize(value, gain, shift):
    centre = jnp.mean(value, axis=-1, keepdims=True)
    centred = value - centre
    spread = jnp.mean(centred * centred, axis=-1, keepdims=True)
    return centred * lax.rsqrt(spread + 1e-06) * gain + shift


def activate(gate_up):
    half = gate_up.shape[1] // 2
    return jax.nn.gelu(gate_up[:, :half], approximate=False) * gate_up[:, half:]


def matmul(left, right):
    return jnp.dot(left, right, preferred_element_type=jnp.float32)


def matmul_left(left, right):
    return lax.dot_general(
        left, right, (((0,), (0,)), ((), ())), preferred_element_type=jnp.float32
    )


def matmul_right(left, right):
    return lax.dot_general(
        left, right, (((1,), (1,)), ((), ())), preferred_element_type=jnp.float32
    )


def alibi_slopes(heads, length):
    order = jnp.arange(heads, dtype=jnp.float32) + 1.0
    return jnp.power(2.0, -8.0 * order / heads) * (512.0 / length)


def block_scores(query_heads, key_heads, query_pos, key_pos, query_seg, key_seg, slopes):
    raw = jnp.einsum("qhd,khd->hqk", query_heads, key_heads, preferred_element_type=jnp.float32)
    distance = jnp.abs(query_pos[:, None] - key_pos[None, :]).astype(jnp.float32)
    scores = raw - slopes[:, None, None] * distance[None]
    same = (query_seg[:, None] == key_seg[None, :])[None]
    return jnp.where(same, scores, -jnp.inf)


def block_grads(
    query_heads,
    back_heads,
    log_total,
    row_dot,
    query_pos,
    query_seg,
    key_heads,
    value_heads,
    key_pos,
    key_seg,
    slopes,
    want_query,
    want_keys,
):
    scores = block_scores(query_heads, key_heads, query_pos, key_pos, query_seg, key_seg, slopes)
    probs = jnp.exp(scores - log_total[:, :, None])
    prob_back = jnp.einsum(
        "qhd,khd->hqk", back_heads, value_heads, preferred_element_type=jnp.float32
    )
    score_back = (probs * (prob_back - row_dot[:, :, None])).astype(jnp.bfloat16)
    query_part = None
    key_part = None
    if want_query:
        query_part = jnp.einsum(
            "hqk,khd->qhd", score_back, key_heads, preferred_element_type=jnp.float32
        )
    if want_keys:
        count = key_heads.shape[0]
        probs_low = probs.astype(jnp.bfloat16)
        value_part = jnp.einsum(
            "hqk,qhd->khd", probs_low, back_heads, preferred_element_type=jnp.float32
        )
        key_grad = jnp.einsum(
            "hqk,qhd->khd", score_back, query_heads, preferred_element_type=jnp.float32
        )
        key_part = jnp.concatenate(
            [key_grad.reshape(count, -1), value_part.reshape(count, -1)], axis=1
        )
    return (query_part, key_part)


def owner_total(received, owners):
    return jnp.sum(received.reshape(received.shape[0], owners, -1), axis=1)


def on_device(
    tokens,
    segments,
    joined_weight,
    query_bias,
    value_bias,
    output_weight,
    output_bias,
    first_gain,
    first_shift,
    widen_weight,
    widen_bias,
    narrow_weight,
    narrow_bias,
    final_gain,
    final_shift,
    cotangent,
):
    rows = tokens.shape[1]
    width = tokens.shape[2]
    heads = width // HEAD_DIM
    seg_row = segments[0]
    length = seg_row.shape[0]
    slopes = alibi_slopes(heads, length)
    here = lax.axis_index("ctx") * rows
    local_pos = here + jnp.arange(rows, dtype=jnp.int32)
    local_seg = lax.dynamic_slice_in_dim(seg_row, here, rows, 0)
    lowest_seg = local_seg[0]
    highest_seg = local_seg[rows - 1]
    scale = 1.0 / math.sqrt(HEAD_DIM)
    full = (
        lax.all_gather(joined_weight, ("seq", "ctx"), axis=0, tiled=True),
        lax.all_gather(query_bias, ("seq", "ctx"), axis=0, tiled=True),
        lax.all_gather(value_bias, ("seq", "ctx"), axis=0, tiled=True),
        lax.all_gather(output_weight, ("seq", "ctx"), axis=0, tiled=True),
        lax.all_gather(output_bias, ("seq", "ctx"), axis=0, tiled=True),
        lax.all_gather(first_gain, ("seq", "ctx"), axis=0, tiled=True),
        lax.all_gather(first_shift, ("seq", "ctx"), axis=0, tiled=True),
        lax.all_gather(widen_weight, ("seq", "ctx"), axis=0, tiled=True),
        lax.all_gather(widen_bias, ("seq", "ctx"), axis=0, tiled=True),
        lax.all_gather(narrow_weight, ("seq", "ctx"), axis=0, tiled=True),
        lax.all_gather(narrow_bias, ("seq", "ctx"), axis=0, tiled=True),
        lax.all_gather(final_gain, ("seq", "ctx"), axis=0, tiled=True),
        lax.all_gather(final_shift, ("seq", "ctx"), axis=0, tiled=True),
    )
    (
        w_joined,
        b_query,
        b_value,
        w_output,
        b_output,
        g_first,
        s_first,
        w_widen,
        b_widen,
        w_narrow,
        b_narrow,
        g_final,
        s_final,
    ) = full
    inputs = tokens[0]
    joined = matmul(inputs, w_joined)
    queries = ((joined[:, :width] + b_query) * scale).astype(jnp.bfloat16)
    keys = joined[:, width : 2 * width].astype(jnp.bfloat16)
    values = (joined[:, 2 * width :] + b_value).astype(jnp.bfloat16)
    query_heads = queries.reshape(rows, heads, HEAD_DIM)
    key_value = jnp.concatenate([keys, values], axis=1)

    def counted_range(seg_block, block):
        return (seg_block[block - 1] >= lowest_seg) & (seg_block[0] <= highest_seg)

    start_state = (
        jnp.full((heads, rows), -1e30, jnp.float32),
        jnp.zeros((heads, rows), jnp.float32),
        jnp.zeros((heads, rows, HEAD_DIM), jnp.float32),
    )
    piece = lax.all_gather(key_value, "ctx", axis=0, tiled=True)
    count = piece.shape[0]
    block = math.gcd(count, 512)

    def forward_step(index, state):
        begin = index * block
        key_seg = lax.dynamic_slice_in_dim(seg_row, begin, block, 0)

        def forward_update(inner):
            top, total, accum = inner
            part = lax.dynamic_slice_in_dim(piece, begin, block, 0).reshape(
                block, 2, heads, HEAD_DIM
            )
            key_pos = begin + jnp.arange(block, dtype=jnp.int32)
            scores = block_scores(
                query_heads, part[:, 0], local_pos, key_pos, local_seg, key_seg, slopes
            )
            new_top = jnp.maximum(top, jnp.max(scores, axis=-1))
            factor = jnp.exp(top - new_top)
            weights = jnp.exp(scores - new_top[:, :, None])
            total = total * factor + jnp.sum(weights, axis=-1)
            accum = accum * factor[:, :, None] + jnp.einsum(
                "hqk,khd->hqd",
                weights.astype(jnp.bfloat16),
                part[:, 1],
                preferred_element_type=jnp.float32,
            )
            return (new_top, total, accum)

        return lax.cond(counted_range(key_seg, block), forward_update, lambda inner: inner, state)

    top, total, accum = lax.fori_loop(0, count // block, forward_step, start_state)
    log_total = top + jnp.log(total)
    mixed_full = accum / total[:, :, None]
    mixed = jnp.transpose(mixed_full, (1, 0, 2)).reshape(rows, width).astype(jnp.bfloat16)
    first_in = inputs.astype(jnp.float32) + matmul(mixed, w_output) + b_output
    first, first_pull = jax.vjp(
        normalize, first_in, g_first.astype(jnp.float32), s_first.astype(jnp.float32)
    )
    first_low = first.astype(jnp.bfloat16)
    gate_up = matmul(first_low, w_widen) + b_widen
    hidden, act_pull = jax.vjp(activate, gate_up)
    hidden_low = hidden.astype(jnp.bfloat16)
    final_in = first + matmul(hidden_low, w_narrow) + b_narrow
    result, final_pull = jax.vjp(
        normalize, final_in, g_final.astype(jnp.float32), s_final.astype(jnp.float32)
    )
    again = (
        lax.all_gather(joined_weight, ("seq", "ctx"), axis=0, tiled=True),
        lax.all_gather(query_bias, ("seq", "ctx"), axis=0, tiled=True),
        lax.all_gather(value_bias, ("seq", "ctx"), axis=0, tiled=True),
        lax.all_gather(output_weight, ("seq", "ctx"), axis=0, tiled=True),
        lax.all_gather(output_bias, ("seq", "ctx"), axis=0, tiled=True),
        lax.all_gather(first_gain, ("seq", "ctx"), axis=0, tiled=True),
        lax.all_gather(first_shift, ("seq", "ctx"), axis=0, tiled=True),
        lax.all_gather(widen_weight, ("seq", "ctx"), axis=0, tiled=True),
        lax.all_gather(widen_bias, ("seq", "ctx"), axis=0, tiled=True),
        lax.all_gather(narrow_weight, ("seq", "ctx"), axis=0, tiled=True),
        lax.all_gather(narrow_bias, ("seq", "ctx"), axis=0, tiled=True),
        lax.all_gather(final_gain, ("seq", "ctx"), axis=0, tiled=True),
        lax.all_gather(final_shift, ("seq", "ctx"), axis=0, tiled=True),
    )
    w_back_joined = again[0]
    w_back_output = again[3]
    w_back_widen = again[7]
    w_back_narrow = again[9]
    final_back, final_gain_grad, final_shift_grad = final_pull(cotangent[0].astype(jnp.float32))
    narrow_back = final_back.astype(jnp.bfloat16)
    narrow_weight_grad = matmul_left(hidden_low, narrow_back)
    narrow_bias_grad = jnp.sum(narrow_back, axis=0, dtype=jnp.float32)
    hidden_back = matmul_right(narrow_back, w_back_narrow)
    (gate_back,) = act_pull(hidden_back)
    widen_back = gate_back.astype(jnp.bfloat16)
    widen_weight_grad = matmul_left(first_low, widen_back)
    widen_bias_grad = jnp.sum(widen_back, axis=0, dtype=jnp.float32)
    first_back = final_back + matmul_right(widen_back, w_back_widen)
    attn_back, first_gain_grad, first_shift_grad = first_pull(first_back)
    output_back = attn_back.astype(jnp.bfloat16)
    output_weight_grad = matmul_left(mixed, output_back)
    output_bias_grad = jnp.sum(output_back, axis=0, dtype=jnp.float32)
    mixed_back = matmul_right(output_back, w_back_output).astype(jnp.bfloat16)
    back_heads = mixed_back.reshape(rows, heads, HEAD_DIM)
    row_dot = jnp.einsum("qhd,hqd->hq", back_heads.astype(jnp.float32), mixed_full)
    query_zero = jnp.zeros((rows, heads, HEAD_DIM), jnp.float32)
    dq_piece = lax.all_gather(key_value, "ctx", axis=0, tiled=True)
    count = dq_piece.shape[0]
    dq_block = math.gcd(count, 512)

    def dq_step(index, state):
        begin = index * dq_block
        key_seg = lax.dynamic_slice_in_dim(seg_row, begin, dq_block, 0)

        def dq_update(inner):
            part = lax.dynamic_slice_in_dim(dq_piece, begin, dq_block, 0).reshape(
                dq_block, 2, heads, HEAD_DIM
            )
            key_pos = begin + jnp.arange(dq_block, dtype=jnp.int32)
            query_part, unused = block_grads(
                query_heads,
                back_heads,
                log_total,
                row_dot,
                local_pos,
                local_seg,
                part[:, 0],
                part[:, 1],
                key_pos,
                key_seg,
                slopes,
                True,
                False,
            )
            return inner + query_part

        return lax.cond(counted_range(key_seg, dq_block), dq_update, lambda inner: inner, state)

    query_sum = lax.fori_loop(0, count // dq_block, dq_step, query_zero)
    local_keys = key_value.reshape(rows, 2, heads, HEAD_DIM)
    query_piece = lax.all_gather(queries, "ctx", axis=0, tiled=True)
    back_piece = lax.all_gather(mixed_back, "ctx", axis=0, tiled=True)
    total_piece = lax.all_gather(
        jnp.transpose(log_total).astype(jnp.bfloat16), "ctx", axis=0, tiled=True
    ).astype(jnp.float32)
    dot_piece = lax.all_gather(
        jnp.transpose(row_dot).astype(jnp.bfloat16), "ctx", axis=0, tiled=True
    ).astype(jnp.float32)
    count = query_piece.shape[0]
    key_block = math.gcd(count, 512)

    def key_step(index, state):
        begin = index * key_block
        query_seg = lax.dynamic_slice_in_dim(seg_row, begin, key_block, 0)

        def key_update(inner):
            q_block = lax.dynamic_slice_in_dim(query_piece, begin, key_block, 0).reshape(
                key_block, heads, HEAD_DIM
            )
            b_block = lax.dynamic_slice_in_dim(back_piece, begin, key_block, 0).reshape(
                key_block, heads, HEAD_DIM
            )
            t_block = jnp.transpose(lax.dynamic_slice_in_dim(total_piece, begin, key_block, 0))
            d_block = jnp.transpose(lax.dynamic_slice_in_dim(dot_piece, begin, key_block, 0))
            query_pos = begin + jnp.arange(key_block, dtype=jnp.int32)
            unused, key_part = block_grads(
                q_block,
                b_block,
                t_block,
                d_block,
                query_pos,
                query_seg,
                local_keys[:, 0],
                local_keys[:, 1],
                local_pos,
                local_seg,
                slopes,
                False,
                True,
            )
            return inner + key_part

        return lax.cond(counted_range(query_seg, key_block), key_update, lambda inner: inner, state)

    key_local = lax.fori_loop(
        0, count // key_block, key_step, jnp.zeros((rows, 2 * width), jnp.float32)
    )
    query_low = query_sum.reshape(rows, width).astype(jnp.bfloat16)
    query_scaled = (query_low.astype(jnp.float32) * scale).astype(jnp.bfloat16)
    key_low = key_local[:, :width].astype(jnp.bfloat16)
    value_low = key_local[:, width:].astype(jnp.bfloat16)
    joined_back = jnp.concatenate([query_scaled, key_low, value_low], axis=1)
    joined_weight_grad = matmul_left(inputs, joined_back)
    query_bias_grad = jnp.sum(query_scaled, axis=0, dtype=jnp.float32)
    value_bias_grad = jnp.sum(value_low, axis=0, dtype=jnp.float32)
    tokens_grad = attn_back + matmul_right(joined_back, w_back_joined)
    owners = lax.axis_size(("seq", "ctx"))
    received = (
        lax.all_to_all(
            joined_weight_grad.astype(jnp.bfloat16),
            ("seq", "ctx"),
            split_axis=0,
            concat_axis=1,
            tiled=True,
        ).astype(joined_weight_grad.dtype),
        lax.all_to_all(
            query_bias_grad[:, None].astype(jnp.bfloat16),
            ("seq", "ctx"),
            split_axis=0,
            concat_axis=1,
            tiled=True,
        ).astype(jnp.float32),
        lax.all_to_all(
            value_bias_grad[:, None].astype(jnp.bfloat16),
            ("seq", "ctx"),
            split_axis=0,
            concat_axis=1,
            tiled=True,
        ).astype(jnp.float32),
        lax.all_to_all(
            output_weight_grad.astype(jnp.bfloat16),
            ("seq", "ctx"),
            split_axis=0,
            concat_axis=1,
            tiled=True,
        ).astype(output_weight_grad.dtype),
        lax.all_to_all(
            output_bias_grad[:, None].astype(jnp.bfloat16),
            ("seq", "ctx"),
            split_axis=0,
            concat_axis=1,
            tiled=True,
        ).astype(jnp.float32),
        lax.all_to_all(
            first_gain_grad[:, None].astype(jnp.bfloat16),
            ("seq", "ctx"),
            split_axis=0,
            concat_axis=1,
            tiled=True,
        ).astype(jnp.float32),
        lax.all_to_all(
            first_shift_grad[:, None].astype(jnp.bfloat16),
            ("seq", "ctx"),
            split_axis=0,
            concat_axis=1,
            tiled=True,
        ).astype(jnp.float32),
        lax.all_to_all(
            widen_weight_grad.astype(jnp.bfloat16),
            ("seq", "ctx"),
            split_axis=0,
            concat_axis=1,
            tiled=True,
        ).astype(widen_weight_grad.dtype),
        lax.all_to_all(
            widen_bias_grad[:, None].astype(jnp.bfloat16),
            ("seq", "ctx"),
            split_axis=0,
            concat_axis=1,
            tiled=True,
        ).astype(jnp.float32),
        lax.all_to_all(
            narrow_weight_grad.astype(jnp.bfloat16),
            ("seq", "ctx"),
            split_axis=0,
            concat_axis=1,
            tiled=True,
        ).astype(narrow_weight_grad.dtype),
        lax.all_to_all(
            narrow_bias_grad[:, None].astype(jnp.bfloat16),
            ("seq", "ctx"),
            split_axis=0,
            concat_axis=1,
            tiled=True,
        ).astype(jnp.float32),
        lax.all_to_all(
            final_gain_grad[:, None].astype(jnp.bfloat16),
            ("seq", "ctx"),
            split_axis=0,
            concat_axis=1,
            tiled=True,
        ).astype(jnp.float32),
        lax.all_to_all(
            final_shift_grad[:, None].astype(jnp.bfloat16),
            ("seq", "ctx"),
            split_axis=0,
            concat_axis=1,
            tiled=True,
        ).astype(jnp.float32),
    )
    owned = tuple((owner_total(item, owners) for item in received))
    (
        r_joined,
        r_query,
        r_value,
        r_output,
        r_obias,
        r_fgain,
        r_fshift,
        r_widen,
        r_wbias,
        r_narrow,
        r_nbias,
        r_lgain,
        r_lshift,
    ) = owned
    summed = (
        lax.psum(r_joined.astype(jnp.bfloat16), "rep").astype(jnp.float32),
        lax.psum(r_query[:, 0].astype(jnp.bfloat16), "rep").astype(jnp.float32),
        lax.psum(r_value[:, 0].astype(jnp.bfloat16), "rep").astype(jnp.float32),
        lax.psum(r_output.astype(jnp.bfloat16), "rep").astype(jnp.float32),
        lax.psum(r_obias[:, 0].astype(jnp.bfloat16), "rep").astype(jnp.float32),
        lax.psum(r_fgain[:, 0].astype(jnp.bfloat16), "rep").astype(jnp.float32),
        lax.psum(r_fshift[:, 0].astype(jnp.bfloat16), "rep").astype(jnp.float32),
        lax.psum(r_widen.astype(jnp.bfloat16), "rep").astype(jnp.float32),
        lax.psum(r_wbias[:, 0].astype(jnp.bfloat16), "rep").astype(jnp.float32),
        lax.psum(r_narrow.astype(jnp.bfloat16), "rep").astype(jnp.float32),
        lax.psum(r_nbias[:, 0].astype(jnp.bfloat16), "rep").astype(jnp.float32),
        lax.psum(r_lgain[:, 0].astype(jnp.bfloat16), "rep").astype(jnp.float32),
        lax.psum(r_lshift[:, 0].astype(jnp.bfloat16), "rep").astype(jnp.float32),
    )
    return (
        result.astype(jnp.bfloat16)[None],
        tokens_grad[None],
        summed[0],
        summed[1],
        summed[2],
        summed[3],
        summed[4],
        summed[5],
        summed[6],
        summed[7],
        summed[8],
        summed[9],
        summed[10],
        summed[11],
        summed[12],
    )


def solution(mesh):
    return jax.shard_map(
        on_device,
        mesh=mesh,
        in_specs=(
            P(("rep", "seq"), "ctx", None),
            P(("rep", "seq"), None),
            P(("seq", "ctx"), None),
            P(("seq", "ctx")),
            P(("seq", "ctx")),
            P(("seq", "ctx"), None),
            P(("seq", "ctx")),
            P(("seq", "ctx")),
            P(("seq", "ctx")),
            P(("seq", "ctx"), None),
            P(("seq", "ctx")),
            P(("seq", "ctx"), None),
            P(("seq", "ctx")),
            P(("seq", "ctx")),
            P(("seq", "ctx")),
            P(("rep", "seq"), "ctx", None),
        ),
        out_specs=(
            P(("rep", "seq"), "ctx", None),
            P(("rep", "seq"), "ctx", None),
            P(("seq", "ctx"), None),
            P(("seq", "ctx")),
            P(("seq", "ctx")),
            P(("seq", "ctx"), None),
            P(("seq", "ctx")),
            P(("seq", "ctx")),
            P(("seq", "ctx")),
            P(("seq", "ctx"), None),
            P(("seq", "ctx")),
            P(("seq", "ctx"), None),
            P(("seq", "ctx")),
            P(("seq", "ctx")),
            P(("seq", "ctx")),
        ),
        check_vma=False,
    )
```

profile of v0, /device:TPU:0, one launch (start us, length us, event | category | flops | bytes accessed | tf_op | source)
XLA Modules:
  0.0 996.8 jit_solution(7779017779086050723)
XLA Ops:
  16.6 63.9 %all-reduce.10 = (bf16[768]{0:T(1024)(128)(2,1)S(1)}, bf16[768]{0:T(1024)(128)(2,1)S(1)}, bf16[768]{0:T(1024)(128)(2,1)S(1)}, bf16[768]{0:T(1024)(128)(2,1)S(1)}...) all-reduce(bf16[768]{0:T(1024)(128)(2,1)S(1)} %dynamic-update-slice, ...), channel_id=1, replica_groups=mesh['rep'=2,'seq'=2,'ctx'=8] {'seq','ctx'}, use_global_device_ids=true, to_apply=%add.2 | all-reduce | flops 6144 | bytes 24576
  86.7 17.6 %all-gather = bf16[16,1,384]{2,1,0:T(2,128)(2,1)S(1)} all-gather(bf16[1,1,384]{2,1,0:T(2,128)(2,1)S(1)} %reshape.555), channel_id=1, replica_groups=mesh['rep'=2,'seq'=2,'ctx'=8] {'seq','ctx'}, dimensions={0}, use_global_device_ids=true | all-gather | bytes 13056 | tf_op jit(solution)/shard_map/all_gather | solution.py:137
  109.4 10.5 %all-gather.11.cloned.1.call-done = bf16[1024,1536]{1,0:T(8,128)(2,1)} async-done(((bf16[128,1536]{1,0:T(8,128)(2,1)}), bf16[1024,1536]{1,0:T(8,128)(2,1)}) %all-gather.11.cloned.1.call-update) | async-done | bytes 3145744 | tf_op jit(solution)/shard_map/all_gather | solution.py:174
  123.9 12.8 %while.52 = (s32[]{:T(128)}, f32[12,128]{1,0:T(8,128)S(1)}, f32[12,128]{1,0:T(8,128)S(1)}, f32[12,128,64]{1,2,0:T(8,128)}, s32[1024]{0:T(1024)S(1)}, /*index=5*/...) while((s32[]{:T(128)}, f32[12,128]{1,0:T(8,128)S(1)}, ...), condition=%wide.region_5.6_spmd.clone, body=%wide.region_0.5_spmd.clone.sunk | while | flops 212799152 | bytes 17352844 | solution.py:205
  127.2 6.2 conditional.9
  138.4 21.2 %all-gather.13.cloned.1.call-done = bf16[768,768]{1,0:T(8,128)(2,1)} async-done(((bf16[48,768]{1,0:T(8,128)(2,1)}), bf16[768,768]{1,0:T(8,128)(2,1)}) %all-gather.13.cloned.1.call-update) | async-done | bytes 1179664 | tf_op jit(solution)/shard_map/all_gather | solution.py:132
  163.2 78.4 %all-gather.15.cloned.1.call-done = bf16[768,6144]{1,0:T(8,128)(2,1)} async-done(((bf16[48,6144]{1,0:T(8,128)(2,1)}), bf16[768,6144]{1,0:T(8,128)(2,1)}) %all-gather.15.cloned.1.call-update) | async-done | bytes 9437200 | tf_op jit(solution)/shard_map/all_gather | solution.py:136
  253.0 42.4 %all-gather.17.cloned.1.call-done = bf16[3072,768]{1,0:T(8,128)(2,1)} async-done(((bf16[192,768]{1,0:T(8,128)(2,1)}), bf16[3072,768]{1,0:T(8,128)(2,1)}) %all-gather.17.cloned.1.call-update) | async-done | bytes 4718608 | tf_op jit(solution)/shard_map/all_gather | solution.py:138
  307.2 8.8 multiply_reduce_fusion
  328.4 22.3 %all-to-all-done.3 = bf16[16,48,768]{2,1,0:T(8,128)(2,1)} async-done(((bf16[16,48,768]{2,1,0:T(8,128)(2,1)}), bf16[16,48,768]{2,1,0:T(8,128)(2,1)}, u32[]{:S(2)}, u32[]{:S(2)}) %all-to-all-start.3) | async-done | bytes 1179680 | tf_op jit(solution)/shard_map/all_to_all | solution.py:371
  361.0 42.6 %all-gather.19.cloned.1.call-done = bf16[1024,768]{1,0:T(8,128)(2,1)} async-done(((bf16[128,768]{1,0:T(8,128)(2,1)}), bf16[1024,768]{1,0:T(8,128)(2,1)}) %all-gather.19.cloned.1.call-update) | async-done | bytes 1572880 | tf_op jit(solution)/shard_map/all_gather | solution.py:292
  406.8 85.5 %all_gather.74 = bf16[1024,12]{0,1:T(8,128)(2,1)S(1)} all-gather(bf16[128,12]{0,1:T(8,128)(2,1)S(1)} %get-tuple-element.1224), channel_id=1, replica_groups=mesh['rep'=2,'seq'=2,'ctx'=8] {'ctx'}, dimensions={0}, use_global_device_ids=true | all-gather | bytes 27648 | tf_op jit(solution)/shard_map/all_gather | solution.py:294
  495.9 12.7 %all_gather.76 = bf16[1024,12]{0,1:T(8,128)(2,1)S(1)} all-gather(bf16[128,12]{0,1:T(8,128)(2,1)S(1)} %convert_bitcast_fusion), channel_id=1, replica_groups=mesh['rep'=2,'seq'=2,'ctx'=8] {'ctx'}, dimensions={0}, use_global_device_ids=true | all-gather | bytes 27648 | tf_op jit(solution)/shard_map/all_gather | solution.py:297
  510.0 17.5 %while.53 = (s32[]{:T(128)}, f32[128,12,64]{0,2,1:T(8,128)}, s32[1024]{0:T(1024)S(1)}, s32[]{:T(128)}, s32[]{:T(128)}, /*index=5*/bf16[1024,1536]{0,1:T(8,128)(2...) while((s32[]{:T(128)}, f32[128,12,64]{0,2,1:T(8,128)}, ...), condition=%wide.region_17.18_spmd.clone, body=%wide.region_14.17_spmd.clone.sunk | while | flops 307856032 | bytes 20737408 | solution.py:290
  514.0 9.8 conditional.10
  533.4 20.1 %while.54 = (s32[]{:T(128)}, f32[128,1536]{0,1:T(8,128)}, s32[1024]{0:T(1024)S(1)}, s32[]{:T(128)}, s32[]{:T(128)}, /*index=5*/bf16[1024,768]{0,1:T(8,128)(2,1)}...) while((s32[]{:T(128)}, f32[128,1536]{0,1:T(8,128)}, ...), condition=%wide.region_21.22_spmd.clone, body=%wide.region_18.21_spmd.clone.sunk | while | flops 412746400 | bytes 30119488 | solution.py:336
  537.3 12.4 %conditional.11 = (f32[128,1536]{0,1:T(8,128)}) conditional(s32[]{:T(128)} %convert_element_type.531, f32[128,1536]{0,1:T(8,128)} %get-tuple-element.1551, (s32[]{:T(128)}, bf16[1024,768]{0,1:T(8,128)(2,1)}, s32[512]{0:T(512)S(1)}, s32[128]{0:T(128)S(1)}, bf16[128,2,12,64]{0,3,2,1:T(8,128)(2,1)}, /*index=5*/s32[]{:T(128)}, ...), branch_computations={%region_19.19_spmd, %region_20.20_spmd.clone} | conditional | flops 412746400 | bytes 30114486 | solution.py:334
  559.5 25.9 %all-to-all-start = ((bf16[16,48,2304]{2,1,0:T(8,128)(2,1)}), bf16[16,48,2304]{2,1,0:T(8,128)(2,1)}, u32[]{:S(2)}, u32[]{:S(2)}) async-start(bf16[16,48,2304]{2,1,0:T(8,128)(2,1)} %bitcast.196), calls=%async_computation | async-start | bytes 7077888 | tf_op jit(solution)/shard_map/all_to_all | solution.py:350
  590.9 69.1 %all-to-all-done = bf16[16,48,2304]{2,1,0:T(8,128)(2,1)} async-done(((bf16[16,48,2304]{2,1,0:T(8,128)(2,1)}), bf16[16,48,2304]{2,1,0:T(8,128)(2,1)}, u32[]{:S(2)}, u32[]{:S(2)}) %all-to-all-start) | async-done | bytes 3538976 | tf_op jit(solution)/shard_map/all_to_all | solution.py:350
  660.0 8.2 all-to-all-start.7
  677.7 183.6 %all-to-all-done.7 = bf16[16,48,6144]{2,1,0:T(8,128)(2,1)} async-done(((bf16[16,48,6144]{2,1,0:T(8,128)(2,1)}), bf16[16,48,6144]{2,1,0:T(8,128)(2,1)}, u32[]{:S(2)}, u32[]{:S(2)}) %all-to-all-start.7) | async-done | bytes 9437216 | tf_op jit(solution)/shard_map/all_to_all | solution.py:399
  861.4 6.4 reduce_sum.388
  868.6 16.1 %all-to-all-start.12 = ((bf16[16,48,1]{1,2,0:T(2,128)(2,1)}), bf16[16,48,1]{1,2,0:T(2,128)(2,1)S(1)}, u32[]{:S(2)}, u32[]{:S(2)}) async-start(bf16[16,48,1]{1,2,0:T(2,128)(2,1)} %convert_element_type.464), calls=%async_computation.12 | async-start | bytes 16384 | tf_op jit(solution)/shard_map/all_to_all | solution.py:434
  885.4 5.7 all-to-all-done.12
  (337 shorter events, 243.7 us)
Async XLA Ops:
  7.2 73.3 %all-gather.9.cloned.1.call-start = ((), (), s32[]{:S(2)}) async-start(), calls=%async_computation.13 | async-start | bytes 3760128 | tf_op jit(solution)/shard_map/all_gather | solution.py:129
  7.9 112.0 %all-gather.11.cloned.1.call-start = ((), (), s32[]{:S(2)}) async-start(), calls=%async_computation.14 | async-start | bytes 3538944 | tf_op jit(solution)/shard_map/all_gather | solution.py:174
  84.2 75.4 %all-gather.13.cloned.1.call-start = ((), (), s32[]{:S(2)}) async-start(), calls=%async_computation.15 | async-start | bytes 1253376 | tf_op jit(solution)/shard_map/all_gather | solution.py:132
  85.0 156.6 %all-gather.15.cloned.1.call-start = ((), (), s32[]{:S(2)}) async-start(), calls=%async_computation.16 | async-start | bytes 10027008 | tf_op jit(solution)/shard_map/all_gather | solution.py:136
  85.5 209.8 %all-gather.17.cloned.1.call-start = ((), (), s32[]{:S(2)}) async-start(), calls=%async_computation.17 | async-start | bytes 5013504 | tf_op jit(solution)/shard_map/all_gather | solution.py:138
  319.2 31.5 %all-to-all-start.3 = ((bf16[16,48,768]{2,1,0:T(8,128)(2,1)}), bf16[16,48,768]{2,1,0:T(8,128)(2,1)}, u32[]{:S(2)}, u32[]{:S(2)}) async-start(bf16[16,48,768]{2,1,0:T(8,128)(2,1)} %bitcast.201), calls=%async_computation.3 | async-start | bytes 2359296 | tf_op jit(solution)/shard_map/all_to_all | solution.py:371
  350.7 208.8 %all-to-all-start.9 = ((bf16[16,192,768]{2,1,0:T(8,128)(2,1)}), bf16[16,192,768]{2,1,0:T(8,128)(2,1)}, u32[]{:S(2)}, u32[]{:S(2)}) async-start(bf16[16,192,768]{2,1,0:T(8,128)(2,1)} %bitcast.193), calls=%async_computation.9 | async-start | bytes 9437184 | tf_op jit(solution)/shard_map/all_to_all | solution.py:413
  355.8 47.8 %all-gather.19.cloned.1.call-start = ((), (), s32[]{:S(2)}) async-start(), calls=%async_computation.18 | async-start | bytes 1769472 | tf_op jit(solution)/shard_map/all_gather | solution.py:292
  356.4 173.5 %all-gather.21.cloned.1.call-start = ((), (), s32[]{:S(2)}) async-start(), calls=%async_computation.19 | async-start | bytes 1769472 | tf_op jit(solution)/shard_map/all_gather | solution.py:293
  559.5 100.5 %all-to-all-start = ((bf16[16,48,2304]{2,1,0:T(8,128)(2,1)}), bf16[16,48,2304]{2,1,0:T(8,128)(2,1)}, u32[]{:S(2)}, u32[]{:S(2)}) async-start(bf16[16,48,2304]{2,1,0:T(8,128)(2,1)} %bitcast.196), calls=%async_computation | async-start | bytes 7077888 | tf_op jit(solution)/shard_map/all_to_all | solution.py:350
  660.0 201.3 %all-to-all-start.7 = ((bf16[16,48,6144]{2,1,0:T(8,128)(2,1)}), bf16[16,48,6144]{2,1,0:T(8,128)(2,1)}, u32[]{:S(2)}, u32[]{:S(2)}) async-start(bf16[16,48,6144]{2,1,0:T(8,128)(2,1)} %bitcast.190), calls=%async_computation.7 | async-start | bytes 18874368 | tf_op jit(solution)/shard_map/all_to_all | solution.py:399
  668.3 314.9 %all-reduce.15.cloned.1.call-start = ((), (), s32[]{:S(2)}) async-start(), calls=%async_computation.20 | async-start | bytes 2359296 | tf_op jit(solution)/shard_map/psum | solution.py:459
  677.7 236.6 %copy-start.50 = (bf16[768]{0:T(1024)(128)(2,1)S(1)}, bf16[768]{0:T(1024)(128)(2,1)}, u32[]{:S(2)}) copy-start(bf16[768]{0:T(1024)(128)(2,1)} %get-tuple-element.1120) | copy-start | bytes 4612
  677.7 246.4 %copy-start.49 = (bf16[768]{0:T(1024)(128)(2,1)S(1)}, bf16[768]{0:T(1024)(128)(2,1)}, u32[]{:S(2)}) copy-start(bf16[768]{0:T(1024)(128)(2,1)} %get-tuple-element.1214) | copy-start | bytes 4612
  677.7 256.3 %copy-start.48 = (bf16[768]{0:T(1024)(128)(2,1)S(1)}, bf16[768]{0:T(1024)(128)(2,1)}, u32[]{:S(2)}) copy-start(bf16[768]{0:T(1024)(128)(2,1)} %get-tuple-element.1118) | copy-start | bytes 4612
  868.6 22.5 %all-to-all-start.12 = ((bf16[16,48,1]{1,2,0:T(2,128)(2,1)}), bf16[16,48,1]{1,2,0:T(2,128)(2,1)S(1)}, u32[]{:S(2)}, u32[]{:S(2)}) async-start(bf16[16,48,1]{1,2,0:T(2,128)(2,1)} %convert_element_type.464), calls=%async_computation.12 | async-start | bytes 16384 | tf_op jit(solution)/shard_map/all_to_all | solution.py:434
  891.1 9.9 all-to-all-start.1
  901.0 9.8 all-to-all-start.4
  910.8 9.9 all-to-all-start.5
  920.7 9.8 all-to-all-start.6
  930.5 9.9 all-to-all-start.10
  941.0 10.4 %all-to-all-start.11 = ((bf16[16,48,1]{1,2,0:T(2,128)(2,1)}), bf16[16,48,1]{1,2,0:T(2,128)(2,1)}, u32[]{:S(2)}, u32[]{:S(2)}) async-start(bf16[16,48,1]{1,2,0:T(2,128)(2,1)} %convert_element_type.463), calls=%async_computation.11 | async-start | bytes 16384 | tf_op jit(solution)/shard_map/all_to_all | solution.py:427
  951.4 10.0 %all-to-all-start.8 = ((bf16[16,2,192]{2,1,0:T(2,128)(2,1)}), bf16[16,2,192]{2,1,0:T(2,128)(2,1)S(1)}, u32[]{:S(2)}, u32[]{:S(2)}) async-start(bf16[16,2,192]{2,1,0:T(2,128)(2,1)} %reshape.577), calls=%async_computation.8 | async-start | bytes 32768 | tf_op jit(solution)/shard_map/all_to_all | solution.py:406
  962.3 11.1 %all-to-all-start.2 = ((bf16[16,48,1]{1,2,0:T(2,128)(2,1)}), bf16[16,48,1]{1,2,0:T(2,128)(2,1)S(1)}, u32[]{:S(2)}, u32[]{:S(2)}) async-start(bf16[16,48,1]{1,2,0:T(2,128)(2,1)} %convert_element_type.457), calls=%async_computation.2 | async-start | bytes 16384 | tf_op jit(solution)/shard_map/all_to_all | solution.py:364
  (57 other events, 1480.2 us)
Sparse Core Ops, SparseCore 0:
  10.3 50.3 all-gather.8
  84.3 35.5 all-gather.10
  122.2 37.3 all-gather.12
  161.8 79.7 all-gather.14
  243.8 51.5 all-gather.16
  358.0 45.5 all-gather.18
  405.8 46.1 all-gather.20
  868.0 54.3 all-reduce.14
where the time goes:
time: 1010 us; the launch traced here: 997 us
  waiting for transfers between devices  515 us (51%)
  blocking collectives  185 us (18%)
  starting transfers between devices  89.8 us (9%)
  matrix products  66.5 us (7%)
  other arithmetic  62.4 us (6%)
  local copies, waits for them, and re-layouts  46.2 us (5%)
  loops' own time  16 us (2%)
  between operations  15.9 us (2%)
    all_to_all x1, waiting for transfers between devices, on_device(): lax.all_to_all(widen_weight_grad.astype(jnp.bfloat16), ('seq', 'ctx'), sp...  184 us
    all_gather x1, blocking collectives, on_device(): lax.all_gather(jnp.transpose(log_total).astype(jnp.bfloat16), 'ctx', axis...  85.5 us
    all_gather x1, waiting for transfers between devices, on_device(): lax.all_gather(widen_weight, ('seq', 'ctx'), axis=0, tiled=True)  78.4 us
    all_to_all x1, waiting for transfers between devices, on_device(): lax.all_to_all(joined_weight_grad.astype(jnp.bfloat16), ('seq', 'ctx'), s...  69.1 us
    unnamed x1, blocking collectives  63.9 us
    all_gather x1, waiting for transfers between devices, on_device(): query_piece = lax.all_gather(queries, 'ctx', axis=0, tiled=True)  42.6 us
    all_gather x1, waiting for transfers between devices, on_device(): lax.all_gather(narrow_weight, ('seq', 'ctx'), axis=0, tiled=True)  42.4 us
    all_to_all x1, starting transfers between devices, on_device(): lax.all_to_all(joined_weight_grad.astype(jnp.bfloat16), ('seq', 'ctx'), s...  25.9 us
  transfers between devices with their start and end apart: 21, of which 17 were waited for; matrix products, arithmetic and copies ran while one was open for 13% of the time, Pallas kernels for 0%

commit v1 on v0

v1 whole, which is shorter than its diff:
```python
import math

import jax
import jax.numpy as jnp
from jax import lax
from jax.experimental import pallas as pl
from jax.experimental.pallas import tpu as pltpu
from jax.sharding import PartitionSpec as P

HEAD_DIM = 64
GROUPS = 4
FAR = 1e30
BF = jnp.bfloat16
F32 = jnp.float32


def dot_nn(left, right):
    return lax.dot_general(left, right, (((1,), (0,)), ((), ())), preferred_element_type=F32)


def dot_tn(left, right):
    return lax.dot_general(left, right, (((0,), (0,)), ((), ())), preferred_element_type=F32)


def dot_nt(left, right):
    return lax.dot_general(left, right, (((1,), (1,)), ((), ())), preferred_element_type=F32)


def head_mask(head, cols):
    lane = lax.broadcasted_iota(jnp.int32, (1, cols), 1)
    return (lane >= head * HEAD_DIM) & (lane < (head + 1) * HEAD_DIM)


def only_head(value, head):
    return jnp.where(head_mask(head, value.shape[1]), value, jnp.zeros_like(value))


def each_chunk(count, body):
    if count <= 4:
        for index in range(count):
            body(index)
    else:
        lax.fori_loop(0, count, lambda index, carry: (body(index), carry)[1], 0)


def forward_kernel(slope_ref, q_ref, kv_ref, qinfo_ref, kinfo_ref, out_ref, inv_ref, acc_ref, sum_ref, *, chunk):
    rows, cols = q_ref.shape
    heads = cols // HEAD_DIM
    count = kv_ref.shape[0] // chunk
    acc_ref[...] = jnp.zeros_like(acc_ref)
    sum_ref[...] = jnp.zeros_like(sum_ref)
    q = q_ref[...]
    qpos = qinfo_ref[:, 0:1]
    qseg = qinfo_ref[:, 1:2]
    ones = jnp.ones((8, chunk), BF)

    def step(index):
        begin = index * chunk
        here = pl.ds(begin, chunk)
        keys = kv_ref[here, :cols]
        values = kv_ref[here, cols:]
        kpos = kinfo_ref[0:1, here]
        kseg = kinfo_ref[1:2, here]
        far = jnp.where(qseg == kseg, jnp.abs(qpos - kpos), FAR)
        for head in range(heads):
            scores = dot_nt(only_head(q, head), keys) - slope_ref[head] * far
            raised = jnp.exp(scores).astype(BF)
            sum_ref[head] += dot_nt(ones, raised)
            acc_ref[head] += dot_nn(raised, values)

    each_chunk(count, step)
    total = jnp.zeros((rows, cols), F32)
    for head in range(heads):
        inv = 1.0 / sum_ref[head]
        inv_ref[head] = inv
        column = jnp.transpose(inv)[:, 0:1]
        total = total + only_head(acc_ref[head] * column, head)
    out_ref[...] = total


def attend_forward(slopes, queries, key_value, qinfo, kinfo, interpret=False):
    count, cols = queries.shape
    heads = cols // HEAD_DIM
    keys = key_value.shape[0]
    chunk = math.gcd(keys, 512)
    rows = math.gcd(count, 128)
    whole = lambda shape: pl.BlockSpec(shape, lambda i: tuple(0 for _ in shape))
    return pl.pallas_call(
        lambda *refs: forward_kernel(*refs, chunk=chunk),
        grid=(count // rows,),
        in_specs=[
            pl.BlockSpec(memory_space=pltpu.SMEM),
            pl.BlockSpec((rows, cols), lambda i: (i, 0)),
            whole((keys, 2 * cols)),
            pl.BlockSpec((rows, 2), lambda i: (i, 0)),
            whole((2, keys)),
        ],
        out_specs=[
            pl.BlockSpec((rows, cols), lambda i: (i, 0)),
            pl.BlockSpec((heads, 8, rows), lambda i: (0, 0, i)),
        ],
        out_shape=[
            jax.ShapeDtypeStruct((count, cols), F32),
            jax.ShapeDtypeStruct((heads, 8, count), F32),
        ],
        scratch_shapes=[pltpu.VMEM((heads, rows, cols), F32), pltpu.VMEM((heads, 8, rows), F32)],
        name="attend_forward",
        interpret=interpret,
    )(slopes, queries, key_value, qinfo, kinfo)


def backward_kernel(
    slope_ref, q_ref, do_ref, out_ref, inv_ref, kv_ref, qinfo_ref, kinfo_ref, dq_ref, dkv_ref, acc_ref, *, chunk
):
    rows, cols = q_ref.shape
    heads = cols // HEAD_DIM
    count = kv_ref.shape[0] // chunk
    q = q_ref[...]
    back = do_ref[...]
    product = back.astype(F32) * out_ref[...]
    qpos = qinfo_ref[0:1, :]
    qseg = qinfo_ref[1:2, :]
    acc_ref[...] = jnp.zeros_like(acc_ref)
    row_dots = []
    for head in range(heads):
        chosen = jnp.broadcast_to(head_mask(head, cols), (8, cols)).astype(F32)
        row_dots.append(
            lax.dot_general(
                chosen,
                product,
                (((1,), (1,)), ((), ())),
                precision=lax.Precision.HIGHEST,
                preferred_element_type=F32,
            )[0:1]
        )

    @pl.when(pl.program_id(0) == 0)
    def _():
        dkv_ref[...] = jnp.zeros_like(dkv_ref)

    def step(index):
        begin = index * chunk
        here = pl.ds(begin, chunk)
        keys = kv_ref[here, :cols]
        values = kv_ref[here, cols:]
        kpos = kinfo_ref[here, 0:1]
        kseg = kinfo_ref[here, 1:2]
        far = jnp.where(qseg == kseg, jnp.abs(qpos - kpos), FAR)
        key_part = jnp.zeros((chunk, cols), F32)
        value_part = jnp.zeros((chunk, cols), F32)
        for head in range(heads):
            q_head = only_head(q, head)
            back_head = only_head(back, head)
            scores = dot_nt(keys, q_head) - slope_ref[head] * far
            probs = jnp.exp(scores) * inv_ref[head, 0:1, :]
            prob_back = dot_nt(values, back_head)
            score_back = (probs * (prob_back - row_dots[head])).astype(BF)
            key_part = key_part + dot_nn(score_back, q_head)
            value_part = value_part + dot_nn(probs.astype(BF), back_head)
            acc_ref[head] += dot_tn(score_back, keys)
        dkv_ref[here, :cols] += key_part
        dkv_ref[here, cols:] += value_part

    each_chunk(count, step)
    total = jnp.zeros((rows, cols), F32)
    for head in range(heads):
        total = total + only_head(acc_ref[head], head)
    dq_ref[...] = total


def attend_backward(slopes, queries, back, mixed, inv, key_value, qinfo, kinfo, interpret=False):
    count, cols = queries.shape
    heads = cols // HEAD_DIM
    keys = key_value.shape[0]
    chunk = math.gcd(keys, 512)
    rows = math.gcd(count, 128)
    whole = lambda shape: pl.BlockSpec(shape, lambda i: tuple(0 for _ in shape))
    by_row = pl.BlockSpec((rows, cols), lambda i: (i, 0))
    return pl.pallas_call(
        lambda *refs: backward_kernel(*refs, chunk=chunk),
        grid=(count // rows,),
        in_specs=[
            pl.BlockSpec(memory_space=pltpu.SMEM),
            by_row,
            by_row,
            by_row,
            pl.BlockSpec((heads, 8, rows), lambda i: (0, 0, i)),
            whole((keys, 2 * cols)),
            pl.BlockSpec((2, rows), lambda i: (0, i)),
            whole((keys, 2)),
        ],
        out_specs=[by_row, whole((keys, 2 * cols))],
        out_shape=[
            jax.ShapeDtypeStruct((count, cols), F32),
            jax.ShapeDtypeStruct((keys, 2 * cols), F32),
        ],
        scratch_shapes=[pltpu.VMEM((heads, rows, cols), F32)],
        name="attend_backward",
        interpret=interpret,
    )(slopes, queries, back, mixed, inv, key_value, qinfo, kinfo)


def norm_stats(value):
    centre = jnp.mean(value, axis=-1, keepdims=True)
    centred = value - centre
    spread = jnp.mean(centred * centred, axis=-1, keepdims=True)
    root = lax.rsqrt(spread + 1e-06)
    return centred * root, root


def norm_back(unit, root, gain, back):
    scaled = back * gain
    return root * (
        scaled
        - jnp.mean(scaled, axis=-1, keepdims=True)
        - unit * jnp.mean(scaled * unit, axis=-1, keepdims=True)
    )


def after(value, *others):
    return lax.optimization_barrier((value,) + others)[0]


class Layout:
    def __init__(self):
        self.size = lax.axis_size("ctx")
        self.members = self.size // GROUPS
        index = lax.axis_index("ctx")
        self.group = index // self.members
        self.member = index % self.members
        self.seq = lax.axis_index("seq")
        self.inner = [
            [g * self.members + m for m in range(self.members)] for g in range(GROUPS)
        ]

    def shift(self, value, steps):
        n, r = self.size, self.members
        return lax.ppermute(value, "ctx", [(i, (i + steps * r) % n) for i in range(n)])

    def swap(self, value, axis):
        return lax.ppermute(value, axis, [(0, 1), (1, 0)])

    def gather(self, value):
        return [value] + [self.shift(value, k) for k in range(1, GROUPS)]

    def scatter_sum(self, parts):
        total = parts[0]
        for k in range(1, GROUPS):
            total = total + self.shift(parts[k].astype(BF), -k).astype(F32)
        return total

    def exchange(self, pieces):
        own = lax.dynamic_index_in_dim(pieces, self.group, 0, keepdims=False)
        out = [own]
        for k in range(1, GROUPS):
            target = (self.group + k) % GROUPS
            out.append(
                self.shift(lax.dynamic_index_in_dim(pieces, target, 0, keepdims=False), k)
            )
        return out

    def ordered(self, relative):
        line = [relative[0], relative[3], relative[2], relative[1]]
        twice = jnp.stack(line + line[:3])
        return lax.dynamic_slice_in_dim(twice, (GROUPS - self.group) % GROUPS, GROUPS, 0)

    def both_seq(self, value):
        other = self.swap(value, "seq")
        first = self.seq == 0
        return jnp.stack([jnp.where(first, value, other), jnp.where(first, other, value)])

    def partner(self, value):
        return lax.ppermute(
            value, "ctx", [(i, i ^ 1) for i in range(self.size)]
        )

    def all_members(self, value, axis):
        if self.members == 2:
            other = self.partner(value)
            first = self.member == 0
            return jnp.stack(
                [jnp.where(first, value, other), jnp.where(first, other, value)], axis
            )
        out = lax.all_gather(value, "ctx", axis_index_groups=self.inner)
        return jnp.moveaxis(out, 0, axis)

    def member_sum(self, pieces):
        if self.members == 2:
            keep = lax.dynamic_index_in_dim(pieces, self.member, 0, keepdims=False)
            give = lax.dynamic_index_in_dim(pieces, 1 - self.member, 0, keepdims=False)
            return keep + self.partner(give.astype(BF)).astype(F32)
        got = lax.all_to_all(
            pieces.astype(BF), "ctx", 0, 0, axis_index_groups=self.inner, tiled=True
        )
        return jnp.sum(got.astype(F32), axis=0)

    def seq_sum(self, pieces):
        keep = lax.dynamic_index_in_dim(pieces, self.seq, 0, keepdims=False)
        give = lax.dynamic_index_in_dim(pieces, 1 - self.seq, 0, keepdims=False)
        return keep + self.swap(give.astype(BF), "seq").astype(F32)

    def rep_sum(self, value):
        low = value.astype(BF)
        return low.astype(F32) + self.swap(low, "rep").astype(F32)


def on_device(
    tokens,
    segments,
    joined_weight,
    query_bias,
    value_bias,
    output_weight,
    output_bias,
    first_gain,
    first_shift,
    widen_weight,
    widen_bias,
    narrow_weight,
    narrow_bias,
    final_gain,
    final_shift,
    cotangent,
):
    at = Layout()
    n, r = at.size, at.members
    rows, width = tokens.shape[1:]
    heads = width // HEAD_DIM
    near_heads = heads // GROUPS
    cols = near_heads * HEAD_DIM
    kb = joined_weight.shape[0]
    ff_own = narrow_weight.shape[0]
    ff = ff_own * 2 * n
    quarter = ff // GROUPS
    span = r * ff_own
    seg_row = segments[0]
    length = seg_row.shape[0]
    scale = 1.0 / math.sqrt(HEAD_DIM)
    inputs = tokens[0]

    x_rel = at.gather(inputs)
    x_four = jnp.concatenate(x_rel, axis=0)

    small = jnp.concatenate(
        [
            query_bias,
            value_bias,
            output_bias,
            first_gain,
            first_shift,
            narrow_bias,
            final_gain,
            final_shift,
            widen_bias,
        ]
    )[None]
    small_all = at.all_members(at.both_seq(at.ordered(at.gather(small))), 2)
    small_all = small_all.reshape(2 * n, -1).astype(F32)

    def vector(place):
        return small_all[:, place * kb : (place + 1) * kb].reshape(width)

    b_query, b_value, b_output, g_first, s_first, b_narrow, g_final, s_final = (
        vector(place) for place in range(8)
    )
    b_widen = lax.dynamic_index_in_dim(
        small_all[:, 8 * kb :].reshape(2, 2, GROUPS, span), at.group, 2, keepdims=False
    ).reshape(2 * quarter)
    b_query = lax.dynamic_index_in_dim(b_query.reshape(GROUPS, cols), at.group, 0, keepdims=False)
    b_value = lax.dynamic_index_in_dim(b_value.reshape(GROUPS, cols), at.group, 0, keepdims=False)

    joined_cut = jnp.transpose(joined_weight.reshape(kb, 3, GROUPS, cols), (2, 0, 1, 3)).reshape(
        GROUPS, kb, 3 * cols
    )
    w_joined = at.all_members(at.both_seq(at.ordered(at.exchange(joined_cut))), 2).reshape(
        width, 3 * cols
    )

    output_low = after(output_weight, x_four)
    out_rel = at.ordered(at.gather(output_low)).reshape(GROUPS * kb, width)
    both = at.both_seq(jnp.concatenate([out_rel, narrow_weight], axis=0))
    both = at.all_members(both, 1)
    w_output = jnp.transpose(
        both[:, :, : GROUPS * kb].reshape(2, r, GROUPS, kb, width), (0, 2, 1, 3, 4)
    ).reshape(width, width)
    w_narrow = both[:, :, GROUPS * kb :].reshape(quarter, width)

    widen_cut = jnp.transpose(
        after(widen_weight, x_four).reshape(kb, 4, GROUPS, span), (2, 0, 1, 3)
    ).reshape(GROUPS, kb, 2 * quarter)
    w_widen = at.all_members(at.both_seq(at.ordered(at.exchange(widen_cut))), 2).reshape(
        width, 2 * quarter
    )

    lanes = jnp.arange(rows, dtype=jnp.int32)
    near = (at.group - jnp.arange(GROUPS, dtype=jnp.int32)) % GROUPS

    def places(member):
        return ((near * r + member)[:, None] * rows + lanes[None]).reshape(-1)

    if r == 2:
        key_members = jnp.stack([at.member, 1 - at.member])
    else:
        key_members = jnp.arange(r, dtype=jnp.int32)
    query_pos = places(at.member)
    key_pos = jnp.concatenate([places(key_members[i]) for i in range(r)])
    query_seg = jnp.take(seg_row, query_pos)
    key_seg = jnp.take(seg_row, key_pos)
    q_info = jnp.stack([query_pos, query_seg]).astype(F32)
    k_info = jnp.stack([key_pos, key_seg]).astype(F32)
    order_heads = at.group * near_heads + jnp.arange(near_heads, dtype=jnp.int32)
    slopes = jnp.power(2.0, -8.0 * (order_heads.astype(F32) + 1.0) / heads) * (512.0 / length)

    joined = dot_nn(x_four, w_joined)
    queries = ((joined[:, :cols] + b_query) * scale).astype(BF)
    kv_own = jnp.concatenate(
        [joined[:, cols : 2 * cols], joined[:, 2 * cols :] + b_value], axis=1
    ).astype(BF)
    if r == 2:
        key_value = jnp.concatenate([kv_own, at.partner(kv_own)], axis=0)
    else:
        key_value = at.all_members(kv_own, 0).reshape(-1, 2 * cols)
    mixed_near, inv = attend_forward(slopes, queries, key_value, jnp.transpose(q_info), k_info)
    mixed_low = mixed_near.astype(BF).reshape(GROUPS, rows, cols)
    mixed_rel = [mixed_low[0]] + [at.shift(mixed_low[k], -k) for k in range(1, GROUPS)]
    mixed_rel = [mixed_rel[0], mixed_rel[3], mixed_rel[2], mixed_rel[1]]
    mixed = jnp.transpose(at.ordered(mixed_rel), (1, 0, 2)).reshape(rows, width)

    first_in = inputs.astype(F32) + dot_nn(mixed, w_output) + b_output
    first_unit, first_root = norm_stats(first_in)
    first = first_unit * g_first + s_first
    first_low = first.astype(BF)

    first_four = jnp.concatenate(at.gather(first_low), axis=0)
    gate_up = dot_nn(first_four, w_widen) + b_widen
    gate, up = gate_up[:, :quarter], gate_up[:, quarter:]
    phi_big = 0.5 * (1.0 + lax.erf(gate * math.sqrt(0.5)))
    gelu = gate * phi_big
    slope_gate = phi_big + gate * jnp.exp(-0.5 * gate * gate) * (1.0 / math.sqrt(2.0 * math.pi))
    hidden = (gelu * up).astype(BF)
    final_part = dot_nn(hidden, w_narrow).reshape(GROUPS, rows, width)
    final_in = first + at.scatter_sum([final_part[k] for k in range(GROUPS)]) + b_narrow
    final_unit, final_root = norm_stats(final_in)
    result = final_unit * g_final + s_final

    upstream = cotangent[0].astype(F32)
    final_back = norm_back(final_unit, final_root, g_final, upstream)
    final_gain_grad = jnp.sum(upstream * final_unit, axis=0)
    final_shift_grad = jnp.sum(upstream, axis=0)
    narrow_back = final_back.astype(BF)
    narrow_bias_grad = jnp.sum(narrow_back.astype(F32), axis=0)
    back_four = jnp.concatenate(at.gather(narrow_back), axis=0)
    hidden_back = dot_nt(back_four, w_narrow)
    widen_back = jnp.concatenate(
        [hidden_back * up * slope_gate, hidden_back * gelu], axis=1
    ).astype(BF)
    first_part = dot_nt(widen_back, w_widen).reshape(GROUPS, rows, width)
    first_back = final_back + at.scatter_sum([first_part[k] for k in range(GROUPS)])
    narrow_grad = dot_tn(hidden, back_four)
    widen_grad = dot_tn(first_four, widen_back)
    widen_bias_grad = jnp.sum(widen_back.astype(F32), axis=0)

    attn_back = norm_back(first_unit, first_root, g_first, first_back)
    first_gain_grad = jnp.sum(first_back * first_unit, axis=0)
    first_shift_grad = jnp.sum(first_back, axis=0)
    output_back = attn_back.astype(BF)
    output_bias_grad = jnp.sum(output_back.astype(F32), axis=0)
    output_grad = dot_tn(mixed, output_back)
    mixed_back = dot_nt(output_back, w_output).astype(BF)
    mixed_back = jnp.transpose(mixed_back.reshape(rows, GROUPS, cols), (1, 0, 2))
    back_near = jnp.concatenate(at.exchange(mixed_back), axis=0)

    query_sum, kv_sum = attend_backward(
        slopes, queries, back_near, mixed_near, inv, key_value, q_info, jnp.transpose(k_info)
    )
    if r == 2:
        half = kv_sum.shape[0] // 2
        kv_back = kv_sum[:half] + at.partner(kv_sum[half:].astype(BF)).astype(F32)
    else:
        kv_back = at.member_sum(kv_sum.reshape(r, -1, 2 * cols))
    query_low = query_sum.astype(BF)
    query_scaled = (query_low.astype(F32) * scale).astype(BF)
    joined_back = jnp.concatenate([query_scaled, kv_back.astype(BF)], axis=1)
    tokens_part = dot_nt(joined_back, w_joined).reshape(GROUPS, rows, width)
    tokens_grad = attn_back + at.scatter_sum([tokens_part[k] for k in range(GROUPS)])
    joined_grad = dot_tn(x_four, joined_back)
    near_bias = jnp.sum(joined_back.astype(F32), axis=0)
    query_bias_grad = near_bias[:cols]
    value_bias_grad = near_bias[2 * cols :]

    narrow_sum = at.member_sum(jnp.transpose(narrow_grad.reshape(2, r, ff_own, width), (1, 0, 2, 3)))
    narrow_total = at.rep_sum(at.seq_sum(narrow_sum))

    def to_rows(grad):
        pieces = jnp.transpose(grad.reshape(2, GROUPS, r, kb, -1), (2, 0, 1, 3, 4))
        mine = at.rep_sum(at.seq_sum(at.member_sum(pieces))).astype(BF)
        return at.ordered(at.exchange(mine))

    widen_total = jnp.transpose(
        to_rows(widen_grad).reshape(GROUPS, kb, 4, span), (1, 2, 0, 3)
    ).reshape(kb, 2 * ff)
    joined_total = jnp.transpose(
        to_rows(joined_grad).reshape(GROUPS, kb, 3, cols), (1, 2, 0, 3)
    ).reshape(kb, 3 * width)

    def spread(vector, parts):
        wide = jnp.zeros((parts, GROUPS, vector.shape[0] // parts), F32)
        return lax.dynamic_update_slice_in_dim(
            wide, vector.reshape(parts, 1, -1), at.group, 1
        ).reshape(-1)

    vectors = [
        spread(query_bias_grad, 1),
        spread(value_bias_grad, 1),
        output_bias_grad,
        first_gain_grad,
        first_shift_grad,
        narrow_bias_grad,
        final_gain_grad,
        final_shift_grad,
    ]
    row = jnp.concatenate(
        [item.reshape(2 * n, kb) for item in vectors]
        + [spread(widen_bias_grad, 4).reshape(2 * n, 8 * kb)],
        axis=1,
    )
    row = jnp.pad(row[:, None, :], ((0, 0), (0, 15), (0, width - 16 * kb)))
    packed = jnp.concatenate([output_grad.reshape(2 * n, kb, width), row], axis=1)
    packed = jnp.transpose(packed.reshape(2, GROUPS, r, kb + 16, width), (2, 0, 1, 3, 4))
    packed = at.seq_sum(at.member_sum(packed)).astype(BF)
    packed = at.exchange(packed)
    packed = sum(item.astype(F32) for item in packed[1:]) + packed[0].astype(F32)
    packed = at.rep_sum(packed)
    output_total = packed[:kb]
    last = packed[kb]

    def owned(place):
        return last[place * kb : (place + 1) * kb]

    return (
        result.astype(BF)[None],
        tokens_grad[None],
        joined_total.astype(F32),
        owned(0),
        owned(1),
        output_total,
        owned(2),
        owned(3),
        owned(4),
        widen_total.astype(F32),
        last[8 * kb : 16 * kb],
        narrow_total,
        owned(5),
        owned(6),
        owned(7),
    )


def solution(mesh):
    tokens = P(("rep", "seq"), "ctx", None)
    matrix = P(("seq", "ctx"), None)
    vector = P(("seq", "ctx"))
    return jax.shard_map(
        on_device,
        mesh=mesh,
        in_specs=(
            tokens,
            P(("rep", "seq"), None),
            matrix,
            vector,
            vector,
            matrix,
            vector,
            vector,
            vector,
            matrix,
            vector,
            matrix,
            vector,
            vector,
            vector,
            tokens,
        ),
        out_specs=(
            tokens,
            tokens,
            matrix,
            vector,
            vector,
            matrix,
            vector,
            vector,
            vector,
            matrix,
            vector,
            matrix,
            vector,
            vector,
            vector,
        ),
        check_vma=False,
    )
```

time: 1010 us -> 343 us (0.34); the launches traced: 997 us -> 342 us
  waiting for transfers between devices: 515 us -> 123 us
  blocking collectives: 185 us -> 0 us
  matrix products: 66.5 us -> 20.3 us
  other arithmetic: 62.4 us -> 33.7 us
  Pallas kernels: 0 us -> 24.9 us
  loops' own time: 16 us -> 0 us
  between operations: 15.9 us -> 2.38 us
    all_to_all x13 -> x0, waiting for transfers between devices: 317 us -> none  [the longest x1 184 us: on_device(): lax.all_to_all(widen_weight_grad.astype(jnp.bfloat16), ('seq', 'ctx'), sp...]
    all_gather x7 -> x0, waiting for transfers between devices: 195 us -> none  [the longest x1 78.4 us: on_device(): lax.all_gather(widen_weight, ('seq', 'ctx'), axis=0, tiled=True)]
    ppermute x0 -> x67, waiting for transfers between devices: none -> 123 us  [the longest x45 95.5 us: shift(): lax.ppermute(value, 'ctx', [(i, (i + steps * r) % n) for i in range(n)])]
    all_gather x3 -> x0, blocking collectives: 116 us -> none  [the longest x1 85.5 us: on_device(): lax.all_gather(jnp.transpose(log_total).astype(jnp.bfloat16), 'ctx', axis...]
    all_to_all x13 -> x0, starting transfers between devices: 89.2 us -> none  [the longest x1 25.9 us: on_device(): lax.all_to_all(joined_weight_grad.astype(jnp.bfloat16), ('seq', 'ctx'), s...]
    ppermute x0 -> x67, starting transfers between devices: none -> 87.8 us  [the longest x45 74.7 us: shift(): lax.ppermute(value, 'ctx', [(i, (i + steps * r) % n) for i in range(n)])]
    unnamed x1 -> x0, blocking collectives: 63.9 us -> none
    dot_general x19 -> x12, matrix products: 66.5 us -> 20.3 us  [the longest x4 8.58 us: dot_nt(): lax.dot_general(left, right, (((1,), (1,)), ((), ())), preferred_element_...]
  transfers between devices with their start and end apart: 21 -> 67, of which waited for: 17 -> 28; matrix products, arithmetic and copies ran while one was open for 13% -> 22% of each run, Pallas kernels for 0% -> 7%
where the time goes in v1:
time: 343 us; the launch traced here: 342 us
  waiting for transfers between devices  123 us (36%)
  starting transfers between devices  87.8 us (26%)
  local copies, waits for them, and re-layouts  50 us (15%)
  other arithmetic  33.7 us (10%)
  Pallas kernels  24.9 us (7%)
  matrix products  20.3 us (6%)
    ppermute x45, waiting for transfers between devices, shift(): lax.ppermute(value, 'ctx', [(i, (i + steps * r) % n) for i in range(n)])  95.5 us
    ppermute x45, starting transfers between devices, shift(): lax.ppermute(value, 'ctx', [(i, (i + steps * r) % n) for i in range(n)])  74.7 us
    ppermute x12, waiting for transfers between devices, swap(): return lax.ppermute(value, axis, [(0, 1), (1, 0)])  27.2 us
    pallas_call x1, Pallas kernels, attend_backward(): pl.pallas_call(lambda *refs: backward_kernel(*refs, chunk=chunk), grid=(c...  15.3 us
    ppermute x12, starting transfers between devices, swap(): return lax.ppermute(value, axis, [(0, 1), (1, 0)])  12.3 us
    pallas_call x1, Pallas kernels, attend_forward(): pl.pallas_call(lambda *refs: forward_kernel(*refs, chunk=chunk), grid=(co...  9.64 us
    dot_general x4, matrix products, dot_nt(): lax.dot_general(left, right, (((1,), (1,)), ((), ())), preferred_element_...  8.58 us
    dot_general x4, matrix products, dot_tn(): lax.dot_general(left, right, (((0,), (0,)), ((), ())), preferred_element_...  7.17 us
  transfers between devices with their start and end apart: 67, of which 28 were waited for; matrix products, arithmetic and copies ran while one was open for 22% of the time, Pallas kernels for 7%

profile of v1, /device:TPU:0, one launch (start us, length us, event | category | flops | bytes accessed | tf_op | source)
XLA Modules:
  0.0 341.8 jit_solution(16682447821569206347)
XLA Ops:
  0.7 6.1 %concatenate.90 = bf16[768]{0:T(1024)(128)(2,1)S(1)} concatenate(bf16[48]{0:T(256)(128)(2,1)} %param.19, bf16[48]{0:T(256)(128)(2,1)} %param.20, bf16[48]{0:T(256)(128)(2,1)} %param.22, bf16[48]{0:T(256)(128)(2,1)} %param.23, bf16[48]{0:T(256)(128)(2,1)} %param.24, bf16[48]{0:T(256)(128)(2,1)} %param.28, bf16[48]{0:T(256)(128)(2,1)} %param.29, bf16[48]{0:T(256)(128)(2,1)} %param.30, ...), dimensions={0} | concatenate | bytes 3072 | tf_op jit(solution)/shard_map/concatenate | solution.py:344
  6.8 5.1 %collective-permute-start.8 = (bf16[1,768]{1,0:T(2,128)(2,1)S(1)}, bf16[1,768]{1,0:T(2,128)(2,1)S(1)}, u32[]{:S(2)}, u32[]{:S(2)}) collective-permute-start(bf16[1,768]{1,0:T(2,128)(2,1)S(1)} %broadcast_in_dim.22), channel_id=1, source_target_pairs={{0,6},{1,7},{2,0},{3,1},{4,2},{5,3},{6,4},{7,5},{8,14},{9,15},{10,... | collective-permute-start | bytes 4616 | tf_op jit(solution)/shard_map/ppermute | solution.py:238
  21.7 4.5 %gather_fusion.1 = s32[1024]{0:T(1024)S(1)} fusion(s32[1024]{0:T(1024)S(1)} %bitcast.298, s32[1024]{0:T(1024)S(1)} %broadcast_clamp_fusion), kind=kCustom, calls=%fused_computation.1 | custom fusion | bytes 12288 | tf_op jit(solution)/shard_map/jit(_take)/gather | solution.py:408
  26.5 3.8 %collective-permute-start.3 = (bf16[48,576]{1,0:T(8,128)(2,1)S(1)}, bf16[48,576]{1,0:T(8,128)(2,1)S(1)}, u32[]{:S(2)}, u32[]{:S(2)}) collective-permute-start(bf16[48,576]{1,0:T(8,128)(2,1)S(1)} %get-tuple-element.90), channel_id=1, source_target_pairs={{0,6},{1,7},{2,0},{3,1},{4,2},{5,3},{6,4},{7,5},{8,14},{9,15},{10,... | collective-permute-start | bytes 165896 | tf_op jit(solution)/shard_map/ppermute | solution.py:238
  40.9 4.5 %collective-permute-done.5 = bf16[48,576]{1,0:T(8,128)(2,1)S(1)} collective-permute-done((bf16[48,576]{1,0:T(8,128)(2,1)S(1)}, bf16[48,576]{1,0:T(8,128)(2,1)S(1)}, u32[]{:S(2)}, u32[]{:S(2)}) %collective-permute-start.5) | collective-permute-done | bytes 55328 | tf_op jit(solution)/shard_map/ppermute | solution.py:238
  62.1 7.5 %collective-permute-done.26 = bf16[48,1536]{1,0:T(8,128)(2,1)S(1)} collective-permute-done((bf16[48,1536]{1,0:T(8,128)(2,1)S(1)}, bf16[48,1536]{1,0:T(8,128)(2,1)S(1)}, u32[]{:S(2)}, u32[]{:S(2)}) %collective-permute-start.26) | collective-permute-done | bytes 147488 | tf_op jit(solution)/shard_map/ppermute | solution.py:238
  77.8 8.0 %collective-permute-done.28 = bf16[4,48,1536]{2,1,0:T(8,128)(2,1)} collective-permute-done((bf16[4,48,1536]{2,1,0:T(8,128)(2,1)}, bf16[4,48,1536]{2,1,0:T(8,128)(2,1)}, u32[]{:S(2)}, u32[]{:S(2)}) %collective-permute-start.28) | collective-permute-done | bytes 589856 | tf_op jit(solution)/shard_map/ppermute | solution.py:241
  89.2 9.6 %attend_forward.1 = (f32[512,192]{1,0:T(8,128)}, f32[3,8,512]{2,1,0:T(8,128)}) custom-call(f32[3]{0:T(128)} %power_multiply_fusion.refs_0_, bf16[512,192]{1,0:T(8,128)(2,1)} %multiply_convert_fusion.3.refs_1_, bf16[1024,384]{1,0:T(8,128)(2,1)} %pad_maximum_fusion.7.refs_2_.refs_5_, f32[512,2]{1,0:T(8,128)} %copy.162.refs_3_, f32[2,1024]{1,0:T(2,128)} %add_convert_fusion.5.refs_4_), custom_call_target="tpu_custom_call" | custom-call | tf_op jit(solution)/shard_map/attend_forward/pallas_call | solution.py:88
  100.7 5.7 %collective-permute-start.15 = (bf16[128,192]{1,0:T(8,128)(2,1)S(1)}, bf16[128,192]{1,0:T(8,128)(2,1)S(1)}, u32[]{:S(2)}, u32[]{:S(2)}) collective-permute-start(bf16[128,192]{1,0:T(8,128)(2,1)S(1)} %get-tuple-element.81), channel_id=1, source_target_pairs={{0,4},{1,5},{2,6},{3,7},{4,0},{5,1},{6,2},{7,3},{8,12},{9,13},{10,... | collective-permute-start | bytes 147464 | tf_op jit(solution)/shard_map/ppermute | solution.py:238
  108.4 4.9 %collective-permute-done.15 = bf16[128,192]{1,0:T(8,128)(2,1)S(1)} collective-permute-done((bf16[128,192]{1,0:T(8,128)(2,1)S(1)}, bf16[128,192]{1,0:T(8,128)(2,1)S(1)}, u32[]{:S(2)}, u32[]{:S(2)}) %collective-permute-start.15) | collective-permute-done | bytes 49184 | tf_op jit(solution)/shard_map/ppermute | solution.py:238
  124.0 12.4 %collective-permute-done.23 = bf16[128,768]{1,0:T(8,128)(2,1)S(1)} collective-permute-done((bf16[128,768]{1,0:T(8,128)(2,1)S(1)}, bf16[128,768]{1,0:T(8,128)(2,1)S(1)}, u32[]{:S(2)}, u32[]{:S(2)}) %collective-permute-start.23) | collective-permute-done | bytes 196640 | tf_op jit(solution)/shard_map/ppermute | solution.py:238
  150.1 7.0 %collective-permute-done.31 = bf16[128,768]{1,0:T(8,128)(2,1)S(1)} collective-permute-done((bf16[128,768]{1,0:T(8,128)(2,1)S(1)}, bf16[128,768]{1,0:T(8,128)(2,1)S(1)}, u32[]{:S(2)}, u32[]{:S(2)}) %collective-permute-start.31) | collective-permute-done | bytes 196640 | tf_op jit(solution)/shard_map/ppermute | solution.py:238
  160.8 5.9 %collective-permute-start.35 = (bf16[128,768]{1,0:T(8,128)(2,1)}, bf16[128,768]{1,0:T(8,128)(2,1)}, u32[]{:S(2)}, u32[]{:S(2)}) collective-permute-start(bf16[128,768]{1,0:T(8,128)(2,1)} %get-tuple-element.35), channel_id=1, source_target_pairs={{0,6},{1,7},{2,0},{3,1},{4,2},{5,3},{6,4},{7,5},{8,14},{9,15},{10,... | collective-permute-start | bytes 589832 | tf_op jit(solution)/shard_map/ppermute | solution.py:238
  173.2 10.8 %collective-permute-done.34 = bf16[128,768]{1,0:T(8,128)(2,1)} collective-permute-done((bf16[128,768]{1,0:T(8,128)(2,1)}, bf16[128,768]{1,0:T(8,128)(2,1)}, u32[]{:S(2)}, u32[]{:S(2)}) %collective-permute-start.34) | collective-permute-done | bytes 196640 | tf_op jit(solution)/shard_map/ppermute | solution.py:238
  211.3 5.4 %collective-permute-start.41 = (bf16[128,192]{1,0:T(8,128)(2,1)S(1)}, bf16[128,192]{1,0:T(8,128)(2,1)S(1)}, u32[]{:S(2)}, u32[]{:S(2)}) collective-permute-start(bf16[128,192]{1,0:T(8,128)(2,1)S(1)} %bitcast.339), channel_id=1, source_target_pairs={{0,6},{1,7},{2,0},{3,1},{4,2},{5,3},{6,4},{7,5},{8,14},{9,15},{10,... | collective-permute-start | bytes 147464 | tf_op jit(solution)/shard_map/ppermute | solution.py:238
  224.0 15.3 %attend_backward.1 = (f32[512,192]{1,0:T(8,128)}, f32[1024,384]{1,0:T(8,128)}) custom-call(f32[3]{0:T(128)} %power_multiply_fusion.refs_0_, bf16[512,192]{1,0:T(8,128)(2,1)} %multiply_convert_fusion.3.refs_1_, bf16[512,192]{1,0:T(8,128)(2,1)} %pad_maximum_fusion.16.refs_2_, f32[512,192]{1,0:T(8,128)} %get-tuple-element.21.refs_3_, ...), custom_call_target="tpu_custom_call" | custom-call | tf_op jit(solution)/shard_map/attend_backward/pallas_call | solution.py:179
  258.9 7.4 %collective-permute-done.44 = bf16[128,768]{1,0:T(8,128)(2,1)} collective-permute-done((bf16[128,768]{1,0:T(8,128)(2,1)}, bf16[128,768]{1,0:T(8,128)(2,1)}, u32[]{:S(2)}, u32[]{:S(2)}) %collective-permute-start.44) | collective-permute-done | bytes 196640 | tf_op jit(solution)/shard_map/ppermute | solution.py:238
  275.1 3.8 %collective-permute-done.66 = bf16[192,768]{1,0:T(8,128)(2,1)S(1)} collective-permute-done((bf16[192,768]{1,0:T(8,128)(2,1)S(1)}, bf16[192,768]{1,0:T(8,128)(2,1)S(1)}, u32[]{:S(2)}, u32[]{:S(2)}) %collective-permute-start.66) | collective-permute-done | bytes 294944 | tf_op jit(solution)/shard_map/ppermute | solution.py:241
  281.5 5.9 %collective-permute-done.48 = bf16[4,48,576]{2,1,0:T(8,128)(2,1)S(1)} collective-permute-done((bf16[4,48,576]{2,1,0:T(8,128)(2,1)S(1)}, bf16[4,48,576]{2,1,0:T(8,128)(2,1)S(1)}, u32[]{:S(2)}, u32[]{:S(2)}) %collective-permute-start.48) | collective-permute-done | bytes 221216 | tf_op jit(solution)/shard_map/ppermute | solution.py:241
  287.5 4.8 %collective-permute-start.49 = (bf16[48,576]{1,0:T(8,128)(2,1)S(1)}, bf16[48,576]{1,0:T(8,128)(2,1)S(1)}, u32[]{:S(2)}, u32[]{:S(2)}) collective-permute-start(bf16[48,576]{1,0:T(8,128)(2,1)S(1)} %get-tuple-element.86), channel_id=1, source_target_pairs={{0,6},{1,7},{2,0},{3,1},{4,2},{5,3},{6,4},{7,5},{8,14},{9,15},{10,... | collective-permute-start | bytes 165896 | tf_op jit(solution)/shard_map/ppermute | solution.py:238
  294.3 4.5 %collective-permute-done.50 = bf16[48,576]{1,0:T(8,128)(2,1)S(1)} collective-permute-done((bf16[48,576]{1,0:T(8,128)(2,1)S(1)}, bf16[48,576]{1,0:T(8,128)(2,1)S(1)}, u32[]{:S(2)}, u32[]{:S(2)}) %collective-permute-start.50) | collective-permute-done | bytes 55328 | tf_op jit(solution)/shard_map/ppermute | solution.py:238
  308.4 5.5 %collective-permute-done.55 = bf16[64,768]{1,0:T(8,128)(2,1)S(1)} collective-permute-done((bf16[64,768]{1,0:T(8,128)(2,1)S(1)}, bf16[64,768]{1,0:T(8,128)(2,1)S(1)}, u32[]{:S(2)}, u32[]{:S(2)}) %collective-permute-start.55) | collective-permute-done | bytes 98336 | tf_op jit(solution)/shard_map/ppermute | solution.py:238
  316.4 5.8 %collective-permute-done.57 = bf16[64,768]{1,0:T(8,128)(2,1)S(1)} collective-permute-done((bf16[64,768]{1,0:T(8,128)(2,1)S(1)}, bf16[64,768]{1,0:T(8,128)(2,1)S(1)}, u32[]{:S(2)}, u32[]{:S(2)}) %collective-permute-start.57) | collective-permute-done | bytes 98336 | tf_op jit(solution)/shard_map/ppermute | solution.py:241
  330.0 8.8 %collective-permute-done.62 = bf16[48,1536]{1,0:T(8,128)(2,1)S(1)} collective-permute-done((bf16[48,1536]{1,0:T(8,128)(2,1)S(1)}, bf16[48,1536]{1,0:T(8,128)(2,1)S(1)}, u32[]{:S(2)}, u32[]{:S(2)}) %collective-permute-start.62) | collective-permute-done | bytes 147488 | tf_op jit(solution)/shard_map/ppermute | solution.py:238
  (468 shorter events, 176.4 us)
Async XLA Ops:
  6.8 19.6 %collective-permute-start.8 = (bf16[1,768]{1,0:T(2,128)(2,1)S(1)}, bf16[1,768]{1,0:T(2,128)(2,1)S(1)}, u32[]{:S(2)}, u32[]{:S(2)}) collective-permute-start(bf16[1,768]{1,0:T(2,128)(2,1)S(1)} %broadcast_in_dim.22), channel_id=1, source_target_pairs={{0,6},{1,7},{2,0},{3,1},{4,2},{5,3},{6,4},{7,5},{8,14},{9,15},{10,... | collective-permute-start | bytes 4616 | tf_op jit(solution)/shard_map/ppermute | solution.py:238
  11.9 18.4 %collective-permute-start.10 = (bf16[1,768]{1,0:T(2,128)(2,1)S(1)}, bf16[1,768]{1,0:T(2,128)(2,1)S(1)}, u32[]{:S(2)}, u32[]{:S(2)}) collective-permute-start(bf16[1,768]{1,0:T(2,128)(2,1)S(1)} %broadcast_in_dim.22), channel_id=1, source_target_pairs={{0,2},{1,3},{2,4},{3,5},{4,6},{5,7},{6,0},{7,1},{8,10},{9,11},{10,... | collective-permute-start | bytes 4616 | tf_op jit(solution)/shard_map/ppermute | solution.py:238
  12.9 34.1 %collective-permute-start.2 = (bf16[128,768]{1,0:T(8,128)(2,1)}, bf16[128,768]{1,0:T(8,128)(2,1)S(1)}, u32[]{:S(2)}, u32[]{:S(2)}) collective-permute-start(bf16[128,768]{1,0:T(8,128)(2,1)} %bitcast.329), channel_id=1, source_target_pairs={{0,6},{1,7},{2,0},{3,1},{4,2},{5,3},{6,4},{7,5},{8,14},{9,15},{10,... | collective-permute-start | bytes 589832 | tf_op jit(solution)/shard_map/ppermute | solution.py:238
  15.7 31.3 %collective-permute-start.1 = (bf16[128,768]{1,0:T(8,128)(2,1)}, bf16[128,768]{1,0:T(8,128)(2,1)S(1)}, u32[]{:S(2)}, u32[]{:S(2)}) collective-permute-start(bf16[128,768]{1,0:T(8,128)(2,1)} %bitcast.330), channel_id=1, source_target_pairs={{0,4},{1,5},{2,6},{3,7},{4,0},{5,1},{6,2},{7,3},{8,12},{9,13},{10,... | collective-permute-start | bytes 589832 | tf_op jit(solution)/shard_map/ppermute | solution.py:238
  26.4 22.0 %collective-permute-start = (bf16[128,768]{1,0:T(8,128)(2,1)S(1)}, bf16[128,768]{1,0:T(8,128)(2,1)S(1)}, u32[]{:S(2)}, u32[]{:S(2)}) collective-permute-start(bf16[128,768]{1,0:T(8,128)(2,1)S(1)} %bitcast.331), channel_id=1, source_target_pairs={{0,2},{1,3},{2,4},{3,5},{4,6},{5,7},{6,0},{7,1},{8,10},{9,11},{10,... | collective-permute-start | bytes 589832 | tf_op jit(solution)/shard_map/ppermute | solution.py:238
  45.5 15.5 %collective-permute-start.6 = (bf16[4,48,576]{2,1,0:T(8,128)(2,1)S(1)}, bf16[4,48,576]{2,1,0:T(8,128)(2,1)}, u32[]{:S(2)}, u32[]{:S(2)}) collective-permute-start(bf16[4,48,576]{2,1,0:T(8,128)(2,1)S(1)} %constant_dynamic-slice_fusion.10), channel_id=1, source_target_pairs={{0,8},{8,0},{1,9},{9,1},{2,10},{10,2},{3,11},{11,3},{4,12},{12,4},... | collective-permute-start | bytes 663560 | tf_op jit(solution)/shard_map/ppermute | solution.py:241
  54.4 15.2 %collective-permute-start.26 = (bf16[48,1536]{1,0:T(8,128)(2,1)S(1)}, bf16[48,1536]{1,0:T(8,128)(2,1)S(1)}, u32[]{:S(2)}, u32[]{:S(2)}) collective-permute-start(bf16[48,1536]{1,0:T(8,128)(2,1)S(1)} %get-tuple-element.72), channel_id=1, source_target_pairs={{0,4},{1,5},{2,6},{3,7},{4,0},{5,1},{6,2},{7,3},{8,12},{9,13},{10,... | collective-permute-start | bytes 442376 | tf_op jit(solution)/shard_map/ppermute | solution.py:238
  70.7 15.2 %collective-permute-start.28 = (bf16[4,48,1536]{2,1,0:T(8,128)(2,1)}, bf16[4,48,1536]{2,1,0:T(8,128)(2,1)}, u32[]{:S(2)}, u32[]{:S(2)}) collective-permute-start(bf16[4,48,1536]{2,1,0:T(8,128)(2,1)} %constant_dynamic-slice_fusion.5), channel_id=1, source_target_pairs={{0,8},{8,0},{1,9},{9,1},{2,10},{10,2},{3,11},{11,3},{4,12},{12,4},... | collective-permute-start | bytes 1769480 | tf_op jit(solution)/shard_map/ppermute | solution.py:241
  77.3 36.3 %collective-permute-start.21 = (bf16[2,384,768]{2,1,0:T(8,128)(2,1)}, bf16[2,384,768]{2,1,0:T(8,128)(2,1)}, u32[]{:S(2)}, u32[]{:S(2)}) collective-permute-start(bf16[2,384,768]{2,1,0:T(8,128)(2,1)} %pad_maximum_fusion.3), channel_id=1, source_target_pairs={{0,1},{1,0},{2,3},{3,2},{4,5},{5,4},{6,7},{7,6},{8,9},{9,8},{10,11... | collective-permute-start | bytes 3538952 | tf_op jit(solution)/shard_map/ppermute | solution.py:273
  88.1 32.5 %collective-permute-start.29 = (bf16[2,4,48,1536]{3,2,1,0:T(8,128)(2,1)}, bf16[2,4,48,1536]{3,2,1,0:T(8,128)(2,1)}, u32[]{:S(2)}, u32[]{:S(2)}) collective-permute-start(bf16[2,4,48,1536]{3,2,1,0:T(8,128)(2,1)} %pad_maximum_fusion.4), channel_id=1, source_target_pairs={{0,1},{1,0},{2,3},{3,2},{4,5},{5,4},{6,7},{7,6},{8,9},{9,8},{10,11... | collective-permute-start | bytes 3538952 | tf_op jit(solution)/shard_map/ppermute | solution.py:273
  118.2 18.2 %collective-permute-start.23 = (bf16[128,768]{1,0:T(8,128)(2,1)S(1)}, bf16[128,768]{1,0:T(8,128)(2,1)S(1)}, u32[]{:S(2)}, u32[]{:S(2)}) collective-permute-start(bf16[128,768]{1,0:T(8,128)(2,1)S(1)} %fusion.40), channel_id=1, source_target_pairs={{0,4},{1,5},{2,6},{3,7},{4,0},{5,1},{6,2},{7,3},{8,12},{9,13},{10,... | collective-permute-start | bytes 589832 | tf_op jit(solution)/shard_map/ppermute | solution.py:238
  118.7 17.7 %collective-permute-start.22 = (bf16[128,768]{1,0:T(8,128)(2,1)S(1)}, bf16[128,768]{1,0:T(8,128)(2,1)S(1)}, u32[]{:S(2)}, u32[]{:S(2)}) collective-permute-start(bf16[128,768]{1,0:T(8,128)(2,1)S(1)} %fusion.40), channel_id=1, source_target_pairs={{0,2},{1,3},{2,4},{3,5},{4,6},{5,7},{6,0},{7,1},{8,10},{9,11},{10,... | collective-permute-start | bytes 589832 | tf_op jit(solution)/shard_map/ppermute | solution.py:238
  140.7 16.4 %collective-permute-start.31 = (bf16[128,768]{1,0:T(8,128)(2,1)S(1)}, bf16[128,768]{1,0:T(8,128)(2,1)S(1)}, u32[]{:S(2)}, u32[]{:S(2)}) collective-permute-start(bf16[128,768]{1,0:T(8,128)(2,1)S(1)} %get-tuple-element.65), channel_id=1, source_target_pairs={{0,4},{1,5},{2,6},{3,7},{4,0},{5,1},{6,2},{7,3},{8,12},{9,13},{10,... | collective-permute-start | bytes 589832 | tf_op jit(solution)/shard_map/ppermute | solution.py:238
  166.8 17.3 %collective-permute-start.34 = (bf16[128,768]{1,0:T(8,128)(2,1)}, bf16[128,768]{1,0:T(8,128)(2,1)}, u32[]{:S(2)}, u32[]{:S(2)}) collective-permute-start(bf16[128,768]{1,0:T(8,128)(2,1)} %get-tuple-element.35), channel_id=1, source_target_pairs={{0,4},{1,5},{2,6},{3,7},{4,0},{5,1},{6,2},{7,3},{8,12},{9,13},{10,... | collective-permute-start | bytes 589832 | tf_op jit(solution)/shard_map/ppermute | solution.py:238
  166.8 17.3 %collective-permute-start.33 = (bf16[128,768]{1,0:T(8,128)(2,1)}, bf16[128,768]{1,0:T(8,128)(2,1)}, u32[]{:S(2)}, u32[]{:S(2)}) collective-permute-start(bf16[128,768]{1,0:T(8,128)(2,1)} %get-tuple-element.35), channel_id=1, source_target_pairs={{0,2},{1,3},{2,4},{3,5},{4,6},{5,7},{6,0},{7,1},{8,10},{9,11},{10,... | collective-permute-start | bytes 589832 | tf_op jit(solution)/shard_map/ppermute | solution.py:238
  191.2 16.2 %collective-permute-start.37 = (bf16[128,768]{1,0:T(8,128)(2,1)}, bf16[128,768]{1,0:T(8,128)(2,1)S(1)}, u32[]{:S(2)}, u32[]{:S(2)}) collective-permute-start(bf16[128,768]{1,0:T(8,128)(2,1)} %get-tuple-element.62), channel_id=1, source_target_pairs={{0,4},{1,5},{2,6},{3,7},{4,0},{5,1},{6,2},{7,3},{8,12},{9,13},{10,... | collective-permute-start | bytes 589832 | tf_op jit(solution)/shard_map/ppermute | solution.py:238
  200.9 71.8 %collective-permute-start.58 = (bf16[2,4,48,1536]{3,2,1,0:T(8,128)(2,1)}, bf16[2,4,48,1536]{3,2,1,0:T(8,128)(2,1)}, u32[]{:S(2)}, u32[]{:S(2)}) collective-permute-start(bf16[2,4,48,1536]{3,2,1,0:T(8,128)(2,1)} %fusion.7), channel_id=1, source_target_pairs={{0,1},{1,0},{2,3},{3,2},{4,5},{5,4},{6,7},{7,6},{8,9},{9,8},{10,11... | collective-permute-start | bytes 3538952 | tf_op jit(solution)/shard_map/ppermute | solution.py:273
  205.1 36.6 %collective-permute-start.64 = (bf16[2,192,768]{2,1,0:T(8,128)(2,1)}, bf16[2,192,768]{2,1,0:T(8,128)(2,1)}, u32[]{:S(2)}, u32[]{:S(2)}) collective-permute-start(bf16[2,192,768]{2,1,0:T(8,128)(2,1)} %fusion.13), channel_id=1, source_target_pairs={{0,1},{1,0},{2,3},{3,2},{4,5},{5,4},{6,7},{7,6},{8,9},{9,8},{10,11... | collective-permute-start | bytes 1769480 | tf_op jit(solution)/shard_map/ppermute | solution.py:273
  245.1 23.3 %collective-permute-start.65 = (bf16[192,768]{1,0:T(8,128)(2,1)}, bf16[192,768]{1,0:T(8,128)(2,1)}, u32[]{:S(2)}, u32[]{:S(2)}) collective-permute-start(bf16[192,768]{1,0:T(8,128)(2,1)} %fusion.41), channel_id=1, source_target_pairs={{0,8},{8,0},{1,9},{9,1},{2,10},{10,2},{3,11},{11,3},{4,12},{12,4},... | collective-permute-start | bytes 884744 | tf_op jit(solution)/shard_map/ppermute | solution.py:241
  248.9 17.5 %collective-permute-start.44 = (bf16[128,768]{1,0:T(8,128)(2,1)}, bf16[128,768]{1,0:T(8,128)(2,1)}, u32[]{:S(2)}, u32[]{:S(2)}) collective-permute-start(bf16[128,768]{1,0:T(8,128)(2,1)} %get-tuple-element.59), channel_id=1, source_target_pairs={{0,4},{1,5},{2,6},{3,7},{4,0},{5,1},{6,2},{7,3},{8,12},{9,13},{10,... | collective-permute-start | bytes 589832 | tf_op jit(solution)/shard_map/ppermute | solution.py:238
  250.1 16.2 %collective-permute-start.43 = (bf16[128,768]{1,0:T(8,128)(2,1)}, bf16[128,768]{1,0:T(8,128)(2,1)}, u32[]{:S(2)}, u32[]{:S(2)}) collective-permute-start(bf16[128,768]{1,0:T(8,128)(2,1)} %get-tuple-element.57), channel_id=1, source_target_pairs={{0,6},{1,7},{2,0},{3,1},{4,2},{5,3},{6,4},{7,5},{8,14},{9,15},{10,... | collective-permute-start | bytes 589832 | tf_op jit(solution)/shard_map/ppermute | solution.py:238
  266.3 15.1 %collective-permute-start.52 = (bf16[2,4,64,768]{3,2,1,0:T(8,128)(2,1)S(1)}, bf16[2,4,64,768]{3,2,1,0:T(8,128)(2,1)S(1)}, u32[]{:S(2)}, u32[]{:S(2)}) collective-permute-start(bf16[2,4,64,768]{3,2,1,0:T(8,128)(2,1)S(1)} %fusion.10), channel_id=1, source_target_pairs={{0,1},{1,0},{2,3},{3,2},{4,5},{5,4},{6,7},{7,6},{8,9},{9,8},{10,11... | collective-permute-start | bytes 2359304 | tf_op jit(solution)/shard_map/ppermute | solution.py:273
  274.5 31.4 %collective-permute-start.59 = (bf16[4,48,1536]{2,1,0:T(8,128)(2,1)S(1)}, bf16[4,48,1536]{2,1,0:T(8,128)(2,1)S(1)}, u32[]{:S(2)}, u32[]{:S(2)}) collective-permute-start(bf16[4,48,1536]{2,1,0:T(8,128)(2,1)S(1)} %fusion.12), channel_id=1, source_target_pairs={{0,8},{8,0},{1,9},{9,1},{2,10},{10,2},{3,11},{11,3},{4,12},{12,4},... | collective-permute-start | bytes 1769480 | tf_op jit(solution)/shard_map/ppermute | solution.py:241
  306.0 16.2 %collective-permute-start.60 = (bf16[4,48,1536]{2,1,0:T(8,128)(2,1)S(1)}, bf16[4,48,1536]{2,1,0:T(8,128)(2,1)S(1)}, u32[]{:S(2)}, u32[]{:S(2)}) collective-permute-start(bf16[4,48,1536]{2,1,0:T(8,128)(2,1)S(1)} %fusion.9), channel_id=1, source_target_pairs={{0,16},{16,0},{1,17},{17,1},{2,18},{18,2},{3,19},{19,3},{4,20},{20... | collective-permute-start | bytes 1769480 | tf_op jit(solution)/shard_map/ppermute | solution.py:241
  (110 other events, 830.1 us)

commit v2 on v1

--- a/solution.py
+++ b/solution.py
@@ -229,6 +229,7 @@
         self.group = index // self.members
         self.member = index % self.members
         self.seq = lax.axis_index("seq")
+        self.rep = lax.axis_index("rep")
         self.inner = [
             [g * self.members + m for m in range(self.members)] for g in range(GROUPS)
         ]
@@ -556,12 +557,826 @@
     )
 
 
+def vmem(shape):
+    return pl.BlockSpec(shape, lambda *_: tuple(0 for _ in shape))
+
+
+SMEM = pl.BlockSpec(memory_space=pltpu.SMEM)
+
+
+def call(body, name, inputs, outputs, scratch=(), grid=(1,), in_specs=None, out_specs=None, flops=0):
+    shapes = [jax.ShapeDtypeStruct(shape, kind) for shape, kind in outputs]
+    if in_specs is None:
+        in_specs = [SMEM if item.ndim == 1 else vmem(item.shape) for item in inputs]
+    if out_specs is None:
+        out_specs = [vmem(shape) for shape, kind in outputs]
+    moved = sum(item.size * item.dtype.itemsize for item in list(inputs) + shapes)
+    return pl.pallas_call(
+        body,
+        grid=grid,
+        in_specs=in_specs,
+        out_specs=out_specs,
+        out_shape=shapes,
+        scratch_shapes=list(scratch),
+        name=name,
+        cost_estimate=pl.CostEstimate(flops=flops, transcendentals=0, bytes_accessed=moved),
+    )(*inputs)
+
+
+def pack_joined(ids, weight, vectors, widen_bias, cols):
+    kb = weight.shape[0]
+    vectors = [item[None] for item in vectors]
+    shape = (kb + 16, 3 * cols)
+
+    def body(*refs):
+        ids_ref, w_ref, wide_ref = refs[0], refs[1], refs[10]
+        all_ref = refs[15]
+        rows = [ref[...].astype(F32) for ref in refs[2:10]]
+        wide = wide_ref[...].astype(F32)
+        rows += [wide[:, k * kb : (k + 1) * kb] for k in range(8)]
+        small = jnp.concatenate(rows, axis=0).astype(BF)
+        for g in range(GROUPS):
+            for part in range(3):
+                at = (part * GROUPS + g) * cols
+                all_ref[g, :kb, part * cols : (part + 1) * cols] = w_ref[:, at : at + cols]
+            all_ref[g, kb:, :] = jnp.zeros((16, 3 * cols), BF)
+            all_ref[g, kb:, :kb] = small
+        for k in range(GROUPS):
+            refs[11 + k][...] = all_ref[(ids_ref[0] + k) % GROUPS]
+
+    inputs = [ids, weight] + vectors + [widen_bias[None]]
+    return call(
+        body,
+        "pack_joined",
+        inputs,
+        [(shape, BF)] * GROUPS,
+        scratch=[pltpu.VMEM((GROUPS,) + shape, BF)],
+    )
+
+
+def place_rows(ids_ref, pieces, out_ref, kb, relative=False):
+    group, m, y = ids_ref[0], ids_ref[1], ids_ref[2]
+    for index, piece in enumerate(pieces):
+        row = y if index % 2 == 0 else 1 - y
+        member = m if index < 2 else 1 - m
+        for g in range(GROUPS):
+            source = (group + GROUPS - g) % GROUPS if relative else g
+            start = pl.multiple_of((row * GROUPS * 2 + source * 2 + member) * kb, 16)
+            out_ref[pl.ds(start, kb), :] = piece[g, :kb, :]
+
+
+def assemble_joined(ids, pieces, kb):
+    cols = pieces[0].shape[2]
+    near = cols // 3
+    width = 4 * GROUPS * kb
+    span = 8 * kb
+
+    def body(ids_ref, a_ref, b_ref, c_ref, d_ref, w_ref, vec_ref, near_ref, wide_ref):
+        place_rows(ids_ref, (a_ref, b_ref, c_ref, d_ref), w_ref, kb, True)
+        g, m, y = ids_ref[0], ids_ref[1], ids_ref[2]
+        blocks = []
+        for row in range(2):
+            for k in range(GROUPS):
+                for member in range(2):
+                    turn = (g + GROUPS - k) % GROUPS
+                    picks = [ref[turn, kb:, :kb].astype(F32) for ref in (a_ref, b_ref, c_ref, d_ref)]
+                    mine = jnp.where(row == y, picks[0], picks[1])
+                    theirs = jnp.where(row == y, picks[2], picks[3])
+                    blocks.append(jnp.where(member == m, mine, theirs))
+        vec = jnp.concatenate(blocks, axis=1)
+        vec_ref[...] = vec
+        total = jnp.zeros((16, near), F32)
+        for k in range(GROUPS):
+            total = jnp.where(g == k, vec[:, k * near : (k + 1) * near], total)
+        near_ref[...] = total
+        lines = []
+        for chunk in range(4):
+            block = jnp.zeros((8, kb), F32)
+            for k in range(GROUPS):
+                at = (chunk * GROUPS + k) * kb
+                block = jnp.where(g == k, vec[8:16, at : at + kb], block)
+            lines += [block[i : i + 1] for i in range(8)]
+        wide_ref[...] = jnp.concatenate(lines, axis=1)
+
+    return call(
+        body,
+        "assemble_joined",
+        [ids] + list(pieces),
+        [((width, cols), BF), ((16, width), F32), ((16, near), F32), ((1, 4 * span), F32)],
+    )
+
+
+def assemble_rows(ids, pieces, name):
+    kb = pieces[0].shape[1]
+    cols = pieces[0].shape[2]
+
+    def body(ids_ref, a_ref, b_ref, c_ref, d_ref, w_ref):
+        place_rows(ids_ref, (a_ref, b_ref, c_ref, d_ref), w_ref, kb)
+
+    return call(body, name, [ids] + list(pieces), [((4 * GROUPS * kb, cols), BF)])[0]
+
+
+def assemble_narrow(ids, pieces):
+    rows, cols = pieces[0].shape
+
+    def body(ids_ref, a_ref, b_ref, c_ref, d_ref, w_ref):
+        m, y = ids_ref[1], ids_ref[2]
+        for index, ref in enumerate((a_ref, b_ref, c_ref, d_ref)):
+            row = y if index % 2 == 0 else 1 - y
+            member = m if index < 2 else 1 - m
+            start = pl.multiple_of((row * 2 + member) * rows, 16)
+            w_ref[pl.ds(start, rows), :] = ref[...]
+
+    return call(body, "assemble_narrow", [ids] + list(pieces), [((4 * rows, cols), BF)])[0]
+
+
+def split_joined(x_four, weight, near, scale):
+    count, width = x_four.shape
+    cols = weight.shape[1] // 3
+
+    def body(x_ref, w_ref, near_ref, q_ref, kv_ref):
+        joined = dot_nn(x_ref[...], w_ref[...])
+        q_ref[...] = ((joined[:, :cols] + near_ref[0:1, :]) * scale).astype(BF)
+        kv_ref[:, :cols] = joined[:, cols : 2 * cols].astype(BF)
+        kv_ref[:, cols:] = (joined[:, 2 * cols :] + near_ref[1:2, :]).astype(BF)
+
+    return call(
+        body,
+        "split_joined",
+        [x_four, weight, near],
+        [((count, cols), BF), ((count, 2 * cols), BF)],
+        flops=2 * count * width * 3 * cols,
+    )
+
+
+def piece_rows(ids_ref, k, rows, sign=1):
+    turn = (ids_ref[0] + (k if sign > 0 else GROUPS - k)) % GROUPS
+    return pl.ds(pl.multiple_of(turn * rows, 16), rows)
+
+
+def attend(ids, slopes, queries, kv_own, kv_other, q_col, k_row):
+    count, cols = queries.shape
+    heads = cols // HEAD_DIM
+    rows = count // GROUPS
+    chunk = kv_own.shape[0]
+
+    def body(ids_ref, slope_ref, q_ref, own_ref, other_ref, qi_ref, ki_ref, out_ref, inv_ref, *sends):
+        q = q_ref[...]
+        qpos = qi_ref[:, 0:1]
+        qseg = qi_ref[:, 1:2]
+        ones = jnp.ones((chunk, 64), BF)
+        q_heads = [only_head(q, head) for head in range(heads)]
+        accs = [None] * heads
+        for side, kv_ref in enumerate((own_ref, other_ref)):
+            here = slice(side * chunk, (side + 1) * chunk)
+            keys = kv_ref[:, :cols]
+            values = jnp.concatenate([kv_ref[:, cols:], ones], axis=1)
+            far = jnp.where(qseg == ki_ref[1:2, here], jnp.abs(qpos - ki_ref[0:1, here]), FAR)
+            for head in range(heads):
+                scores = dot_nt(q_heads[head], keys) - slope_ref[head] * far
+                part = dot_nn(jnp.exp(scores).astype(BF), values)
+                accs[head] = part if side == 0 else accs[head] + part
+        total = jnp.zeros((count, cols), F32)
+        for head in range(heads):
+            inv = 1.0 / accs[head][:, cols : cols + 1]
+            inv_ref[head] = jnp.transpose(jnp.broadcast_to(inv, (count, 128)))[:8]
+            total = total + only_head(accs[head][:, :cols] * inv, head)
+        out_ref[...] = total
+        for k, ref in enumerate(sends):
+            ref[...] = out_ref[piece_rows(ids_ref, k, rows), :].astype(BF)
+
+    return call(
+        body,
+        "attend",
+        [ids, slopes, queries, kv_own, kv_other, q_col, k_row],
+        [((count, cols), F32), ((heads, 8, count), F32)] + [((rows, cols), BF)] * GROUPS,
+        flops=4 * count * 2 * chunk * cols,
+    )
+
+
+def attend_back(ids, slopes, queries, back_rel, mixed, inv, kv_own, kv_other, q_row, k_col, scale):
+    count, cols = queries.shape
+    heads = cols // HEAD_DIM
+    rows = count // GROUPS
+    chunk = kv_own.shape[0]
+
+    def body(ids_ref, slope_ref, q_ref, *refs):
+        pieces = refs[:GROUPS]
+        out_ref, inv_ref, own_ref, other_ref, qi_ref, ki_ref, dq_ref, keep_ref, give_ref, do_ref = refs[GROUPS:]
+        for k, ref in enumerate(pieces):
+            do_ref[piece_rows(ids_ref, k, rows, -1), :] = ref[...]
+        q = q_ref[...]
+        back = do_ref[...]
+        product = back.astype(F32) * out_ref[...]
+        qpos = qi_ref[0:1, :]
+        qseg = qi_ref[1:2, :]
+        q_heads = [only_head(q, head) for head in range(heads)]
+        b_heads = [only_head(back, head) for head in range(heads)]
+        place = lax.broadcasted_iota(jnp.int32, (8, cols), 0)
+        lane = lax.broadcasted_iota(jnp.int32, (8, cols), 1)
+        row_dots = lax.dot_general(
+            (lane // HEAD_DIM == place).astype(F32),
+            product,
+            (((1,), (1,)), ((), ())),
+            precision=lax.Precision.HIGHEST,
+            preferred_element_type=F32,
+        )
+        query_parts = [None] * heads
+        for side, kv_ref in enumerate((own_ref, other_ref)):
+            here = slice(side * chunk, (side + 1) * chunk)
+            keys = kv_ref[:, :cols]
+            values = kv_ref[:, cols:]
+            far = jnp.where(qseg == ki_ref[here, 1:2], jnp.abs(qpos - ki_ref[here, 0:1]), FAR)
+            key_part = None
+            value_part = None
+            for head in range(heads):
+                scores = dot_nt(keys, q_heads[head]) - slope_ref[head] * far
+                probs = jnp.exp(scores) * inv_ref[head, 0:1, :]
+                prob_back = dot_nt(values, b_heads[head])
+                score_back = (probs * (prob_back - row_dots[head : head + 1])).astype(BF)
+                k_part = dot_nn(score_back, q_heads[head])
+                v_part = dot_nn(probs.astype(BF), b_heads[head])
+                q_part = dot_tn(score_back, keys)
+                key_part = k_part if head == 0 else key_part + k_part
+                value_part = v_part if head == 0 else value_part + v_part
+                query_parts[head] = q_part if side == 0 else query_parts[head] + q_part
+            target = keep_ref if side == 0 else give_ref
+            target[:, :cols] = key_part.astype(target.dtype)
+            target[:, cols:] = value_part.astype(target.dtype)
+        total = jnp.zeros((count, cols), F32)
+        for head in range(heads):
+            total = total + only_head(query_parts[head], head)
+        dq_ref[...] = (total.astype(BF).astype(F32) * scale).astype(BF)
+
+    return call(
+        body,
+        "attend_back",
+        [ids, slopes, queries] + list(back_rel) + [mixed, inv, kv_own, kv_other, q_row, k_col],
+        [((count, cols), BF), ((chunk, 2 * cols), F32), ((chunk, 2 * cols), BF)],
+        scratch=[pltpu.VMEM((count, cols), BF)],
+        flops=10 * count * 2 * chunk * cols,
+    )
+
+
+def close_attention(ids, inputs, mixed_rel, weight, vec):
+    rows, width = inputs.shape
+    cols = mixed_rel[0].shape[1]
+
+    def body(ids_ref, x_ref, a_ref, b_ref, c_ref, d_ref, w_ref, vec_ref, first_ref, low_ref, unit_ref, root_ref):
+        total = x_ref[...].astype(F32) + vec_ref[2:3, :]
+        for k, ref in enumerate((a_ref, b_ref, c_ref, d_ref)):
+            total = total + dot_nn(ref[...], w_ref[piece_rows(ids_ref, k, cols, -1), :])
+        unit, root = norm_stats(total)
+        first = unit * vec_ref[3:4, :] + vec_ref[4:5, :]
+        first_ref[...] = first
+        low_ref[...] = first.astype(BF)
+        unit_ref[...] = unit
+        root_ref[...] = root
+
+    return call(
+        body,
+        "close_attention",
+        [ids, inputs] + list(mixed_rel) + [weight, vec],
+        [((rows, width), F32), ((rows, width), BF), ((rows, width), F32), ((rows, 1), F32)],
+        flops=2 * rows * width * width,
+    )
+
+
+def block_of(quarter):
+    return math.gcd(quarter, 256)
+
+
+def join_pieces(refs):
+    return jnp.concatenate([ref[...] for ref in refs], axis=0)
+
+
+def send_pieces(total, refs, rows):
+    for k, ref in enumerate(refs):
+        ref[...] = total[k * rows : (k + 1) * rows, :].astype(ref.dtype)
+
+
+def widen_narrow(rel, w_gate, w_up, w_narrow, wide):
+    rows, width = rel[0].shape
+    quarter = w_narrow.shape[0]
+    count = GROUPS * rows
+
+    def body(*refs):
+        wg_ref, wu_ref, wn_ref, wide_ref = refs[4:8]
+        hid_ref, gate_ref, up_ref = refs[12:15]
+        value = join_pieces(refs[:4])
+        gate = dot_nn(value, wg_ref[...]) + wide_ref[:, :quarter]
+        up = dot_nn(value, wu_ref[...]) + wide_ref[:, quarter:]
+        gate_ref[...] = gate
+        up_ref[...] = up
+        hidden = (gate * (0.5 + 0.5 * lax.erf(gate * math.sqrt(0.5))) * up).astype(BF)
+        hid_ref[...] = hidden
+        send_pieces(dot_nn(hidden, wn_ref[...]), refs[8:12], rows)
+
+    return call(
+        body,
+        "widen_narrow",
+        list(rel) + [w_gate, w_up, w_narrow, wide],
+        [((rows, width), F32)]
+        + [((rows, width), BF)] * 3
+        + [((count, quarter), BF), ((count, quarter), F32), ((count, quarter), F32)],
+        flops=6 * count * width * quarter,
+    )
+
+
+def gate_slopes(gate, up):
+    phi_big = 0.5 + 0.5 * lax.erf(gate * math.sqrt(0.5))
+    slope = phi_big + gate * jnp.exp(-0.5 * gate * gate) * (1.0 / math.sqrt(2.0 * math.pi))
+    return up * slope, gate * phi_big
+
+
+def widen_narrow_back(rel, w_gate, w_up, w_narrow, gate_factor, up_factor):
+    rows, width = rel[0].shape
+    quarter = w_narrow.shape[0]
+    count = GROUPS * rows
+
+    def body(*refs):
+        wg_ref, wu_ref, wn_ref, gf_ref, uf_ref = refs[4:9]
+        bg_ref, bu_ref = refs[13:15]
+        hidden_back = dot_nt(join_pieces(refs[:4]), wn_ref[...])
+        gate_back = (hidden_back * gf_ref[...]).astype(BF)
+        up_back = (hidden_back * uf_ref[...]).astype(BF)
+        bg_ref[...] = gate_back
+        bu_ref[...] = up_back
+        total = dot_nt(gate_back, wg_ref[...]) + dot_nt(up_back, wu_ref[...])
+        send_pieces(total, refs[9:13], rows)
+
+    return call(
+        body,
+        "widen_narrow_back",
+        list(rel) + [w_gate, w_up, w_narrow, gate_factor, up_factor],
+        [((rows, width), F32)] + [((rows, width), BF)] * 3 + [((count, quarter), BF)] * 2,
+        flops=6 * count * width * quarter,
+    )
+
+
+def turn_final(own, received, first, upstream, vec):
+    rows, width = own.shape
+
+    def body(own_ref, a_ref, b_ref, c_ref, first_ref, up_ref, vec_ref, res_ref, back_ref, low_ref, sum_ref):
+        total = first_ref[...] + vec_ref[5:6, :] + own_ref[...]
+        for ref in (a_ref, b_ref, c_ref):
+            total = total + ref[...].astype(F32)
+        unit, root = norm_stats(total)
+        gain = vec_ref[6:7, :]
+        res_ref[...] = (unit * gain + vec_ref[7:8, :]).astype(BF)
+        upstream = up_ref[...].astype(F32)
+        back = norm_back(unit, root, gain, upstream)
+        low = back.astype(BF)
+        back_ref[...] = back
+        low_ref[...] = low
+        sum_ref[...] = jnp.zeros_like(sum_ref)
+        sum_ref[0:1, :] = jnp.sum(low.astype(F32), axis=0, keepdims=True)
+        sum_ref[1:2, :] = jnp.sum(upstream * unit, axis=0, keepdims=True)
+        sum_ref[2:3, :] = jnp.sum(upstream, axis=0, keepdims=True)
+
+    return call(
+        body,
+        "turn_final",
+        [own] + list(received) + [first, upstream, vec],
+        [((rows, width), BF), ((rows, width), F32), ((rows, width), BF), ((8, width), F32)],
+    )
+
+
+def turn_first(ids, own, received, final_back, unit, root, weight, vec):
+    rows, width = own.shape
+    cols = width // GROUPS
+
+    def body(ids_ref, own_ref, a_ref, b_ref, c_ref, fb_ref, unit_ref, root_ref, w_ref, vec_ref, *outs):
+        attn_ref, low_ref, sum_ref = outs[:3]
+        total = fb_ref[...] + own_ref[...]
+        for ref in (a_ref, b_ref, c_ref):
+            total = total + ref[...].astype(F32)
+        unit = unit_ref[...]
+        back = norm_back(unit, root_ref[...], vec_ref[3:4, :], total)
+        low = back.astype(BF)
+        attn_ref[...] = back
+        low_ref[...] = low
+        for k, ref in enumerate(outs[3:]):
+            ref[...] = dot_nt(low, w_ref[piece_rows(ids_ref, k, cols), :]).astype(BF)
+        sum_ref[...] = jnp.zeros_like(sum_ref)
+        sum_ref[0:1, :] = jnp.sum(low.astype(F32), axis=0, keepdims=True)
+        sum_ref[1:2, :] = jnp.sum(total * unit, axis=0, keepdims=True)
+        sum_ref[2:3, :] = jnp.sum(total, axis=0, keepdims=True)
+
+    return call(
+        body,
+        "turn_first",
+        [ids, own] + list(received) + [final_back, unit, root, weight, vec],
+        [((rows, width), F32), ((rows, width), BF), ((8, width), F32)] + [((rows, cols), BF)] * GROUPS,
+        flops=2 * rows * width * width,
+    )
+
+
+def split_rows(ids_ref, full_ref, keep_ref, give_ref, kb, lead=()):
+    m, y = ids_ref[1], ids_ref[2]
+    for turn in range(2):
+        row = y if turn == 0 else 1 - y
+        for g in range(GROUPS):
+            base = (row * GROUPS + g) * 2
+            mine = pl.ds(pl.multiple_of((base + m) * kb, 16), kb)
+            other = pl.ds(pl.multiple_of((base + 1 - m) * kb, 16), kb)
+            keep_ref[lead + (turn, g, slice(0, kb), slice(None))] = full_ref[mine, :]
+            give_ref[lead + (turn, g, slice(0, kb), slice(None))] = full_ref[other, :].astype(BF)
+
+
+def widen_grads(ids, rel, gate_back, up_back, kb):
+    rows, width = rel[0].shape
+    count, quarter = gate_back.shape
+    block = block_of(quarter)
+    steps = quarter // block
+
+    def body(ids_ref, a_ref, b_ref, c_ref, d_ref, gate_ref, up_ref, keep_ref, give_ref, gs_ref, us_ref, full_ref):
+        value = jnp.concatenate([a_ref[...], b_ref[...], c_ref[...], d_ref[...]], axis=0)
+        x = ids_ref[3]
+        for turn, (ref, sum_ref) in enumerate(((gate_ref, gs_ref), (up_ref, us_ref))):
+            back = ref[...]
+            full_ref[...] = dot_tn(value, back)
+            sum_ref[...] = jnp.sum(back.astype(F32), axis=0, keepdims=True)
+            split_rows(ids_ref, full_ref, keep_ref, give_ref, kb, ((x + turn) % 2,))
+
+    piece = vmem((rows, width))
+    tall = pl.BlockSpec((count, block), lambda i: (0, i))
+    line = pl.BlockSpec((1, block), lambda i: (0, i))
+    cut = pl.BlockSpec((2, 2, GROUPS, kb, block), lambda i: (0, 0, 0, 0, i))
+    shape = (2, 2, GROUPS, kb, quarter)
+    return call(
+        body,
+        "widen_grads",
+        [ids] + list(rel) + [gate_back, up_back],
+        [(shape, F32), (shape, BF), ((1, quarter), F32), ((1, quarter), F32)],
+        scratch=[pltpu.VMEM((width, block), F32)],
+        grid=(steps,),
+        in_specs=[SMEM] + [piece] * 4 + [tall] * 2,
+        out_specs=[cut, cut, line, line],
+        flops=4 * count * width * quarter,
+    )
+
+
+def narrow_grads(ids, hidden, rel):
+    rows, width = rel[0].shape
+    count, quarter = hidden.shape
+    own = quarter // 4
+
+    def body(ids_ref, h_ref, a_ref, b_ref, c_ref, d_ref, keep_ref, give_ref, full_ref):
+        value = jnp.concatenate([a_ref[...], b_ref[...], c_ref[...], d_ref[...]], axis=0)
+        full_ref[...] = dot_tn(h_ref[...], value)
+        m, y = ids_ref[1], ids_ref[2]
+        for turn in range(2):
+            base = (y if turn == 0 else 1 - y) * 2
+            mine = pl.ds(pl.multiple_of((base + m) * own, 16), own)
+            other = pl.ds(pl.multiple_of((base + 1 - m) * own, 16), own)
+            keep_ref[turn] = full_ref[mine, :]
+            give_ref[turn] = full_ref[other, :].astype(BF)
+
+    return call(
+        body,
+        "narrow_grads",
+        [ids, hidden] + list(rel),
+        [((2, own, width), F32), ((2, own, width), BF)],
+        scratch=[pltpu.VMEM((quarter, width), F32)],
+        flops=2 * count * width * quarter,
+    )
+
+
+def place_small(ids_ref, blocks, keep_ref, give_ref, kb):
+    m, y = ids_ref[1], ids_ref[2]
+    for turn in range(2):
+        for g in range(GROUPS):
+            picked = []
+            for member in range(2):
+                first = jnp.where(y == 0, blocks[0][g][member], blocks[1][g][member])
+                second = jnp.where(y == 0, blocks[1][g][member], blocks[0][g][member])
+                picked.append(first if turn == 0 else second)
+            cols = keep_ref.shape[3]
+            mine = jnp.where(m == 0, picked[0], picked[1])
+            other = jnp.where(m == 0, picked[1], picked[0])
+            keep_ref[turn, g, kb:, :] = jnp.zeros((16, cols), F32)
+            give_ref[turn, g, kb:, :] = jnp.zeros((16, cols), BF)
+            keep_ref[turn, g, kb:, :kb] = mine
+            give_ref[turn, g, kb:, :kb] = other.astype(BF)
+
+
+def output_grads(ids, mixed_rel, back, first_sums, final_sums, gate_sum, up_sum, kb):
+    rows, width = back.shape
+    cols = mixed_rel[0].shape[1]
+
+    def body(ids_ref, *refs):
+        back_ref, fs_ref, ls_ref, gs_ref, us_ref, keep_ref, give_ref, full_ref = refs[GROUPS:]
+        for k, ref in enumerate(refs[:GROUPS]):
+            full_ref[piece_rows(ids_ref, k, cols, -1), :] = dot_tn(ref[...], back_ref[...])
+        split_rows(ids_ref, full_ref, keep_ref, give_ref, kb)
+        g_own = ids_ref[0]
+        sums = jnp.concatenate([fs_ref[0:3, :], ls_ref[0:3, :]], axis=0)
+        wide = (gs_ref[...], us_ref[...])
+        span = 8 * kb
+        blocks = []
+        for row in range(2):
+            blocks.append([])
+            for g in range(GROUPS):
+                blocks[-1].append([])
+                for member in range(2):
+                    b = row * 8 + g * 2 + member
+                    part = wide[b // 8][:, ((b // 4) % 2) * span : ((b // 4) % 2 + 1) * span]
+                    part = jnp.where(g_own == b % GROUPS, part, 0.0)
+                    lines = [part[:, i * kb : (i + 1) * kb] for i in range(8)]
+                    lines = [sums[:, b * kb : (b + 1) * kb]] + lines + [jnp.zeros((2, kb), F32)]
+                    blocks[-1][-1].append(jnp.concatenate(lines, axis=0))
+        place_small(ids_ref, blocks, keep_ref, give_ref, kb)
+
+    shape = (2, GROUPS, kb + 16, width)
+    return call(
+        body,
+        "output_grads",
+        [ids] + list(mixed_rel) + [back, first_sums, final_sums, gate_sum, up_sum],
+        [(shape, F32), (shape, BF)],
+        scratch=[pltpu.VMEM((width, width), F32)],
+        flops=2 * rows * width * width,
+    )
+
+
+def tokens_parts(ids, back, weight):
+    count, cols = back.shape
+    rows = count // GROUPS
+    width = weight.shape[0]
+
+    def body(ids_ref, jb_ref, w_ref, *outs):
+        for k, ref in enumerate(outs):
+            part = dot_nt(jb_ref[piece_rows(ids_ref, k, rows, -1), :], w_ref[...])
+            ref[...] = part.astype(ref.dtype)
+
+    return call(
+        body,
+        "tokens_parts",
+        [ids, back, weight],
+        [((rows, width), F32)] + [((rows, width), BF)] * 3,
+        flops=2 * count * width * cols,
+    )
+
+
+def joined_grads(ids, x_four, query_back, keep, got, kb):
+    count, width = x_four.shape
+    cols = query_back.shape[1]
+    wide = 3 * cols
+
+    def body(ids_ref, x_ref, q_ref, kv_ref, got_ref, keep_ref, give_ref, back_ref, full_ref):
+        back_ref[:, :cols] = q_ref[...]
+        back_ref[:, cols:] = (kv_ref[...] + got_ref[...].astype(F32)).astype(BF)
+        full_ref[...] = dot_tn(x_ref[...], back_ref[...])
+        split_rows(ids_ref, full_ref, keep_ref, give_ref, kb)
+        g_own = ids_ref[0]
+        sums = jnp.sum(back_ref[...].astype(F32), axis=0, keepdims=True)
+        pair = jnp.concatenate([sums[:, :cols], sums[:, 2 * cols :], jnp.zeros((14, cols), F32)], axis=0)
+        blocks = []
+        for row in range(2):
+            blocks.append([])
+            for g in range(GROUPS):
+                blocks[-1].append([])
+                for member in range(2):
+                    b = row * 8 + g * 2 + member
+                    part = pair[:, (b % GROUPS) * kb : (b % GROUPS + 1) * kb]
+                    blocks[-1][-1].append(jnp.where(g_own == b // GROUPS, part, 0.0))
+        place_small(ids_ref, blocks, keep_ref, give_ref, kb)
+
+    shape = (2, GROUPS, kb + 16, wide)
+    return call(
+        body,
+        "joined_grads",
+        [ids, x_four, query_back, keep, got],
+        [(shape, F32), (shape, BF), ((count, wide), BF)],
+        scratch=[pltpu.VMEM((width, wide), F32)],
+        flops=2 * count * width * wide,
+    )
+
+
+def finish_widen(ids, own, other):
+    kb, cols = own.shape[1:]
+    span = cols // 2
+
+    def body(ids_ref, own_ref, other_ref, out_ref):
+        x = ids_ref[3]
+        for part in range(2):
+            for g in range(GROUPS):
+                picked = jnp.where(x == part, own_ref[g].astype(F32), other_ref[g].astype(F32))
+                for row in range(2):
+                    at = ((part * 2 + row) * GROUPS + g) * span
+                    out_ref[:, at : at + span] = picked[:, row * span : (row + 1) * span]
+
+    return call(body, "finish_widen", [ids, own, other], [((kb, 4 * GROUPS * span), F32)])[0]
+
+
+def finish_joined(got, kb):
+    wide = got.shape[2]
+    cols = wide // 3
+
+    def body(got_ref, out_ref, small_ref):
+        for g in range(GROUPS):
+            for part in range(3):
+                at = (part * GROUPS + g) * cols
+                out_ref[:, at : at + cols] = got_ref[g, :kb, part * cols : (part + 1) * cols].astype(F32)
+        small = jnp.zeros((16, wide), F32)
+        for g in range(GROUPS):
+            small = small + got_ref[g, kb:, :].astype(F32)
+        small_ref[...] = small
+
+    return call(body, "finish_joined", [got], [((kb, GROUPS * wide), F32), ((16, wide), F32)])
+
+
+def fast_device(
+    tokens,
+    segments,
+    joined_weight,
+    query_bias,
+    value_bias,
+    output_weight,
+    output_bias,
+    first_gain,
+    first_shift,
+    widen_weight,
+    widen_bias,
+    narrow_weight,
+    narrow_bias,
+    final_gain,
+    final_shift,
+    cotangent,
+):
+    at = Layout()
+    n, r = at.size, at.members
+    rows, width = tokens.shape[1:]
+    heads = width // HEAD_DIM
+    near_heads = heads // GROUPS
+    cols = near_heads * HEAD_DIM
+    kb = joined_weight.shape[0]
+    ff_own = narrow_weight.shape[0]
+    quarter = 4 * ff_own
+    span = 2 * ff_own
+    seg_row = segments[0]
+    length = seg_row.shape[0]
+    scale = 1.0 / math.sqrt(HEAD_DIM)
+    inputs = tokens[0]
+    columns = [[g * r + m for g in range(GROUPS)] for m in range(r)]
+    ids = jnp.stack([at.group, at.member, at.seq, at.rep]).astype(jnp.int32)
+
+    def across(value):
+        return lax.all_to_all(value, "ctx", 0, 0, axis_index_groups=columns, tiled=True)
+
+    def spread_out(value):
+        far = at.swap(value, "seq")
+        return (value, far, at.partner(value), at.partner(far))
+
+    x_four = across(jnp.broadcast_to(inputs[None], (GROUPS, rows, width))).reshape(-1, width)
+    packed = pack_joined(
+        ids,
+        joined_weight,
+        [
+            query_bias,
+            value_bias,
+            output_bias,
+            first_gain,
+            first_shift,
+            narrow_bias,
+            final_gain,
+            final_shift,
+        ],
+        widen_bias,
+        cols,
+    )
+    joined_got = jnp.stack([packed[0]] + [at.shift(packed[k], k) for k in range(1, GROUPS)])
+    joined_parts = spread_out(joined_got)
+    w_joined, vec, near, wide = assemble_joined(ids, joined_parts, kb)
+    narrow_parts = spread_out(after(narrow_weight, joined_parts[1]))
+    output_cut = jnp.broadcast_to(after(output_weight, x_four)[None], (GROUPS, kb, width))
+    output_got = across(output_cut)
+    widen_cut = widen_weight.reshape(kb, 2, 2, GROUPS, span)
+    widen_got = [
+        across(
+            after(jnp.transpose(widen_cut[:, t], (2, 0, 1, 3)).reshape(GROUPS, kb, quarter), output_got)
+        )
+        for t in range(2)
+    ]
+
+    queries, kv_own = split_joined(x_four, w_joined, near, scale)
+    kv_other = at.partner(kv_own)
+    lanes = jnp.arange(rows, dtype=jnp.int32)
+
+    def places(member):
+        return ((jnp.arange(GROUPS, dtype=jnp.int32) * r + member)[:, None] * rows + lanes).reshape(-1)
+
+    by_member = jnp.transpose(seg_row.reshape(GROUPS, r, rows), (1, 0, 2)).reshape(r, -1)
+
+    def documents(member):
+        return lax.dynamic_index_in_dim(by_member, member, 0, keepdims=False)
+
+    q_row = jnp.stack([places(at.member), documents(at.member)]).astype(F32)
+    o_row = jnp.stack([places(1 - at.member), documents(1 - at.member)]).astype(F32)
+    k_row = jnp.concatenate([q_row, o_row], axis=1)
+    q_col = jnp.transpose(q_row)
+    k_col = jnp.transpose(k_row)
+    order_heads = at.group * near_heads + jnp.arange(near_heads, dtype=jnp.int32)
+    slopes = jnp.power(2.0, -8.0 * (order_heads.astype(F32) + 1.0) / heads) * (512.0 / length)
+    attended = attend(ids, slopes, queries, kv_own, kv_other, q_col, k_row)
+    mixed_near, inv = attended[:2]
+    mixed_send = attended[2:]
+    mixed_rel = [mixed_send[0]] + [at.shift(mixed_send[k], k) for k in range(1, GROUPS)]
+    w_output = assemble_rows(ids, spread_out(output_got), "assemble_output")
+    w_narrow = assemble_narrow(ids, narrow_parts)
+    w_gate = assemble_rows(ids, spread_out(widen_got[0]), "assemble_gate")
+    w_up = assemble_rows(ids, spread_out(widen_got[1]), "assemble_up")
+
+    first, first_low, first_unit, first_root = close_attention(ids, inputs, mixed_rel, w_output, vec)
+    first_rel = at.gather(first_low)
+    own, s1, s2, s3, hidden, gate, up = widen_narrow(first_rel, w_gate, w_up, w_narrow, wide)
+    received = [at.shift(s1, -1), at.shift(s2, -2), at.shift(s3, -3)]
+    gate_factor, up_factor = gate_slopes(gate, up)
+    result, final_back, narrow_back, final_sums = turn_final(own, received, first, cotangent[0], vec)
+
+    back_rel = at.gather(narrow_back)
+    own, s1, s2, s3, gate_back, up_back = widen_narrow_back(
+        back_rel, w_gate, w_up, w_narrow, gate_factor, up_factor
+    )
+    received = [at.shift(s1, -1), at.shift(s2, -2), at.shift(s3, -3)]
+    narrow_keep, narrow_give = narrow_grads(ids, hidden, back_rel)
+    widen_keep, widen_give, gate_sum, up_sum = widen_grads(ids, first_rel, gate_back, up_back, kb)
+    turned = turn_first(ids, own, received, final_back, first_unit, first_root, w_output, vec)
+    attn_back, output_back, first_sums = turned[:3]
+    back_send = turned[3:]
+    back_near = [back_send[0]] + [at.shift(back_send[k], k) for k in range(1, GROUPS)]
+
+    narrow_got = at.partner(after(narrow_give, received[2]))
+    widen_got = at.partner(after(widen_give, received[2]))
+    output_keep, output_give = output_grads(
+        ids, mixed_rel, output_back, first_sums, final_sums, gate_sum, up_sum, kb
+    )
+
+    def seq_send(keep, got):
+        return (keep + got.astype(F32)).astype(BF)
+
+    narrow_far = at.swap(seq_send(narrow_keep[1], narrow_got[1]), "seq")
+    widen_far = at.swap(seq_send(widen_keep[:, 1], widen_got[:, 1]), "seq")
+    output_got = at.partner(output_give)
+
+    query_back, kv_keep, kv_give = attend_back(
+        ids, slopes, queries, back_near, mixed_near, inv, kv_own, kv_other, q_row, k_col, scale
+    )
+    kv_give, narrow_far, widen_far, output_got = lax.optimization_barrier(
+        (kv_give, narrow_far, widen_far, output_got)
+    )
+    kv_got = at.partner(kv_give)
+
+    narrow_sum = (narrow_keep[0] + narrow_got[0].astype(F32) + narrow_far.astype(F32)).astype(BF)
+    narrow_total = narrow_sum.astype(F32) + at.swap(narrow_sum, "rep").astype(F32)
+    widen_sum = widen_keep[:, 0] + widen_got[:, 0].astype(F32) + widen_far.astype(F32)
+    widen_mine = widen_sum[0] + at.swap(widen_sum[1].astype(BF), "rep").astype(F32)
+    output_far = at.swap(seq_send(output_keep[1], output_got[1]), "seq")
+    output_sum = (output_keep[0] + output_got[0].astype(F32) + output_far.astype(F32)).astype(BF)
+
+    joined_keep, joined_give, joined_back = joined_grads(ids, x_four, query_back, kv_keep, kv_got, kb)
+    joined_got = at.partner(joined_give)
+    own, s1, s2, s3 = tokens_parts(ids, joined_back, w_joined)
+    received = [at.shift(s1, -1), at.shift(s2, -2), at.shift(s3, -3)]
+    joined_far = at.swap(seq_send(joined_keep[1], joined_got[1]), "seq")
+    joined_sum = (joined_keep[0] + joined_got[0].astype(F32) + joined_far.astype(F32)).astype(BF)
+    joined_mine = (joined_sum.astype(F32) + at.swap(joined_sum, "rep").astype(F32)).astype(BF)
+    widen_own = across(widen_mine.astype(BF))
+    widen_total = finish_widen(ids, widen_own, at.swap(widen_own, "rep"))
+    output_all = across(after(output_sum, widen_own))
+    output_mine = jnp.sum(output_all.astype(F32), axis=0).astype(BF)
+    output_total = output_mine.astype(F32) + at.swap(output_mine, "rep").astype(F32)
+    joined_total, pair = finish_joined(across(joined_mine), kb)
+    tokens_grad = attn_back + own
+    for item in received:
+        tokens_grad = tokens_grad + item.astype(F32)
+    last = output_total[kb:, :kb]
+    return (
+        result[None],
+        tokens_grad[None],
+        joined_total,
+        pair[0, :kb],
+        pair[1, :kb],
+        output_total[:kb],
+        last[0],
+        last[1],
+        last[2],
+        widen_total,
+        last[6:14].reshape(-1),
+        narrow_total,
+        last[3],
+        last[4],
+        last[5],
+    )
+
+
 def solution(mesh):
     tokens = P(("rep", "seq"), "ctx", None)
     matrix = P(("seq", "ctx"), None)
     vector = P(("seq", "ctx"))
+    near = mesh.shape["ctx"] == 2 * GROUPS and mesh.shape["rep"] == 2
     return jax.shard_map(
-        on_device,
+        fast_device if near else on_device,
         mesh=mesh,
         in_specs=(
             tokens,

time: 343 us -> 312 us (0.910)
  Pallas kernels: 24.9 us -> 75.3 us
  local copies, waits for them, and re-layouts: 50 us -> 21.6 us
  waiting for transfers between devices: 123 us -> 95.4 us
  matrix products: 20.3 us -> 0 us
  other arithmetic: 33.7 us -> 23.5 us
  starting transfers between devices: 87.8 us -> 93.1 us
    pallas_call x2 -> x21, Pallas kernels: 24.9 us -> 75.3 us  [call(): pl.pallas_call(body, grid=grid, in_specs=in_specs, out_specs=out_specs, o...]
    ppermute x45 -> x24, waiting for transfers between devices: 95.5 us -> 62.7 us  [shift(): lax.ppermute(value, 'ctx', [(i, (i + steps * r) % n) for i in range(n)])]
    ppermute x45 -> x24, starting transfers between devices: 74.7 us -> 44.7 us  [shift(): lax.ppermute(value, 'ctx', [(i, (i + steps * r) % n) for i in range(n)])]
    all_to_all x0 -> x7, starting transfers between devices: none -> 28.9 us  [across(): lax.all_to_all(value, 'ctx', 0, 0, axis_index_groups=columns, tiled=True)]
    all_to_all x0 -> x7, waiting for transfers between devices: none -> 22.9 us  [across(): lax.all_to_all(value, 'ctx', 0, 0, axis_index_groups=columns, tiled=True)]
    dot_general x12 -> x0, matrix products: 20.3 us -> none  [the longest x4 8.58 us: dot_nt(): lax.dot_general(left, right, (((1,), (1,)), ((), ())), preferred_element_...]
    ppermute x12 -> x14, waiting for transfers between devices: 27.2 us -> 9.81 us  [swap(): return lax.ppermute(value, axis, [(0, 1), (1, 0)])]
    convert_element_type x18 -> x1, local copies, waits for them, and re-layouts: 8.95 us -> 0.03 us  [fast_device(): widen_sum[1].astype(BF)]
  transfers between devices with their start and end apart: 67 -> 61, of which waited for: 28 -> 20; matrix products, arithmetic and copies ran while one was open for 22% -> 10% of each run, Pallas kernels for 7% -> 19%
where the time goes in v2:
time: 312 us; the launch traced here: 310 us
  waiting for transfers between devices  95.4 us (31%)
  starting transfers between devices  93.1 us (30%)
  Pallas kernels  75.3 us (24%)
  other arithmetic  23.5 us (8%)
  local copies, waits for them, and re-layouts  21.6 us (7%)
    pallas_call x21, Pallas kernels, call(): pl.pallas_call(body, grid=grid, in_specs=in_specs, out_specs=out_specs, o...  75.3 us
    ppermute x24, waiting for transfers between devices, shift(): lax.ppermute(value, 'ctx', [(i, (i + steps * r) % n) for i in range(n)])  62.7 us
    ppermute x24, starting transfers between devices, shift(): lax.ppermute(value, 'ctx', [(i, (i + steps * r) % n) for i in range(n)])  44.7 us
    all_to_all x7, starting transfers between devices, across(): lax.all_to_all(value, 'ctx', 0, 0, axis_index_groups=columns, tiled=True)  28.9 us
    all_to_all x7, waiting for transfers between devices, across(): lax.all_to_all(value, 'ctx', 0, 0, axis_index_groups=columns, tiled=True)  22.9 us
    ppermute x14, starting transfers between devices, swap(): return lax.ppermute(value, axis, [(0, 1), (1, 0)])  17.7 us
    ppermute x14, waiting for transfers between devices, swap(): return lax.ppermute(value, axis, [(0, 1), (1, 0)])  9.81 us
    unnamed x119, local copies, waits for them, and re-layouts  7.93 us
  transfers between devices with their start and end apart: 61, of which 20 were waited for; matrix products, arithmetic and copies ran while one was open for 10% of the time, Pallas kernels for 19%

profile of v2, /device:TPU:0, one launch (start us, length us, event | category | flops | bytes accessed | tf_op | source)
XLA Modules:
  0.0 310.2 jit_solution(777361975652268918)
XLA Ops:
  2.6 6.3 %all-to-all-start = ((bf16[4,128,768]{2,1,0:T(8,128)(2,1)}), bf16[4,128,768]{2,1,0:T(8,128)(2,1)S(1)}, u32[]{:S(2)}, u32[]{:S(2)}) async-start(bf16[4,128,768]{2,1,0:T(8,128)(2,1)} %broadcast_in_dim.48), calls=%async_computation | async-start | bytes 1572864 | tf_op jit(solution)/shard_map/all_to_all | solution.py:1225
  19.9 13.7 %all-to-all-done = bf16[4,128,768]{2,1,0:T(8,128)(2,1)S(1)} async-done(((bf16[4,128,768]{2,1,0:T(8,128)(2,1)}), bf16[4,128,768]{2,1,0:T(8,128)(2,1)S(1)}, u32[]{:S(2)}, u32[]{:S(2)}) %all-to-all-start) | async-done | bytes 786464 | tf_op jit(solution)/shard_map/all_to_all | solution.py:1225
  39.6 6.1 %collective-permute-done.3.b_ref = bf16[4,64,576]{2,1,0:T(8,128)(2,1)S(1)} collective-permute-done((bf16[4,64,576]{2,1,0:T(8,128)(2,1)S(1)}, bf16[4,64,576]{2,1,0:T(8,128)(2,1)S(1)}, u32[]{:S(2)}, u32[]{:S(2)}) %collective-permute-start.3) | collective-permute-done | bytes 294944 | tf_op jit(solution)/shard_map/ppermute | solution.py:242
  46.0 4.5 %all-to-all-start.3 = ((bf16[4,48,768]{2,1,0:T(8,128)(2,1)}), bf16[4,48,768]{2,1,0:T(8,128)(2,1)S(1)}, u32[]{:S(2)}, u32[]{:S(2)}) async-start(bf16[4,48,768]{2,1,0:T(8,128)(2,1)} %reshape.130), calls=%async_computation.3 | async-start | bytes 589824 | tf_op jit(solution)/shard_map/all_to_all | solution.py:1225
  70.1 4.7 %attend.1 = (f32[512,192]{1,0:T(8,128)}, f32[3,8,512]{2,1,0:T(8,128)}, bf16[128,192]{1,0:T(8,128)(2,1)}, bf16[128,192]{1,0:T(8,128)(2,1)}, bf16[128,192]{1,0:T(8,128)(2,1)}, /*index=5*/bf16[128,192]{1,0:T(8,128)(2,1)}) custom-call(s32[4]{0:T(128)} %pad_add_fusion.refs_0_.ids_ref, f32[3]{0:T(128)} %power_multiply_fusion.slope_ref, ...), custom_call_target="tpu_custom_call" | custom-call | flops 402653184 | bytes 1634332 | tf_op jit(solution)/shard_map/attend/pallas_call | solution.py:574
  110.2 5.1 %collective-permute-done.14.refs_2_.c_ref = bf16[128,768]{1,0:T(8,128)(2,1)S(1)} collective-permute-done((bf16[128,768]{1,0:T(8,128)(2,1)}, bf16[128,768]{1,0:T(8,128)(2,1)S(1)}, u32[]{:S(2)}, u32[]{:S(2)}) %collective-permute-start.14) | collective-permute-done | bytes 196640 | tf_op jit(solution)/shard_map/ppermute | solution.py:239
  116.0 5.7 %widen_narrow.1 = (f32[128,768]{1,0:T(8,128)}, bf16[128,768]{1,0:T(8,128)(2,1)}, bf16[128,768]{1,0:T(8,128)(2,1)}, bf16[128,768]{1,0:T(8,128)(2,1)}, bf16[512,76...) custom-call(bf16[128,768]{1,0:T(8,128)(2,1)} %get-tuple-element.104.refs_0_.a_ref, ...), custom_call_target="tpu_custom_call" | custom-call | flops 1811939328 | bytes 9246720 | tf_op jit(solution)/shard_map/widen_narrow/pallas_call | solution.py:574
  121.6 5.8 %collective-permute-start.25 = (bf16[128,768]{1,0:T(8,128)(2,1)}, bf16[128,768]{1,0:T(8,128)(2,1)S(1)}, u32[]{:S(2)}, u32[]{:S(2)}) collective-permute-start(bf16[128,768]{1,0:T(8,128)(2,1)} %get-tuple-element.110), channel_id=1, source_target_pairs={{0,6},{1,7},{2,0},{3,1},{4,2},{5,3},{6,4},{7,5},{8,14},{9,15},{10,... | collective-permute-start | bytes 589832 | tf_op jit(solution)/shard_map/ppermute | solution.py:239
  128.1 5.0 %collective-permute-done.25.a_ref = bf16[128,768]{1,0:T(8,128)(2,1)S(1)} collective-permute-done((bf16[128,768]{1,0:T(8,128)(2,1)}, bf16[128,768]{1,0:T(8,128)(2,1)S(1)}, u32[]{:S(2)}, u32[]{:S(2)}) %collective-permute-start.25) | collective-permute-done | bytes 196640 | tf_op jit(solution)/shard_map/ppermute | solution.py:239
  133.1 12.3 %collective-permute-done.26.b_ref = bf16[128,768]{1,0:T(8,128)(2,1)S(1)} collective-permute-done((bf16[128,768]{1,0:T(8,128)(2,1)}, bf16[128,768]{1,0:T(8,128)(2,1)S(1)}, u32[]{:S(2)}, u32[]{:S(2)}) %collective-permute-start.26) | collective-permute-done | bytes 196640 | tf_op jit(solution)/shard_map/ppermute | solution.py:239
  153.1 3.7 %fusion.19 = (f32[512,768]{1,0:T(8,128)}, f32[512,768]{1,0:T(8,128)}) fusion(f32[512,768]{1,0:T(8,128)S(1)} %copy-done.3, f32[512,768]{1,0:T(8,128)} %get-tuple-element.116), kind=kLoop, calls=%fused_computation.60 | loop fusion | flops 3932160 | bytes 6291456 | tf_op jit(solution)/shard_map/mul | solution.py:889
  158.8 6.7 %collective-permute-done.29.refs_2_.c_ref = bf16[128,768]{1,0:T(8,128)(2,1)S(1)} collective-permute-done((bf16[128,768]{1,0:T(8,128)(2,1)}, bf16[128,768]{1,0:T(8,128)(2,1)S(1)}, u32[]{:S(2)}, u32[]{:S(2)}) %collective-permute-start.29) | collective-permute-done | bytes 196640 | tf_op jit(solution)/shard_map/ppermute | solution.py:239
  166.2 7.0 %widen_narrow_back.1 = (f32[128,768]{1,0:T(8,128)}, bf16[128,768]{1,0:T(8,128)(2,1)}, bf16[128,768]{1,0:T(8,128)(2,1)}, bf16[128,768]{1,0:T(8,128)(2,1)}, bf16[5...) custom-call(bf16[128,768]{1,0:T(8,128)(2,1)} %get-tuple-element.115.refs_0_.a_ref, bf16[128,768]{1,0:T(8,128)(2,1)} %copy-done.37, ...), custom_call_target="tpu_custom_call" | custom-call | flops 1811939328 | bytes 10027008 | tf_op jit(solution)/shard_map/widen_narrow_back/pallas_call | solution.py:574
  173.2 3.7 %collective-permute-start.33 = (bf16[128,768]{1,0:T(8,128)(2,1)}, bf16[128,768]{1,0:T(8,128)(2,1)S(1)}, u32[]{:S(2)}, u32[]{:S(2)}) collective-permute-start(bf16[128,768]{1,0:T(8,128)(2,1)} %get-tuple-element.121), channel_id=1, source_target_pairs={{0,2},{1,3},{2,4},{3,5},{4,6},{5,7},{6,0},{7,1},{8,10},{9,11},{10,... | collective-permute-start | bytes 589832 | tf_op jit(solution)/shard_map/ppermute | solution.py:239
  176.9 5.3 %widen_grads.1 = (f32[2,2,4,48,768]{4,3,2,1,0:T(8,128)}, bf16[2,2,4,48,768]{4,3,2,1,0:T(8,128)(2,1)}, f32[1,768]{1,0:T(1,128)}, f32[1,768]{1,0:T(1,128)}) custom-call(s32[4]{0:T(128)} %pad_add_fusion.refs_0_.ids_ref, bf16[128,768]{1,0:T(8,128)(2,1)} %get-tuple-element.104.refs_0_.a_ref, bf16[128,768]{1,0:T(8,128)(2,1)} %copy-done.50, ...), custom_call_target="tpu_custom_call" | custom-call | flops 1207959552 | bytes 5904400 | tf_op jit(solution)/shard_map/widen_grads/pallas_call | solution.py:574
  191.1 5.0 %collective-permute-done.31.a_ref = bf16[128,768]{1,0:T(8,128)(2,1)S(1)} collective-permute-done((bf16[128,768]{1,0:T(8,128)(2,1)S(1)}, bf16[128,768]{1,0:T(8,128)(2,1)S(1)}, u32[]{:S(2)}, u32[]{:S(2)}) %collective-permute-start.31) | collective-permute-done | bytes 196640 | tf_op jit(solution)/shard_map/ppermute | solution.py:239
  196.1 8.3 %collective-permute-done.32.b_ref = bf16[128,768]{1,0:T(8,128)(2,1)S(1)} collective-permute-done((bf16[128,768]{1,0:T(8,128)(2,1)S(1)}, bf16[128,768]{1,0:T(8,128)(2,1)S(1)}, u32[]{:S(2)}, u32[]{:S(2)}) %collective-permute-start.32) | collective-permute-done | bytes 196640 | tf_op jit(solution)/shard_map/ppermute | solution.py:239
  228.0 8.0 %attend_back.1 = (bf16[512,192]{1,0:T(8,128)(2,1)}, f32[512,384]{1,0:T(8,128)}, bf16[512,384]{1,0:T(8,128)(2,1)}) custom-call(s32[4]{0:T(128)} %pad_add_fusion.refs_0_.ids_ref, f32[3]{0:T(128)} %power_multiply_fusion.slope_ref, bf16[512,192]{1,0:T(8,128)(2,1)} %get-tuple-element.96.q_ref, bf16[128,192]{1,0:T(8,128)(2,1)} %get-tuple-element.126.refs_0_, ...), custom_call_target="tpu_custom_call" | custom-call | flops 1006632960 | bytes 3010588 | tf_op jit(solution)/shard_map/attend_back/pallas_call | solution.py:574
  239.8 4.3 %joined_grads.1 = (f32[2,4,64,576]{3,2,1,0:T(8,128)}, bf16[2,4,64,576]{3,2,1,0:T(8,128)(2,1)}, bf16[512,576]{1,0:T(8,128)(2,1)}) custom-call(s32[4]{0:T(128)} %pad_add_fusion.refs_0_.ids_ref, bf16[512,768]{1,0:T(8,128)(2,1)} %bitcast.92, bf16[512,192]{1,0:T(8,128)(2,1)} %get-tuple-element.132.q_ref, f32[512,384]{1,0:T(8,128)} %get-tuple-element.133.kv_ref, ...), custom_call_target="tpu_custom_call" | custom-call | flops 452984832 | bytes 4522000 | tf_op jit(solution)/shard_map/joined_grads/pallas_call | solution.py:574
  251.0 3.7 %all-to-all-start.5 = ((bf16[4,48,768]{2,1,0:T(8,128)(2,1)}), bf16[4,48,768]{2,1,0:T(8,128)(2,1)S(1)}, u32[]{:S(2)}, u32[]{:S(2)}) async-start(bf16[4,48,768]{2,1,0:T(8,128)(2,1)} %fusion.12), calls=%async_computation.5 | async-start | bytes 589824 | tf_op jit(solution)/shard_map/all_to_all | solution.py:1225
  261.1 3.8 %collective-permute-start.43 = (bf16[128,768]{1,0:T(8,128)(2,1)}, bf16[128,768]{1,0:T(8,128)(2,1)}, u32[]{:S(2)}, u32[]{:S(2)}) collective-permute-start(bf16[128,768]{1,0:T(8,128)(2,1)} %get-tuple-element.153), channel_id=1, source_target_pairs={{0,6},{1,7},{2,0},{3,1},{4,2},{5,3},{6,4},{7,5},{8,14},{9,15},{10,... | collective-permute-start | bytes 589832 | tf_op jit(solution)/shard_map/ppermute | solution.py:239
  268.0 4.0 %all-to-all-start.6 = ((bf16[4,64,768]{2,1,0:T(8,128)(2,1)}), bf16[4,64,768]{2,1,0:T(8,128)(2,1)S(1)}, u32[]{:S(2)}, u32[]{:S(2)}) async-start(bf16[4,64,768]{2,1,0:T(8,128)(2,1)} %fusion.8), calls=%async_computation.6 | async-start | bytes 786432 | tf_op jit(solution)/shard_map/all_to_all | solution.py:1225
  277.3 9.4 %collective-permute-done.44 = bf16[128,768]{1,0:T(8,128)(2,1)} collective-permute-done((bf16[128,768]{1,0:T(8,128)(2,1)}, bf16[128,768]{1,0:T(8,128)(2,1)}, u32[]{:S(2)}, u32[]{:S(2)}) %collective-permute-start.44) | collective-permute-done | bytes 196640 | tf_op jit(solution)/shard_map/ppermute | solution.py:239
  299.3 7.0 %all-to-all-done.4.got_ref = bf16[4,64,576]{2,1,0:T(8,128)(2,1)S(1)} async-done(((bf16[4,64,576]{2,1,0:T(8,128)(2,1)}), bf16[4,64,576]{2,1,0:T(8,128)(2,1)S(1)}, u32[]{:S(2)}, u32[]{:S(2)}) %all-to-all-start.4) | async-done | bytes 294944 | tf_op jit(solution)/shard_map/all_to_all | solution.py:1225
  (282 shorter events, 159.9 us)
Async XLA Ops:
  2.6 31.0 %all-to-all-start = ((bf16[4,128,768]{2,1,0:T(8,128)(2,1)}), bf16[4,128,768]{2,1,0:T(8,128)(2,1)S(1)}, u32[]{:S(2)}, u32[]{:S(2)}) async-start(bf16[4,128,768]{2,1,0:T(8,128)(2,1)} %broadcast_in_dim.48), calls=%async_computation | async-start | bytes 1572864 | tf_op jit(solution)/shard_map/all_to_all | solution.py:1225
  12.0 25.8 %collective-permute-start = (bf16[64,576]{1,0:T(8,128)(2,1)}, bf16[64,576]{1,0:T(8,128)(2,1)S(1)}, u32[]{:S(2)}, u32[]{:S(2)}) collective-permute-start(bf16[64,576]{1,0:T(8,128)(2,1)} %get-tuple-element.91), channel_id=1, source_target_pairs={{0,2},{1,3},{2,4},{3,5},{4,6},{5,7},{6,0},{7,1},{8,10},{9,11},{10,... | collective-permute-start | bytes 221192 | tf_op jit(solution)/shard_map/ppermute | solution.py:239
  14.0 23.8 %collective-permute-start.1 = (bf16[64,576]{1,0:T(8,128)(2,1)}, bf16[64,576]{1,0:T(8,128)(2,1)S(1)}, u32[]{:S(2)}, u32[]{:S(2)}) collective-permute-start(bf16[64,576]{1,0:T(8,128)(2,1)} %get-tuple-element.92), channel_id=1, source_target_pairs={{0,4},{1,5},{2,6},{3,7},{4,0},{5,1},{6,2},{7,3},{8,12},{9,13},{10,... | collective-permute-start | bytes 221192 | tf_op jit(solution)/shard_map/ppermute | solution.py:239
  16.3 21.5 %collective-permute-start.2 = (bf16[64,576]{1,0:T(8,128)(2,1)}, bf16[64,576]{1,0:T(8,128)(2,1)S(1)}, u32[]{:S(2)}, u32[]{:S(2)}) collective-permute-start(bf16[64,576]{1,0:T(8,128)(2,1)} %get-tuple-element.93), channel_id=1, source_target_pairs={{0,6},{1,7},{2,0},{3,1},{4,2},{5,3},{6,4},{7,5},{8,14},{9,15},{10,... | collective-permute-start | bytes 221192 | tf_op jit(solution)/shard_map/ppermute | solution.py:239
  60.7 20.5 %all-to-all-start.2 = ((bf16[4,48,768]{2,1,0:T(8,128)(2,1)}), bf16[4,48,768]{2,1,0:T(8,128)(2,1)S(1)}, u32[]{:S(2)}, u32[]{:S(2)}) async-start(bf16[4,48,768]{2,1,0:T(8,128)(2,1)} %reshape.129), calls=%async_computation.2 | async-start | bytes 589824 | tf_op jit(solution)/shard_map/all_to_all | solution.py:1225
  67.8 21.2 %collective-permute-start.11 = (bf16[4,48,768]{2,1,0:T(8,128)(2,1)S(1)}, bf16[4,48,768]{2,1,0:T(8,128)(2,1)S(1)}, u32[]{:S(2)}, u32[]{:S(2)}) collective-permute-start(bf16[4,48,768]{2,1,0:T(8,128)(2,1)S(1)} %all-to-all-done.1.a_ref), channel_id=1, source_target_pairs={{0,1},{1,0},{2,3},{3,2},{4,5},{5,4},{6,7},{7,6},{8,9},{9,8},{10,11... | collective-permute-start | bytes 884744 | tf_op jit(solution)/shard_map/ppermute | solution.py:274
  68.0 21.0 %collective-permute-start.19 = (bf16[4,48,768]{2,1,0:T(8,128)(2,1)S(1)}, bf16[4,48,768]{2,1,0:T(8,128)(2,1)S(1)}, u32[]{:S(2)}, u32[]{:S(2)}) collective-permute-start(bf16[4,48,768]{2,1,0:T(8,128)(2,1)S(1)} %all-to-all-done.3.a_ref), channel_id=1, source_target_pairs={{0,8},{8,0},{1,9},{9,1},{2,10},{10,2},{3,11},{11,3},{4,12},{12,4},... | collective-permute-start | bytes 884744 | tf_op jit(solution)/shard_map/ppermute | solution.py:242
  89.5 18.3 %collective-permute-start.17 = (bf16[4,48,768]{2,1,0:T(8,128)(2,1)S(1)}, bf16[4,48,768]{2,1,0:T(8,128)(2,1)}, u32[]{:S(2)}, u32[]{:S(2)}) collective-permute-start(bf16[4,48,768]{2,1,0:T(8,128)(2,1)S(1)} %all-to-all-done.2.a_ref), channel_id=1, source_target_pairs={{0,1},{1,0},{2,3},{3,2},{4,5},{5,4},{6,7},{7,6},{8,9},{9,8},{10,11... | collective-permute-start | bytes 884744 | tf_op jit(solution)/shard_map/ppermute | solution.py:274
  127.5 17.9 %collective-permute-start.26 = (bf16[128,768]{1,0:T(8,128)(2,1)}, bf16[128,768]{1,0:T(8,128)(2,1)S(1)}, u32[]{:S(2)}, u32[]{:S(2)}) collective-permute-start(bf16[128,768]{1,0:T(8,128)(2,1)} %get-tuple-element.111), channel_id=1, source_target_pairs={{0,4},{1,5},{2,6},{3,7},{4,0},{5,1},{6,2},{7,3},{8,12},{9,13},{10,... | collective-permute-start | bytes 589832 | tf_op jit(solution)/shard_map/ppermute | solution.py:239
  127.7 17.7 %collective-permute-start.27 = (bf16[128,768]{1,0:T(8,128)(2,1)}, bf16[128,768]{1,0:T(8,128)(2,1)S(1)}, u32[]{:S(2)}, u32[]{:S(2)}) collective-permute-start(bf16[128,768]{1,0:T(8,128)(2,1)} %get-tuple-element.112), channel_id=1, source_target_pairs={{0,2},{1,3},{2,4},{3,5},{4,6},{5,7},{6,0},{7,1},{8,10},{9,11},{10,... | collective-permute-start | bytes 589832 | tf_op jit(solution)/shard_map/ppermute | solution.py:239
  148.9 16.6 %collective-permute-start.29 = (bf16[128,768]{1,0:T(8,128)(2,1)}, bf16[128,768]{1,0:T(8,128)(2,1)S(1)}, u32[]{:S(2)}, u32[]{:S(2)}) collective-permute-start(bf16[128,768]{1,0:T(8,128)(2,1)} %get-tuple-element.115.refs_0_.a_ref), channel_id=1, source_target_pairs={{0,4},{1,5},{2,6},{3,7},{4,0},{5,1},{6,2},{7,3},{8,12},{9,13},{10,... | collective-permute-start | bytes 589832 | tf_op jit(solution)/shard_map/ppermute | solution.py:239
  184.6 27.0 %collective-permute-start.39 = (bf16[2,2,4,48,768]{4,3,2,0,1:T(8,128)(2,1)}, bf16[2,2,4,48,768]{4,3,2,0,1:T(8,128)(2,1)S(1)}, u32[]{:S(2)}, u32[]{:S(2)}) collective-permute-start(bf16[2,2,4,48,768]{4,3,2,0,1:T(8,128)(2,1)} %copy.55), channel_id=1, source_target_pairs={{0,1},{1,0},{2,3},{3,2},{4,5},{5,4},{6,7},{7,6},{8,9},{9,8},{10,11... | collective-permute-start | bytes 3538952 | tf_op jit(solution)/shard_map/ppermute | solution.py:274
  188.3 25.7 %collective-permute-start.37 = (bf16[2,192,768]{2,1,0:T(8,128)(2,1)}, bf16[2,192,768]{2,1,0:T(8,128)(2,1)}, u32[]{:S(2)}, u32[]{:S(2)}) collective-permute-start(bf16[2,192,768]{2,1,0:T(8,128)(2,1)} %get-tuple-element.138), channel_id=1, source_target_pairs={{0,1},{1,0},{2,3},{3,2},{4,5},{5,4},{6,7},{7,6},{8,9},{9,8},{10,11... | collective-permute-start | bytes 1769480 | tf_op jit(solution)/shard_map/ppermute | solution.py:274
  211.6 24.4 %collective-permute-start.41 = (bf16[2,4,64,768]{3,2,1,0:T(8,128)(2,1)}, bf16[2,4,64,768]{3,2,1,0:T(8,128)(2,1)}, u32[]{:S(2)}, u32[]{:S(2)}) collective-permute-start(bf16[2,4,64,768]{3,2,1,0:T(8,128)(2,1)} %get-tuple-element.149), channel_id=1, source_target_pairs={{0,1},{1,0},{2,3},{3,2},{4,5},{5,4},{6,7},{7,6},{8,9},{9,8},{10,11... | collective-permute-start | bytes 2359304 | tf_op jit(solution)/shard_map/ppermute | solution.py:274
  212.6 23.4 %collective-permute-start.40 = (bf16[2,4,48,768]{3,2,1,0:T(8,128)(2,1)}, bf16[2,4,48,768]{3,2,1,0:T(8,128)(2,1)}, u32[]{:S(2)}, u32[]{:S(2)}) collective-permute-start(bf16[2,4,48,768]{3,2,1,0:T(8,128)(2,1)} %fusion.10), channel_id=1, source_target_pairs={{0,8},{8,0},{1,9},{9,1},{2,10},{10,2},{3,11},{11,3},{4,12},{12,4},... | collective-permute-start | bytes 1769480 | tf_op jit(solution)/shard_map/ppermute | solution.py:242
  215.8 20.1 %collective-permute-start.38 = (bf16[192,768]{1,0:T(8,128)(2,1)}, bf16[192,768]{1,0:T(8,128)(2,1)}, u32[]{:S(2)}, u32[]{:S(2)}) collective-permute-start(bf16[192,768]{1,0:T(8,128)(2,1)} %fusion.16), channel_id=1, source_target_pairs={{0,8},{8,0},{1,9},{9,1},{2,10},{10,2},{3,11},{11,3},{4,12},{12,4},... | collective-permute-start | bytes 884744 | tf_op jit(solution)/shard_map/ppermute | solution.py:242
  246.3 28.4 %collective-permute-start.53 = (bf16[192,768]{1,0:T(8,128)(2,1)}, bf16[192,768]{1,0:T(8,128)(2,1)}, u32[]{:S(2)}, u32[]{:S(2)}) collective-permute-start(bf16[192,768]{1,0:T(8,128)(2,1)} %fusion.13), channel_id=1, source_target_pairs={{0,16},{16,0},{1,17},{17,1},{2,18},{18,2},{3,19},{19,3},{4,20},{20... | collective-permute-start | bytes 884744 | tf_op jit(solution)/shard_map/ppermute | solution.py:242
  248.7 16.2 %collective-permute-start.49 = (bf16[4,64,768]{2,1,0:T(8,128)(2,1)}, bf16[4,64,768]{2,1,0:T(8,128)(2,1)}, u32[]{:S(2)}, u32[]{:S(2)}) collective-permute-start(bf16[4,64,768]{2,1,0:T(8,128)(2,1)} %fusion.14), channel_id=1, source_target_pairs={{0,8},{8,0},{1,9},{9,1},{2,10},{10,2},{3,11},{11,3},{4,12},{12,4},... | collective-permute-start | bytes 1179656 | tf_op jit(solution)/shard_map/ppermute | solution.py:242
  251.0 17.0 %all-to-all-start.5 = ((bf16[4,48,768]{2,1,0:T(8,128)(2,1)}), bf16[4,48,768]{2,1,0:T(8,128)(2,1)S(1)}, u32[]{:S(2)}, u32[]{:S(2)}) async-start(bf16[4,48,768]{2,1,0:T(8,128)(2,1)} %fusion.12), calls=%async_computation.5 | async-start | bytes 589824 | tf_op jit(solution)/shard_map/all_to_all | solution.py:1225
  264.9 21.8 %collective-permute-start.44 = (bf16[128,768]{1,0:T(8,128)(2,1)}, bf16[128,768]{1,0:T(8,128)(2,1)}, u32[]{:S(2)}, u32[]{:S(2)}) collective-permute-start(bf16[128,768]{1,0:T(8,128)(2,1)} %get-tuple-element.154), channel_id=1, source_target_pairs={{0,4},{1,5},{2,6},{3,7},{4,0},{5,1},{6,2},{7,3},{8,12},{9,13},{10,... | collective-permute-start | bytes 589832 | tf_op jit(solution)/shard_map/ppermute | solution.py:239
  264.9 21.8 %collective-permute-start.45 = (bf16[128,768]{1,0:T(8,128)(2,1)}, bf16[128,768]{1,0:T(8,128)(2,1)}, u32[]{:S(2)}, u32[]{:S(2)}) collective-permute-start(bf16[128,768]{1,0:T(8,128)(2,1)} %get-tuple-element.155), channel_id=1, source_target_pairs={{0,2},{1,3},{2,4},{3,5},{4,6},{5,7},{6,0},{7,1},{8,10},{9,11},{10,... | collective-permute-start | bytes 589832 | tf_op jit(solution)/shard_map/ppermute | solution.py:239
  268.0 23.5 %all-to-all-start.6 = ((bf16[4,64,768]{2,1,0:T(8,128)(2,1)}), bf16[4,64,768]{2,1,0:T(8,128)(2,1)S(1)}, u32[]{:S(2)}, u32[]{:S(2)}) async-start(bf16[4,64,768]{2,1,0:T(8,128)(2,1)} %fusion.8), calls=%async_computation.6 | async-start | bytes 786432 | tf_op jit(solution)/shard_map/all_to_all | solution.py:1225
  272.0 16.7 %collective-permute-start.52 = (bf16[4,48,768]{2,1,0:T(8,128)(2,1)S(1)}, bf16[4,48,768]{2,1,0:T(8,128)(2,1)S(1)}, u32[]{:S(2)}, u32[]{:S(2)}) collective-permute-start(bf16[4,48,768]{2,1,0:T(8,128)(2,1)S(1)} %all-to-all-done.5.own_ref), channel_id=1, source_target_pairs={{0,16},{16,0},{1,17},{17,1},{2,18},{18,2},{3,19},{19,3},{4,20},{20... | collective-permute-start | bytes 884744 | tf_op jit(solution)/shard_map/ppermute | solution.py:242
  274.7 18.4 %collective-permute-start.48 = (bf16[4,64,576]{2,1,0:T(8,128)(2,1)S(1)}, bf16[4,64,576]{2,1,0:T(8,128)(2,1)S(1)}, u32[]{:S(2)}, u32[]{:S(2)}) collective-permute-start(bf16[4,64,576]{2,1,0:T(8,128)(2,1)S(1)} %fusion.9), channel_id=1, source_target_pairs={{0,16},{16,0},{1,17},{17,1},{2,18},{18,2},{3,19},{19,3},{4,20},{20... | collective-permute-start | bytes 884744 | tf_op jit(solution)/shard_map/ppermute | solution.py:242
  (96 other events, 888.5 us)

commit v3 on v2

--- a/solution.py
+++ b/solution.py
@@ -240,6 +240,11 @@
 
     def swap(self, value, axis):
         return lax.ppermute(value, axis, [(0, 1), (1, 0)])
+
+    def plane(self, value, k):
+        if k == 3:
+            return lax.ppermute(value, ("rep", "seq"), [(i, 3 - i) for i in range(4)])
+        return self.swap(value, "rep" if k == 1 else "seq")
 
     def gather(self, value):
         return [value] + [self.shift(value, k) for k in range(1, GROUPS)]
@@ -561,6 +566,27 @@
     return pl.BlockSpec(shape, lambda *_: tuple(0 for _ in shape))
 
 
+COSTS = {
+    "pack_joined": 0,
+    "assemble_joined": 0,
+    "pick_widen": 0,
+    "pack_widen": 0,
+    "split_joined": 3,
+    "attend": 5,
+    "attend_back": 8,
+    "close_attention": 3,
+    "widen_narrow": 6,
+    "widen_narrow_back": 7,
+    "turn_final": 3,
+    "turn_first": 3,
+    "wide_grads": 6,
+    "output_grads": 3,
+    "tokens_parts": 4,
+    "joined_grads": 4,
+    "finish_widen": 3,
+    "finish_joined": 2,
+}
+
 SMEM = pl.BlockSpec(memory_space=pltpu.SMEM)
 
 
@@ -579,7 +605,7 @@
         out_shape=shapes,
         scratch_shapes=list(scratch),
         name=name,
-        cost_estimate=pl.CostEstimate(flops=flops, transcendentals=0, bytes_accessed=moved),
+        cost_estimate=pl.CostEstimate(flops=int(COSTS[name] * 5 * 1e9), transcendentals=0, bytes_accessed=0),
     )(*inputs)
 
 
@@ -633,7 +659,7 @@
 
     def body(ids_ref, a_ref, b_ref, c_ref, d_ref, w_ref, vec_ref, near_ref, wide_ref):
         place_rows(ids_ref, (a_ref, b_ref, c_ref, d_ref), w_ref, kb, True)
-        g, m, y = ids_ref[0], ids_ref[1], ids_ref[2]
+        g, m, y, x = ids_ref[0], ids_ref[1], ids_ref[2], ids_ref[3]
         blocks = []
         for row in range(2):
             for k in range(GROUPS):
@@ -650,12 +676,16 @@
             total = jnp.where(g == k, vec[:, k * near : (k + 1) * near], total)
         near_ref[...] = total
         lines = []
-        for chunk in range(4):
-            block = jnp.zeros((8, kb), F32)
-            for k in range(GROUPS):
-                at = (chunk * GROUPS + k) * kb
-                block = jnp.where(g == k, vec[8:16, at : at + kb], block)
-            lines += [block[i : i + 1] for i in range(8)]
+        for part in range(2):
+            for c in range(8):
+                low = 8 + (c % 2) * 4
+                picks = []
+                for row in range(2):
+                    at = (part * 8 + row * 4 + c // 2) * kb
+                    picks.append(vec[low : low + 4, at : at + kb])
+                both = jnp.where(y == 0, picks[0], picks[1])
+                pair = jnp.where(x == 0, both[0:2], both[2:4])
+                lines += [pair[0:1], pair[1:2]]
         wide_ref[...] = jnp.concatenate(lines, axis=1)
 
     return call(
@@ -666,28 +696,62 @@
     )
 
 
-def assemble_rows(ids, pieces, name):
-    kb = pieces[0].shape[1]
-    cols = pieces[0].shape[2]
-
-    def body(ids_ref, a_ref, b_ref, c_ref, d_ref, w_ref):
-        place_rows(ids_ref, (a_ref, b_ref, c_ref, d_ref), w_ref, kb)
-
-    return call(body, name, [ids] + list(pieces), [((4 * GROUPS * kb, cols), BF)])[0]
-
-
-def assemble_narrow(ids, pieces):
-    rows, cols = pieces[0].shape
-
-    def body(ids_ref, a_ref, b_ref, c_ref, d_ref, w_ref):
-        m, y = ids_ref[1], ids_ref[2]
-        for index, ref in enumerate((a_ref, b_ref, c_ref, d_ref)):
-            row = y if index % 2 == 0 else 1 - y
-            member = m if index < 2 else 1 - m
-            start = pl.multiple_of((row * 2 + member) * rows, 16)
-            w_ref[pl.ds(start, rows), :] = ref[...]
-
-    return call(body, "assemble_narrow", [ids] + list(pieces), [((4 * rows, cols), BF)])[0]
+def pick_widen(ids, weight, narrow):
+    kb, total = weight.shape
+    own, width = narrow.shape
+    half = own // 2
+    side = total // 4
+    count = side // own
+    quarter = count * half
+
+    wide = 2 * quarter
+
+    def body(ids_ref, w_ref, n_ref, near_ref, far_ref, low_ref, all_ref):
+        y, x = ids_ref[2], ids_ref[3]
+        for row in range(2):
+            for col in range(2):
+                pieces = []
+                for part in range(2):
+                    for c in range(count):
+                        at = part * 2 * side + row * side + c * own + col * half
+                        pieces.append(w_ref[:, at : at + half])
+                all_ref[row * 2 + col] = jnp.concatenate(pieces, axis=1)
+        near_ref[...] = all_ref[y * 2 + x]
+        far_ref[...] = all_ref[(1 - y) * 2 + x]
+        low_ref[...] = n_ref[pl.ds(pl.multiple_of(x * half, 16), half), :]
+
+    return call(
+        body,
+        "pick_widen",
+        [ids, weight, narrow],
+        [((kb, wide), BF), ((kb, wide), BF), ((half, width), BF)],
+        scratch=[pltpu.VMEM((4, kb, wide), BF)],
+    )
+
+
+def pack_widen(ids, near, got, low):
+    kb, cols = near.shape
+    width = low.shape[1]
+
+    def body(ids_ref, near_ref, got_ref, low_ref, out_ref):
+        y = ids_ref[2]
+        out_ref[pl.ds(pl.multiple_of(y * kb, 16), kb), :cols] = near_ref[...]
+        out_ref[pl.ds(pl.multiple_of((1 - y) * kb, 16), kb), :cols] = got_ref[...]
+        out_ref[:, cols:] = low_ref[...]
+
+    return call(body, "pack_widen", [ids, near, got, low], [((2 * kb, cols + width), BF)])[0]
+
+
+def owner_order(value, kb):
+    half = value.shape[1] // (2 * kb)
+    blocks = [y * half + c for c in range(half) for y in range(2)]
+    return jnp.concatenate([value[:, b * kb : (b + 1) * kb] for b in blocks], axis=1)
+
+
+def column_order(value, kb):
+    half = value.shape[1] // (2 * kb)
+    blocks = [c * 2 + y for y in range(2) for c in range(half)]
+    return jnp.concatenate([value[:, b * kb : (b + 1) * kb] for b in blocks], axis=1)
 
 
 def split_joined(x_four, weight, near, scale):
@@ -818,7 +882,7 @@
     )
 
 
-def close_attention(ids, inputs, mixed_rel, weight, vec):
+def close_attention(ids, inputs, mixed_rel, weight, vec, kb):
     rows, width = inputs.shape
     cols = mixed_rel[0].shape[1]
 
@@ -829,7 +893,7 @@
         unit, root = norm_stats(total)
         first = unit * vec_ref[3:4, :] + vec_ref[4:5, :]
         first_ref[...] = first
-        low_ref[...] = first.astype(BF)
+        low_ref[...] = owner_order(first, kb).astype(BF)
         unit_ref[...] = unit
         root_ref[...] = root
 
@@ -855,27 +919,27 @@
         ref[...] = total[k * rows : (k + 1) * rows, :].astype(ref.dtype)
 
 
-def widen_narrow(rel, w_gate, w_up, w_narrow, wide):
+def widen_narrow(rel, weights, wide):
     rows, width = rel[0].shape
-    quarter = w_narrow.shape[0]
+    quarter = wide.shape[1] // 2
     count = GROUPS * rows
 
     def body(*refs):
-        wg_ref, wu_ref, wn_ref, wide_ref = refs[4:8]
-        hid_ref, gate_ref, up_ref = refs[12:15]
+        w_ref, wide_ref = refs[4:6]
+        hid_ref, gate_ref, up_ref = refs[10:13]
         value = join_pieces(refs[:4])
-        gate = dot_nn(value, wg_ref[...]) + wide_ref[:, :quarter]
-        up = dot_nn(value, wu_ref[...]) + wide_ref[:, quarter:]
+        gate = dot_nn(value, w_ref[:, :quarter]) + wide_ref[:, :quarter]
+        up = dot_nn(value, w_ref[:, quarter : 2 * quarter]) + wide_ref[:, quarter:]
         gate_ref[...] = gate
         up_ref[...] = up
         hidden = (gate * (0.5 + 0.5 * lax.erf(gate * math.sqrt(0.5))) * up).astype(BF)
         hid_ref[...] = hidden
-        send_pieces(dot_nn(hidden, wn_ref[...]), refs[8:12], rows)
+        send_pieces(dot_nn(hidden, w_ref[:, 2 * quarter :]), refs[6:10], rows)
 
     return call(
         body,
         "widen_narrow",
-        list(rel) + [w_gate, w_up, w_narrow, wide],
+        list(rel) + [weights, wide],
         [((rows, width), F32)]
         + [((rows, width), BF)] * 3
         + [((count, quarter), BF), ((count, quarter), F32), ((count, quarter), F32)],
@@ -889,26 +953,25 @@
     return up * slope, gate * phi_big
 
 
-def widen_narrow_back(rel, w_gate, w_up, w_narrow, gate_factor, up_factor):
+def widen_narrow_back(rel, weights, gate_factor, up_factor):
     rows, width = rel[0].shape
-    quarter = w_narrow.shape[0]
-    count = GROUPS * rows
+    count, quarter = gate_factor.shape
 
     def body(*refs):
-        wg_ref, wu_ref, wn_ref, gf_ref, uf_ref = refs[4:9]
-        bg_ref, bu_ref = refs[13:15]
-        hidden_back = dot_nt(join_pieces(refs[:4]), wn_ref[...])
+        w_ref, gf_ref, uf_ref = refs[4:7]
+        bg_ref, bu_ref = refs[11:13]
+        hidden_back = dot_nt(join_pieces(refs[:4]), w_ref[:, 2 * quarter :])
         gate_back = (hidden_back * gf_ref[...]).astype(BF)
         up_back = (hidden_back * uf_ref[...]).astype(BF)
         bg_ref[...] = gate_back
         bu_ref[...] = up_back
-        total = dot_nt(gate_back, wg_ref[...]) + dot_nt(up_back, wu_ref[...])
-        send_pieces(total, refs[9:13], rows)
+        total = dot_nt(gate_back, w_ref[:, :quarter]) + dot_nt(up_back, w_ref[:, quarter : 2 * quarter])
+        send_pieces(total, refs[7:11], rows)
 
     return call(
         body,
         "widen_narrow_back",
-        list(rel) + [w_gate, w_up, w_narrow, gate_factor, up_factor],
+        list(rel) + [weights, gate_factor, up_factor],
         [((rows, width), F32)] + [((rows, width), BF)] * 3 + [((count, quarter), BF)] * 2,
         flops=6 * count * width * quarter,
     )
@@ -942,15 +1005,16 @@
     )
 
 
-def turn_first(ids, own, received, final_back, unit, root, weight, vec):
+def turn_first(ids, own, received, final_back, unit, root, weight, vec, kb):
     rows, width = own.shape
     cols = width // GROUPS
 
     def body(ids_ref, own_ref, a_ref, b_ref, c_ref, fb_ref, unit_ref, root_ref, w_ref, vec_ref, *outs):
         attn_ref, low_ref, sum_ref = outs[:3]
-        total = fb_ref[...] + own_ref[...]
+        total = own_ref[...]
         for ref in (a_ref, b_ref, c_ref):
             total = total + ref[...].astype(F32)
+        total = fb_ref[...] + column_order(total, kb)
         unit = unit_ref[...]
         back = norm_back(unit, root_ref[...], vec_ref[3:4, :], total)
         low = back.astype(BF)
@@ -984,62 +1048,26 @@
             give_ref[lead + (turn, g, slice(0, kb), slice(None))] = full_ref[other, :].astype(BF)
 
 
-def widen_grads(ids, rel, gate_back, up_back, kb):
-    rows, width = rel[0].shape
+def wide_grads(first_rel, gate_back, up_back, hidden, back_rel):
+    rows, width = first_rel[0].shape
     count, quarter = gate_back.shape
-    block = block_of(quarter)
-    steps = quarter // block
-
-    def body(ids_ref, a_ref, b_ref, c_ref, d_ref, gate_ref, up_ref, keep_ref, give_ref, gs_ref, us_ref, full_ref):
-        value = jnp.concatenate([a_ref[...], b_ref[...], c_ref[...], d_ref[...]], axis=0)
-        x = ids_ref[3]
+
+    def body(*refs):
+        gate_ref, up_ref, hid_ref = refs[8:11]
+        out_ref, gs_ref, us_ref = refs[11:14]
+        value = join_pieces(refs[:4])
         for turn, (ref, sum_ref) in enumerate(((gate_ref, gs_ref), (up_ref, us_ref))):
             back = ref[...]
-            full_ref[...] = dot_tn(value, back)
+            out_ref[:, turn * quarter : (turn + 1) * quarter] = dot_tn(value, back).astype(BF)
             sum_ref[...] = jnp.sum(back.astype(F32), axis=0, keepdims=True)
-            split_rows(ids_ref, full_ref, keep_ref, give_ref, kb, ((x + turn) % 2,))
-
-    piece = vmem((rows, width))
-    tall = pl.BlockSpec((count, block), lambda i: (0, i))
-    line = pl.BlockSpec((1, block), lambda i: (0, i))
-    cut = pl.BlockSpec((2, 2, GROUPS, kb, block), lambda i: (0, 0, 0, 0, i))
-    shape = (2, 2, GROUPS, kb, quarter)
-    return call(
-        body,
-        "widen_grads",
-        [ids] + list(rel) + [gate_back, up_back],
-        [(shape, F32), (shape, BF), ((1, quarter), F32), ((1, quarter), F32)],
-        scratch=[pltpu.VMEM((width, block), F32)],
-        grid=(steps,),
-        in_specs=[SMEM] + [piece] * 4 + [tall] * 2,
-        out_specs=[cut, cut, line, line],
-        flops=4 * count * width * quarter,
-    )
-
-
-def narrow_grads(ids, hidden, rel):
-    rows, width = rel[0].shape
-    count, quarter = hidden.shape
-    own = quarter // 4
-
-    def body(ids_ref, h_ref, a_ref, b_ref, c_ref, d_ref, keep_ref, give_ref, full_ref):
-        value = jnp.concatenate([a_ref[...], b_ref[...], c_ref[...], d_ref[...]], axis=0)
-        full_ref[...] = dot_tn(h_ref[...], value)
-        m, y = ids_ref[1], ids_ref[2]
-        for turn in range(2):
-            base = (y if turn == 0 else 1 - y) * 2
-            mine = pl.ds(pl.multiple_of((base + m) * own, 16), own)
-            other = pl.ds(pl.multiple_of((base + 1 - m) * own, 16), own)
-            keep_ref[turn] = full_ref[mine, :]
-            give_ref[turn] = full_ref[other, :].astype(BF)
-
-    return call(
-        body,
-        "narrow_grads",
-        [ids, hidden] + list(rel),
-        [((2, own, width), F32), ((2, own, width), BF)],
-        scratch=[pltpu.VMEM((quarter, width), F32)],
-        flops=2 * count * width * quarter,
+        out_ref[:, 2 * quarter :] = dot_tn(hid_ref[...], join_pieces(refs[4:8])).astype(BF)
+
+    return call(
+        body,
+        "wide_grads",
+        list(first_rel) + list(back_rel) + [gate_back, up_back, hidden],
+        [((width, 2 * quarter + width), BF), ((1, quarter), F32), ((1, quarter), F32)],
+        flops=6 * count * width * quarter,
     )
 
 
@@ -1070,10 +1098,9 @@
         for k, ref in enumerate(refs[:GROUPS]):
             full_ref[piece_rows(ids_ref, k, cols, -1), :] = dot_tn(ref[...], back_ref[...])
         split_rows(ids_ref, full_ref, keep_ref, give_ref, kb)
-        g_own = ids_ref[0]
+        y, x = ids_ref[2], ids_ref[3]
         sums = jnp.concatenate([fs_ref[0:3, :], ls_ref[0:3, :]], axis=0)
         wide = (gs_ref[...], us_ref[...])
-        span = 8 * kb
         blocks = []
         for row in range(2):
             blocks.append([])
@@ -1081,9 +1108,11 @@
                 blocks[-1].append([])
                 for member in range(2):
                     b = row * 8 + g * 2 + member
-                    part = wide[b // 8][:, ((b // 4) % 2) * span : ((b // 4) % 2 + 1) * span]
-                    part = jnp.where(g_own == b % GROUPS, part, 0.0)
-                    lines = [part[:, i * kb : (i + 1) * kb] for i in range(8)]
+                    lines = []
+                    for i in range(8):
+                        at = ((b % 4) * 4 + (i // 4) * 2 + i % 2) * kb
+                        mine = (y == (b % 8) // 4) & (x == (i % 4) // 2)
+                        lines.append(jnp.where(mine, wide[b // 8][:, at : at + kb], 0.0))
                     lines = [sums[:, b * kb : (b + 1) * kb]] + lines + [jnp.zeros((2, kb), F32)]
                     blocks[-1][-1].append(jnp.concatenate(lines, axis=0))
         place_small(ids_ref, blocks, keep_ref, give_ref, kb)
@@ -1153,20 +1182,38 @@
     )
 
 
-def finish_widen(ids, own, other):
-    kb, cols = own.shape[1:]
-    span = cols // 2
-
-    def body(ids_ref, own_ref, other_ref, out_ref):
-        x = ids_ref[3]
+def finish_widen(ids, pieces, low, low_got):
+    kb, cols = pieces[0].shape
+    half, width = low.shape
+    quarter = cols // 2
+    count = quarter // half
+
+    def body(ids_ref, *refs):
+        low_ref, got_ref, out_ref, narrow_ref, all_ref = refs[4:]
+        y, x = ids_ref[2], ids_ref[3]
+        for k in range(4):
+            row = y if k < 2 else 1 - y
+            col = x if k % 2 == 0 else 1 - x
+            all_ref[row * 2 + col] = refs[k][...].astype(F32)
         for part in range(2):
-            for g in range(GROUPS):
-                picked = jnp.where(x == part, own_ref[g].astype(F32), other_ref[g].astype(F32))
-                for row in range(2):
-                    at = ((part * 2 + row) * GROUPS + g) * span
-                    out_ref[:, at : at + span] = picked[:, row * span : (row + 1) * span]
-
-    return call(body, "finish_widen", [ids, own, other], [((kb, 4 * GROUPS * span), F32)])[0]
+            for row in range(2):
+                picks = []
+                for c in range(count):
+                    for col in range(2):
+                        at = part * quarter + c * half
+                        picks.append(all_ref[row * 2 + col, :, at : at + half])
+                at = (part * 2 + row) * 2 * quarter
+                out_ref[:, at : at + 2 * quarter] = jnp.concatenate(picks, axis=1)
+        narrow_ref[pl.ds(pl.multiple_of(x * half, 16), half), :] = low_ref[...].astype(F32)
+        narrow_ref[pl.ds(pl.multiple_of((1 - x) * half, 16), half), :] = got_ref[...].astype(F32)
+
+    return call(
+        body,
+        "finish_widen",
+        [ids] + list(pieces) + [low, low_got],
+        [((kb, 8 * quarter), F32), ((2 * half, width), F32)],
+        scratch=[pltpu.VMEM((4, kb, cols), F32)],
+    )
 
 
 def finish_joined(got, kb):
@@ -1228,7 +1275,7 @@
         far = at.swap(value, "seq")
         return (value, far, at.partner(value), at.partner(far))
 
-    x_four = across(jnp.broadcast_to(inputs[None], (GROUPS, rows, width))).reshape(-1, width)
+    w_output = lax.all_gather(output_weight, ("seq", "ctx"), tiled=True)
     packed = pack_joined(
         ids,
         joined_weight,
@@ -1245,19 +1292,15 @@
         widen_bias,
         cols,
     )
-    joined_got = jnp.stack([packed[0]] + [at.shift(packed[k], k) for k in range(1, GROUPS)])
+    joined_rel = [packed[0]] + [at.shift(packed[k], k) for k in range(1, GROUPS)]
+    x_cut = jnp.broadcast_to(after(inputs, *joined_rel)[None], (GROUPS, rows, width))
+    x_four = across(x_cut).reshape(-1, width)
+    joined_got = jnp.stack(joined_rel)
     joined_parts = spread_out(joined_got)
     w_joined, vec, near, wide = assemble_joined(ids, joined_parts, kb)
-    narrow_parts = spread_out(after(narrow_weight, joined_parts[1]))
-    output_cut = jnp.broadcast_to(after(output_weight, x_four)[None], (GROUPS, kb, width))
-    output_got = across(output_cut)
-    widen_cut = widen_weight.reshape(kb, 2, 2, GROUPS, span)
-    widen_got = [
-        across(
-            after(jnp.transpose(widen_cut[:, t], (2, 0, 1, 3)).reshape(GROUPS, kb, quarter), output_got)
-        )
-        for t in range(2)
-    ]
+    widen_near, widen_far, narrow_low = pick_widen(after(ids, packed[3]), widen_weight, narrow_weight)
+    widen_got = at.swap(after(widen_far, joined_parts[1]), "seq")
+    w_wide = lax.all_gather(pack_widen(ids, widen_near, widen_got, narrow_low), "ctx", tiled=True)
 
     queries, kv_own = split_joined(x_four, w_joined, near, scale)
     kv_other = at.partner(kv_own)
@@ -1282,32 +1325,27 @@
     mixed_near, inv = attended[:2]
     mixed_send = attended[2:]
     mixed_rel = [mixed_send[0]] + [at.shift(mixed_send[k], k) for k in range(1, GROUPS)]
-    w_output = assemble_rows(ids, spread_out(output_got), "assemble_output")
-    w_narrow = assemble_narrow(ids, narrow_parts)
-    w_gate = assemble_rows(ids, spread_out(widen_got[0]), "assemble_gate")
-    w_up = assemble_rows(ids, spread_out(widen_got[1]), "assemble_up")
-
-    first, first_low, first_unit, first_root = close_attention(ids, inputs, mixed_rel, w_output, vec)
-    first_rel = at.gather(first_low)
-    own, s1, s2, s3, hidden, gate, up = widen_narrow(first_rel, w_gate, w_up, w_narrow, wide)
-    received = [at.shift(s1, -1), at.shift(s2, -2), at.shift(s3, -3)]
+    first, first_low, first_unit, first_root = close_attention(
+        ids, inputs, mixed_rel, w_output, vec, kb
+    )
+    first_rel = [first_low] + [at.plane(first_low, k) for k in (1, 2, 3)]
+    own, s1, s2, s3, hidden, gate, up = widen_narrow(first_rel, w_wide, wide)
+    received = [at.plane(s1, 1), at.plane(s2, 2), at.plane(s3, 3)]
     gate_factor, up_factor = gate_slopes(gate, up)
     result, final_back, narrow_back, final_sums = turn_final(own, received, first, cotangent[0], vec)
 
-    back_rel = at.gather(narrow_back)
-    own, s1, s2, s3, gate_back, up_back = widen_narrow_back(
-        back_rel, w_gate, w_up, w_narrow, gate_factor, up_factor
-    )
-    received = [at.shift(s1, -1), at.shift(s2, -2), at.shift(s3, -3)]
-    narrow_keep, narrow_give = narrow_grads(ids, hidden, back_rel)
-    widen_keep, widen_give, gate_sum, up_sum = widen_grads(ids, first_rel, gate_back, up_back, kb)
-    turned = turn_first(ids, own, received, final_back, first_unit, first_root, w_output, vec)
+    back_rel = [narrow_back] + [at.plane(narrow_back, k) for k in (1, 2, 3)]
+    own, s1, s2, s3, gate_back, up_back = widen_narrow_back(back_rel, w_wide, gate_factor, up_factor)
+    received = [at.plane(s1, 1), at.plane(s2, 2), at.plane(s3, 3)]
+    wide_grad, gate_sum, up_sum = wide_grads(
+        first_rel, gate_back, up_back, hidden, back_rel
+    )
+    wide_sum = lax.psum_scatter(wide_grad, "ctx", tiled=True)
+    turned = turn_first(ids, own, received, final_back, first_unit, first_root, w_output, vec, kb)
     attn_back, output_back, first_sums = turned[:3]
     back_send = turned[3:]
     back_near = [back_send[0]] + [at.shift(back_send[k], k) for k in range(1, GROUPS)]
 
-    narrow_got = at.partner(after(narrow_give, received[2]))
-    widen_got = at.partner(after(widen_give, received[2]))
     output_keep, output_give = output_grads(
         ids, mixed_rel, output_back, first_sums, final_sums, gate_sum, up_sum, kb
     )
@@ -1315,39 +1353,36 @@
     def seq_send(keep, got):
         return (keep + got.astype(F32)).astype(BF)
 
-    narrow_far = at.swap(seq_send(narrow_keep[1], narrow_got[1]), "seq")
-    widen_far = at.swap(seq_send(widen_keep[:, 1], widen_got[:, 1]), "seq")
     output_got = at.partner(output_give)
 
     query_back, kv_keep, kv_give = attend_back(
         ids, slopes, queries, back_near, mixed_near, inv, kv_own, kv_other, q_row, k_col, scale
     )
-    kv_give, narrow_far, widen_far, output_got = lax.optimization_barrier(
-        (kv_give, narrow_far, widen_far, output_got)
-    )
+    output_far = at.swap(seq_send(output_keep[1], output_got[1]), "seq")
+    kv_give, output_far = lax.optimization_barrier((kv_give, output_far))
     kv_got = at.partner(kv_give)
 
-    narrow_sum = (narrow_keep[0] + narrow_got[0].astype(F32) + narrow_far.astype(F32)).astype(BF)
-    narrow_total = narrow_sum.astype(F32) + at.swap(narrow_sum, "rep").astype(F32)
-    widen_sum = widen_keep[:, 0] + widen_got[:, 0].astype(F32) + widen_far.astype(F32)
-    widen_mine = widen_sum[0] + at.swap(widen_sum[1].astype(BF), "rep").astype(F32)
-    output_far = at.swap(seq_send(output_keep[1], output_got[1]), "seq")
     output_sum = (output_keep[0] + output_got[0].astype(F32) + output_far.astype(F32)).astype(BF)
-
+    output_both = (output_sum.astype(F32) + at.swap(output_sum, "rep").astype(F32)).astype(BF)
     joined_keep, joined_give, joined_back = joined_grads(ids, x_four, query_back, kv_keep, kv_got, kb)
     joined_got = at.partner(joined_give)
     own, s1, s2, s3 = tokens_parts(ids, joined_back, w_joined)
     received = [at.shift(s1, -1), at.shift(s2, -2), at.shift(s3, -3)]
     joined_far = at.swap(seq_send(joined_keep[1], joined_got[1]), "seq")
     joined_sum = (joined_keep[0] + joined_got[0].astype(F32) + joined_far.astype(F32)).astype(BF)
-    joined_mine = (joined_sum.astype(F32) + at.swap(joined_sum, "rep").astype(F32)).astype(BF)
-    widen_own = across(widen_mine.astype(BF))
-    widen_total = finish_widen(ids, widen_own, at.swap(widen_own, "rep"))
-    output_all = across(after(output_sum, widen_own))
-    output_mine = jnp.sum(output_all.astype(F32), axis=0).astype(BF)
-    output_total = output_mine.astype(F32) + at.swap(output_mine, "rep").astype(F32)
+    wide_sum = after(wide_sum, joined_got)
+    low_sum = wide_sum[:, 2 * quarter :]
+    row_own = lax.dynamic_slice_in_dim(wide_sum, at.seq * kb, kb, 0)[:, : 2 * quarter]
+    row_far = lax.dynamic_slice_in_dim(wide_sum, (1 - at.seq) * kb, kb, 0)[:, : 2 * quarter]
+    joined_both = (joined_sum.astype(F32) + at.swap(joined_sum, "rep").astype(F32)).astype(BF)
+    widen_pieces = [row_own, at.plane(row_own, 1), at.plane(row_far, 2), at.plane(row_far, 3)]
+    low_got = at.plane(low_sum, 1)
+    joined_mine = after(joined_both, low_got, *widen_pieces)
+    widen_total, narrow_total = finish_widen(ids, widen_pieces, low_sum, low_got)
+    output_all = across(after(output_both, joined_far))
+    output_total = jnp.sum(after(output_all, joined_mine).astype(F32), axis=0)
     joined_total, pair = finish_joined(across(joined_mine), kb)
-    tokens_grad = attn_back + own
+    tokens_grad = after(attn_back, joined_mine) + own
     for item in received:
         tokens_grad = tokens_grad + item.astype(F32)
     last = output_total[kb:, :kb]

time: 312 us -> 259 us (0.83)
  starting transfers between devices: 93.1 us -> 62.1 us
  other arithmetic: 23.5 us -> 9.38 us
  between operations: 1.22 us -> 14.1 us
  waiting for transfers between devices: 95.4 us -> 83.5 us
  Pallas kernels: 75.3 us -> 68.1 us
    ppermute x24 -> x12, waiting for transfers between devices: 62.7 us -> 22.4 us  [shift(): lax.ppermute(value, 'ctx', [(i, (i + steps * r) % n) for i in range(n)])]
    ppermute x14 -> x17, waiting for transfers between devices: 9.81 us -> 44.1 us  [swap(): return lax.ppermute(value, axis, [(0, 1), (1, 0)])]
    ppermute x24 -> x12, starting transfers between devices: 44.7 us -> 21.1 us  [shift(): lax.ppermute(value, 'ctx', [(i, (i + steps * r) % n) for i in range(n)])]
    all_to_all x7 -> x3, waiting for transfers between devices: 22.9 us -> 3.17 us  [across(): lax.all_to_all(value, 'ctx', 0, 0, axis_index_groups=columns, tiled=True)]
    all_to_all x7 -> x3, starting transfers between devices: 28.9 us -> 14.2 us  [across(): lax.all_to_all(value, 'ctx', 0, 0, axis_index_groups=columns, tiled=True)]
    all_gather x0 -> x2, waiting for transfers between devices: none -> 9.73 us  [the longest x1 9.71 us: fast_device(): lax.all_gather(pack_widen(ids, widen_near, widen_got, narrow_low), 'ctx',...]
    pallas_call x21 -> x18, Pallas kernels: 75.3 us -> 68.1 us  [call(): pl.pallas_call(body, grid=grid, in_specs=in_specs, out_specs=out_specs, o...]
    ppermute x0 -> x5, starting transfers between devices: none -> 5.94 us  [plane(): return lax.ppermute(value, ('rep', 'seq'), [(i, 3 - i) for i in range(4)])]
  transfers between devices with their start and end apart: 61 -> 46, of which waited for: 20 -> 25; matrix products, arithmetic and copies ran while one was open for 10% -> 7% of each run, Pallas kernels for 19% -> 17%
where the time goes in v3:
time: 259 us; the launch traced here: 258 us
  waiting for transfers between devices  83.5 us (32%)
  Pallas kernels  68.1 us (26%)
  starting transfers between devices  62.1 us (24%)
  local copies, waits for them, and re-layouts  20.6 us (8%)
  between operations  14.1 us (5%)
  other arithmetic  9.38 us (4%)
    pallas_call x18, Pallas kernels, call(): pl.pallas_call(body, grid=grid, in_specs=in_specs, out_specs=out_specs, o...  68.1 us
    ppermute x17, waiting for transfers between devices, swap(): return lax.ppermute(value, axis, [(0, 1), (1, 0)])  44.1 us
    ppermute x12, waiting for transfers between devices, shift(): lax.ppermute(value, 'ctx', [(i, (i + steps * r) % n) for i in range(n)])  22.4 us
    ppermute x12, starting transfers between devices, shift(): lax.ppermute(value, 'ctx', [(i, (i + steps * r) % n) for i in range(n)])  21.1 us
    ppermute x17, starting transfers between devices, swap(): return lax.ppermute(value, axis, [(0, 1), (1, 0)])  20 us
    all_to_all x3, starting transfers between devices, across(): lax.all_to_all(value, 'ctx', 0, 0, axis_index_groups=columns, tiled=True)  14.2 us
    unnamed x103, local copies, waits for them, and re-layouts  10.4 us
    all_gather x1, waiting for transfers between devices, fast_device(): lax.all_gather(pack_widen(ids, widen_near, widen_got, narrow_low), 'ctx',...  9.71 us
  transfers between devices with their start and end apart: 46, of which 25 were waited for; matrix products, arithmetic and copies ran while one was open for 7% of the time, Pallas kernels for 17%

profile of v3, /device:TPU:0, one launch (start us, length us, event | category | flops | bytes accessed | tf_op | source)
XLA Modules:
  0.0 257.7 jit_solution(1516377003590706739)
XLA Ops:
  25.1 5.3 %all-to-all-start = ((bf16[4,128,768]{2,1,0:T(8,128)(2,1)}), bf16[4,128,768]{2,1,0:T(8,128)(2,1)S(1)}, u32[]{:S(2)}, u32[]{:S(2)}) async-start(bf16[4,128,768]{2,1,0:T(8,128)(2,1)} %broadcast_in_dim.52), calls=%async_computation | async-start | bytes 1572864 | tf_op jit(solution)/shard_map/all_to_all | solution.py:1272
  34.4 3.9 %collective-permute-done.3.b_ref = bf16[4,64,576]{2,1,0:T(8,128)(2,1)S(1)} collective-permute-done((bf16[4,64,576]{2,1,0:T(8,128)(2,1)S(1)}, bf16[4,64,576]{2,1,0:T(8,128)(2,1)S(1)}, u32[]{:S(2)}, u32[]{:S(2)}) %collective-permute-start.3) | collective-permute-done | bytes 294944 | tf_op jit(solution)/shard_map/ppermute | solution.py:242
  39.9 4.6 %collective-permute-done.13.got_ref = bf16[48,1536]{1,0:T(8,128)(2,1)S(1)} collective-permute-done((bf16[48,1536]{1,0:T(8,128)(2,1)}, bf16[48,1536]{1,0:T(8,128)(2,1)S(1)}, u32[]{:S(2)}, u32[]{:S(2)}) %collective-permute-start.13) | collective-permute-done | bytes 147488 | tf_op jit(solution)/shard_map/ppermute | solution.py:242
  60.4 4.7 %attend.1 = (f32[512,192]{1,0:T(8,128)}, f32[3,8,512]{2,1,0:T(8,128)}, bf16[128,192]{1,0:T(8,128)(2,1)}, bf16[128,192]{1,0:T(8,128)(2,1)}, bf16[128,192]{1,0:T(8,128)(2,1)}, /*index=5*/bf16[128,192]{1,0:T(8,128)(2,1)}) custom-call(s32[4]{0:T(128)} %pad_add_fusion.refs_0_.ids_ref, f32[3]{0:T(128)} %power_multiply_fusion.slope_ref, ...), custom_call_target="tpu_custom_call" | custom-call | flops 24999999488 | tf_op jit(solution)/shard_map/attend/pallas_call | solution.py:600
  70.0 3.5 %collective-permute-done.7.b_ref.refs_1_ = bf16[128,192]{1,0:T(8,128)(2,1)S(1)} collective-permute-done((bf16[128,192]{1,0:T(8,128)(2,1)}, bf16[128,192]{1,0:T(8,128)(2,1)S(1)}, u32[]{:S(2)}, u32[]{:S(2)}) %collective-permute-start.7) | collective-permute-done | bytes 49184 | tf_op jit(solution)/shard_map/ppermute | solution.py:239
  73.5 5.0 %collective-permute-done.8.c_ref.refs_2_ = bf16[128,192]{1,0:T(8,128)(2,1)S(1)} collective-permute-done((bf16[128,192]{1,0:T(8,128)(2,1)}, bf16[128,192]{1,0:T(8,128)(2,1)S(1)}, u32[]{:S(2)}, u32[]{:S(2)}) %collective-permute-start.8) | collective-permute-done | bytes 49184 | tf_op jit(solution)/shard_map/ppermute | solution.py:239
  85.5 4.5 %collective-permute-done.10.refs_1_ = bf16[128,768]{1,0:T(8,128)(2,1)S(1)} collective-permute-done((bf16[128,768]{1,0:T(8,128)(2,1)}, bf16[128,768]{1,0:T(8,128)(2,1)S(1)}, u32[]{:S(2)}, u32[]{:S(2)}) %collective-permute-start.10) | collective-permute-done | bytes 196640 | tf_op jit(solution)/shard_map/ppermute | solution.py:242
  90.0 3.7 %collective-permute-done.11.refs_2_ = bf16[128,768]{1,0:T(8,128)(2,1)S(1)} collective-permute-done((bf16[128,768]{1,0:T(8,128)(2,1)}, bf16[128,768]{1,0:T(8,128)(2,1)S(1)}, u32[]{:S(2)}, u32[]{:S(2)}) %collective-permute-start.11) | collective-permute-done | bytes 196640 | tf_op jit(solution)/shard_map/ppermute | solution.py:242
  93.8 9.7 %all-gather.5.cloned.1.call-done.refs_4_ = bf16[768,2304]{1,0:T(8,128)(2,1)} async-done(((bf16[96,2304]{1,0:T(8,128)(2,1)}), bf16[768,2304]{1,0:T(8,128)(2,1)}) %all-gather.5.cloned.1.call-update) | async-done | bytes 3538960 | tf_op jit(solution)/shard_map/all_gather | solution.py:1303
  103.5 5.7 %widen_narrow.1 = (f32[128,768]{1,0:T(8,128)}, bf16[128,768]{1,0:T(8,128)(2,1)}, bf16[128,768]{1,0:T(8,128)(2,1)}, bf16[128,768]{1,0:T(8,128)(2,1)}, bf16[512,76...) custom-call(bf16[128,768]{1,0:T(8,128)(2,1)} %get-tuple-element.105.refs_0_, bf16[128,768]{1,0:T(8,128)(2,1)} %copy-done.25, ...), custom_call_target="tpu_custom_call" | custom-call | flops 30000001024 | tf_op jit(solution)/shard_map/widen_narrow/pallas_call | solution.py:600
  112.7 4.5 %collective-permute-done.14.a_ref = bf16[128,768]{1,0:T(8,128)(2,1)S(1)} collective-permute-done((bf16[128,768]{1,0:T(8,128)(2,1)}, bf16[128,768]{1,0:T(8,128)(2,1)S(1)}, u32[]{:S(2)}, u32[]{:S(2)}) %collective-permute-start.14) | collective-permute-done | bytes 196640 | tf_op jit(solution)/shard_map/ppermute | solution.py:242
  117.2 4.7 %collective-permute-done.15.b_ref = bf16[128,768]{1,0:T(8,128)(2,1)S(1)} collective-permute-done((bf16[128,768]{1,0:T(8,128)(2,1)}, bf16[128,768]{1,0:T(8,128)(2,1)S(1)}, u32[]{:S(2)}, u32[]{:S(2)}) %collective-permute-start.15) | collective-permute-done | bytes 196640 | tf_op jit(solution)/shard_map/ppermute | solution.py:242
  133.5 3.5 %collective-permute-done.18.refs_2_.refs_6_ = bf16[128,768]{1,0:T(8,128)(2,1)S(1)} collective-permute-done((bf16[128,768]{1,0:T(8,128)(2,1)}, bf16[128,768]{1,0:T(8,128)(2,1)S(1)}, u32[]{:S(2)}, u32[]{:S(2)}) %collective-permute-start.18) | collective-permute-done | bytes 196640 | tf_op jit(solution)/shard_map/ppermute | solution.py:242
  137.6 6.9 %widen_narrow_back.1 = (f32[128,768]{1,0:T(8,128)}, bf16[128,768]{1,0:T(8,128)(2,1)}, bf16[128,768]{1,0:T(8,128)(2,1)}, bf16[128,768]{1,0:T(8,128)(2,1)}, bf16[5...) custom-call(bf16[128,768]{1,0:T(8,128)(2,1)} %get-tuple-element.118.refs_0_.refs_4_, bf16[128,768]{1,0:T(8,128)(2,1)} %copy-done.30, ...), custom_call_target="tpu_custom_call" | custom-call | flops 35000000512 | tf_op jit(solution)/shard_map/widen_narrow_back/pallas_call | solution.py:600
  148.0 6.0 %wide_grads.1 = (bf16[768,2304]{1,0:T(8,128)(2,1)}, f32[1,768]{1,0:T(1,128)}, f32[1,768]{1,0:T(1,128)}) custom-call(bf16[128,768]{1,0:T(8,128)(2,1)} %get-tuple-element.105.refs_0_, bf16[128,768]{1,0:T(8,128)(2,1)} %copy-done.25, bf16[128,768]{1,0:T(8,128)(2,1)} %copy-done.26, bf16[128,768]{1,0:T(8,128)(2,1)} %copy-done.27, ...), custom_call_target="tpu_custom_call" | custom-call | flops 30000001024 | tf_op jit(solution)/shard_map/wide_grads/pallas_call | solution.py:600
  173.8 8.0 %attend_back.1 = (bf16[512,192]{1,0:T(8,128)(2,1)}, f32[512,384]{1,0:T(8,128)}, bf16[512,384]{1,0:T(8,128)(2,1)}) custom-call(s32[4]{0:T(128)} %pad_add_fusion.refs_0_.ids_ref, f32[3]{0:T(128)} %power_multiply_fusion.slope_ref, bf16[512,192]{1,0:T(8,128)(2,1)} %get-tuple-element.98.q_ref, bf16[128,192]{1,0:T(8,128)(2,1)} %get-tuple-element.129.refs_0_, ...), custom_call_target="tpu_custom_call" | custom-call | flops 40000000000 | tf_op jit(solution)/shard_map/attend_back/pallas_call | solution.py:600
  184.6 4.2 %joined_grads.1 = (f32[2,4,64,576]{3,2,1,0:T(8,128)}, bf16[2,4,64,576]{3,2,1,0:T(8,128)(2,1)}, bf16[512,576]{1,0:T(8,128)(2,1)}) custom-call(s32[4]{0:T(128)} %pad_add_fusion.refs_0_.ids_ref, bf16[512,768]{1,0:T(8,128)(2,1)} %bitcast.64, bf16[512,192]{1,0:T(8,128)(2,1)} %get-tuple-element.135.q_ref, f32[512,384]{1,0:T(8,128)} %get-tuple-element.136.kv_ref, ...), custom_call_target="tpu_custom_call" | custom-call | flops 20000000000 | tf_op jit(solution)/shard_map/joined_grads/pallas_call | solution.py:600
  193.3 8.4 %collective-permute-done.39 = bf16[4,64,768]{2,1,0:T(8,128)(2,1)S(1)} collective-permute-done((bf16[4,64,768]{2,1,0:T(8,128)(2,1)S(1)}, bf16[4,64,768]{2,1,0:T(8,128)(2,1)S(1)}, u32[]{:S(2)}, u32[]{:S(2)}) %collective-permute-start.39) | collective-permute-done | bytes 393248 | tf_op jit(solution)/shard_map/ppermute | solution.py:242
  202.6 5.1 %all-to-all-start.2 = ((bf16[4,64,768]{2,1,0:T(8,128)(2,1)}), bf16[4,64,768]{2,1,0:T(8,128)(2,1)S(1)}, u32[]{:S(2)}, u32[]{:S(2)}) async-start(bf16[4,64,768]{2,1,0:T(8,128)(2,1)} %add_convert_fusion), calls=%async_computation.3 | async-start | bytes 786432 | tf_op jit(solution)/shard_map/all_to_all | solution.py:1272
  209.5 3.4 %tokens_parts.1 = (f32[128,768]{1,0:T(8,128)}, bf16[128,768]{1,0:T(8,128)(2,1)}, bf16[128,768]{1,0:T(8,128)(2,1)}, bf16[128,768]{1,0:T(8,128)(2,1)}) custom-call(s32[4]{0:T(128)} %pad_add_fusion.refs_0_.ids_ref, bf16[512,576]{1,0:T(8,128)(2,1)} %get-tuple-element.155.jb_ref, bf16[768,576]{1,0:T(8,128)(2,1)} %get-tuple-element.96.w_ref), custom_call_target="tpu_custom_call" | custom-call | flops 20000000000 | tf_op jit(solution)/shard_map/tokens_parts/pallas_call | solution.py:600
  212.9 3.8 %collective-permute-start.36 = (bf16[128,768]{1,0:T(8,128)(2,1)}, bf16[128,768]{1,0:T(8,128)(2,1)S(1)}, u32[]{:S(2)}, u32[]{:S(2)}) collective-permute-start(bf16[128,768]{1,0:T(8,128)(2,1)} %get-tuple-element.157), channel_id=1, source_target_pairs={{0,6},{1,7},{2,0},{3,1},{4,2},{5,3},{6,4},{7,5},{8,14},{9,15},{10,... | collective-permute-start | bytes 589832 | tf_op jit(solution)/shard_map/ppermute | solution.py:239
  224.6 4.0 %collective-permute-done.33.refs_1_ = bf16[48,1536]{1,0:T(8,128)(2,1)S(1)} collective-permute-done((bf16[48,1536]{1,0:T(8,128)(2,1)S(1)}, bf16[48,1536]{1,0:T(8,128)(2,1)S(1)}, u32[]{:S(2)}, u32[]{:S(2)}) %collective-permute-start.33) | collective-permute-done | bytes 147488 | tf_op jit(solution)/shard_map/ppermute | solution.py:242
  230.8 3.7 %all-to-all-start.1 = ((bf16[4,64,576]{2,1,0:T(8,128)(2,1)}), bf16[4,64,576]{2,1,0:T(8,128)(2,1)S(1)}, u32[]{:S(2)}, u32[]{:S(2)}) async-start(bf16[4,64,576]{2,1,0:T(8,128)(2,1)} %add_convert_fusion.2), calls=%async_computation.2 | async-start | bytes 655360 | tf_op jit(solution)/shard_map/all_to_all | solution.py:1272
  238.9 5.0 %collective-permute-done.37 = bf16[128,768]{1,0:T(8,128)(2,1)S(1)} collective-permute-done((bf16[128,768]{1,0:T(8,128)(2,1)S(1)}, bf16[128,768]{1,0:T(8,128)(2,1)S(1)}, u32[]{:S(2)}, u32[]{:S(2)}) %collective-permute-start.37) | collective-permute-done | bytes 196640 | tf_op jit(solution)/shard_map/ppermute | solution.py:239
  (224 shorter events, 121.7 us)
Async XLA Ops:
  7.2 71.3 %all-gather.3.cloned.1.call-start = ((), (), s32[]{:S(2)}) async-start(), calls=%async_computation.4 | async-start | bytes 1253376 | tf_op jit(solution)/shard_map/all_gather | solution.py:1278
  25.1 28.6 %all-to-all-start = ((bf16[4,128,768]{2,1,0:T(8,128)(2,1)}), bf16[4,128,768]{2,1,0:T(8,128)(2,1)S(1)}, u32[]{:S(2)}, u32[]{:S(2)}) async-start(bf16[4,128,768]{2,1,0:T(8,128)(2,1)} %broadcast_in_dim.52), calls=%async_computation | async-start | bytes 1572864 | tf_op jit(solution)/shard_map/all_to_all | solution.py:1272
  30.4 73.1 %all-gather.5.cloned.1.call-start = ((), (), s32[]{:S(2)}) async-start(), calls=%async_computation.5 | async-start | bytes 3981312 | tf_op jit(solution)/shard_map/all_gather | solution.py:1303
  47.0 169.7 %reduce-scatter.2.cloned.1.call-start = ((), (), s32[]{:S(2)}) async-start(), calls=%async_computation.6 | async-start | bytes 3981312 | tf_op jit(solution)/shard_map/reduce_scatter | solution.py:1343
  67.0 11.5 %collective-permute-start.8 = (bf16[128,192]{1,0:T(8,128)(2,1)}, bf16[128,192]{1,0:T(8,128)(2,1)S(1)}, u32[]{:S(2)}, u32[]{:S(2)}) collective-permute-start(bf16[128,192]{1,0:T(8,128)(2,1)} %get-tuple-element.102), channel_id=1, source_target_pairs={{0,4},{1,5},{2,6},{3,7},{4,0},{5,1},{6,2},{7,3},{8,12},{9,13},{10,... | collective-permute-start | bytes 147464 | tf_op jit(solution)/shard_map/ppermute | solution.py:239
  68.5 10.0 %collective-permute-start.9 = (bf16[128,192]{1,0:T(8,128)(2,1)}, bf16[128,192]{1,0:T(8,128)(2,1)S(1)}, u32[]{:S(2)}, u32[]{:S(2)}) collective-permute-start(bf16[128,192]{1,0:T(8,128)(2,1)} %get-tuple-element.103), channel_id=1, source_target_pairs={{0,6},{1,7},{2,0},{3,1},{4,2},{5,3},{6,4},{7,5},{8,14},{9,15},{10,... | collective-permute-start | bytes 147464 | tf_op jit(solution)/shard_map/ppermute | solution.py:239
  83.6 10.2 %collective-permute-start.11 = (bf16[128,768]{1,0:T(8,128)(2,1)}, bf16[128,768]{1,0:T(8,128)(2,1)S(1)}, u32[]{:S(2)}, u32[]{:S(2)}) collective-permute-start(bf16[128,768]{1,0:T(8,128)(2,1)} %get-tuple-element.105.refs_0_), channel_id=1, source_target_pairs={{0,8},{8,0},{1,9},{9,1},{2,10},{10,2},{3,11},{11,3},{4,12},{12,4},... | collective-permute-start | bytes 589832 | tf_op jit(solution)/shard_map/ppermute | solution.py:242
  110.7 11.2 %collective-permute-start.15 = (bf16[128,768]{1,0:T(8,128)(2,1)}, bf16[128,768]{1,0:T(8,128)(2,1)S(1)}, u32[]{:S(2)}, u32[]{:S(2)}) collective-permute-start(bf16[128,768]{1,0:T(8,128)(2,1)} %get-tuple-element.114), channel_id=1, source_target_pairs={{0,8},{8,0},{1,9},{9,1},{2,10},{10,2},{3,11},{11,3},{4,12},{12,4},... | collective-permute-start | bytes 589832 | tf_op jit(solution)/shard_map/ppermute | solution.py:242
  112.2 9.7 %collective-permute-start.16 = (bf16[128,768]{1,0:T(8,128)(2,1)}, bf16[128,768]{1,0:T(8,128)(2,1)S(1)}, u32[]{:S(2)}, u32[]{:S(2)}) collective-permute-start(bf16[128,768]{1,0:T(8,128)(2,1)} %get-tuple-element.115), channel_id=1, source_target_pairs={{0,24},{8,16},{16,8},{24,0},{1,25},{9,17},{17,9},{25,1},{2,26},{10... | collective-permute-start | bytes 589832 | tf_op jit(solution)/shard_map/ppermute | solution.py:246
  126.6 10.3 %collective-permute-start.18 = (bf16[128,768]{1,0:T(8,128)(2,1)}, bf16[128,768]{1,0:T(8,128)(2,1)S(1)}, u32[]{:S(2)}, u32[]{:S(2)}) collective-permute-start(bf16[128,768]{1,0:T(8,128)(2,1)} %get-tuple-element.118.refs_0_.refs_4_), channel_id=1, source_target_pairs={{0,8},{8,0},{1,9},{9,1},{2,10},{10,2},{3,11},{11,3},{4,12},{12,4},... | collective-permute-start | bytes 589832 | tf_op jit(solution)/shard_map/ppermute | solution.py:242
  127.5 9.4 %collective-permute-start.19 = (bf16[128,768]{1,0:T(8,128)(2,1)}, bf16[128,768]{1,0:T(8,128)(2,1)}, u32[]{:S(2)}, u32[]{:S(2)}) collective-permute-start(bf16[128,768]{1,0:T(8,128)(2,1)} %get-tuple-element.118.refs_0_.refs_4_), channel_id=1, source_target_pairs={{0,24},{8,16},{16,8},{24,0},{1,25},{9,17},{17,9},{25,1},{2,26},{10... | collective-permute-start | bytes 589832 | tf_op jit(solution)/shard_map/ppermute | solution.py:246
  144.5 9.5 %collective-permute-start.20 = (bf16[128,768]{1,0:T(8,128)(2,1)}, bf16[128,768]{1,0:T(8,128)(2,1)S(1)}, u32[]{:S(2)}, u32[]{:S(2)}) collective-permute-start(bf16[128,768]{1,0:T(8,128)(2,1)} %get-tuple-element.122), channel_id=1, source_target_pairs={{0,16},{16,0},{1,17},{17,1},{2,18},{18,2},{3,19},{19,3},{4,20},{20... | collective-permute-start | bytes 589832 | tf_op jit(solution)/shard_map/ppermute | solution.py:242
  163.5 9.7 %collective-permute-start.24 = (bf16[128,192]{1,0:T(8,128)(2,1)S(1)}, bf16[128,192]{1,0:T(8,128)(2,1)S(1)}, u32[]{:S(2)}, u32[]{:S(2)}) collective-permute-start(bf16[128,192]{1,0:T(8,128)(2,1)S(1)} %copy-done.46), channel_id=1, source_target_pairs={{0,4},{1,5},{2,6},{3,7},{4,0},{5,1},{6,2},{7,3},{8,12},{9,13},{10,... | collective-permute-start | bytes 147464 | tf_op jit(solution)/shard_map/ppermute | solution.py:239
  167.6 14.2 %collective-permute-start.27 = (bf16[4,64,768]{2,1,0:T(8,128)(2,1)S(1)}, bf16[4,64,768]{2,1,0:T(8,128)(2,1)S(1)}, u32[]{:S(2)}, u32[]{:S(2)}) collective-permute-start(bf16[4,64,768]{2,1,0:T(8,128)(2,1)S(1)} %fusion.7), channel_id=1, source_target_pairs={{0,8},{8,0},{1,9},{9,1},{2,10},{10,2},{3,11},{11,3},{4,12},{12,4},... | collective-permute-start | bytes 1179656 | tf_op jit(solution)/shard_map/ppermute | solution.py:242
  190.3 11.4 %collective-permute-start.39 = (bf16[4,64,768]{2,1,0:T(8,128)(2,1)S(1)}, bf16[4,64,768]{2,1,0:T(8,128)(2,1)S(1)}, u32[]{:S(2)}, u32[]{:S(2)}) collective-permute-start(bf16[4,64,768]{2,1,0:T(8,128)(2,1)S(1)} %fusion.5), channel_id=1, source_target_pairs={{0,16},{16,0},{1,17},{17,1},{2,18},{18,2},{3,19},{19,3},{4,20},{20... | collective-permute-start | bytes 1179656 | tf_op jit(solution)/shard_map/ppermute | solution.py:242
  192.3 10.3 %collective-permute-start.30 = (bf16[4,64,576]{2,1,0:T(8,128)(2,1)S(1)}, bf16[4,64,576]{2,1,0:T(8,128)(2,1)}, u32[]{:S(2)}, u32[]{:S(2)}) collective-permute-start(bf16[4,64,576]{2,1,0:T(8,128)(2,1)S(1)} %fusion.8), channel_id=1, source_target_pairs={{0,8},{8,0},{1,9},{9,1},{2,10},{10,2},{3,11},{11,3},{4,12},{12,4},... | collective-permute-start | bytes 884744 | tf_op jit(solution)/shard_map/ppermute | solution.py:242
  202.6 27.5 %all-to-all-start.2 = ((bf16[4,64,768]{2,1,0:T(8,128)(2,1)}), bf16[4,64,768]{2,1,0:T(8,128)(2,1)S(1)}, u32[]{:S(2)}, u32[]{:S(2)}) async-start(bf16[4,64,768]{2,1,0:T(8,128)(2,1)} %add_convert_fusion), calls=%async_computation.3 | async-start | bytes 786432 | tf_op jit(solution)/shard_map/all_to_all | solution.py:1272
  208.8 13.5 %collective-permute-start.31 = (bf16[4,64,576]{2,1,0:T(8,128)(2,1)S(1)}, bf16[4,64,576]{2,1,0:T(8,128)(2,1)S(1)}, u32[]{:S(2)}, u32[]{:S(2)}) collective-permute-start(bf16[4,64,576]{2,1,0:T(8,128)(2,1)S(1)} %fusion.6), channel_id=1, source_target_pairs={{0,16},{16,0},{1,17},{17,1},{2,18},{18,2},{3,19},{19,3},{4,20},{20... | collective-permute-start | bytes 884744 | tf_op jit(solution)/shard_map/ppermute | solution.py:242
  212.9 26.0 %collective-permute-start.36 = (bf16[128,768]{1,0:T(8,128)(2,1)}, bf16[128,768]{1,0:T(8,128)(2,1)S(1)}, u32[]{:S(2)}, u32[]{:S(2)}) collective-permute-start(bf16[128,768]{1,0:T(8,128)(2,1)} %get-tuple-element.157), channel_id=1, source_target_pairs={{0,6},{1,7},{2,0},{3,1},{4,2},{5,3},{6,4},{7,5},{8,14},{9,15},{10,... | collective-permute-start | bytes 589832 | tf_op jit(solution)/shard_map/ppermute | solution.py:239
  217.8 10.8 %collective-permute-start.34 = (bf16[48,1536]{1,0:T(8,128)(2,1)S(1)}, bf16[48,1536]{1,0:T(8,128)(2,1)S(1)}, u32[]{:S(2)}, u32[]{:S(2)}) collective-permute-start(bf16[48,1536]{1,0:T(8,128)(2,1)S(1)} %get-tuple-element.169), channel_id=1, source_target_pairs={{0,8},{8,0},{1,9},{9,1},{2,10},{10,2},{3,11},{11,3},{4,12},{12,4},... | collective-permute-start | bytes 442376 | tf_op jit(solution)/shard_map/ppermute | solution.py:242
  218.7 11.2 %collective-permute-start.35 = (bf16[48,1536]{1,0:T(8,128)(2,1)S(1)}, bf16[48,1536]{1,0:T(8,128)(2,1)S(1)}, u32[]{:S(2)}, u32[]{:S(2)}) collective-permute-start(bf16[48,1536]{1,0:T(8,128)(2,1)S(1)} %get-tuple-element.169), channel_id=1, source_target_pairs={{0,24},{8,16},{16,8},{24,0},{1,25},{9,17},{17,9},{25,1},{2,26},{10... | collective-permute-start | bytes 442376 | tf_op jit(solution)/shard_map/ppermute | solution.py:246
  228.5 15.4 %collective-permute-start.37 = (bf16[128,768]{1,0:T(8,128)(2,1)S(1)}, bf16[128,768]{1,0:T(8,128)(2,1)S(1)}, u32[]{:S(2)}, u32[]{:S(2)}) collective-permute-start(bf16[128,768]{1,0:T(8,128)(2,1)S(1)} %copy-done.29), channel_id=1, source_target_pairs={{0,4},{1,5},{2,6},{3,7},{4,0},{5,1},{6,2},{7,3},{8,12},{9,13},{10,... | collective-permute-start | bytes 589832 | tf_op jit(solution)/shard_map/ppermute | solution.py:239
  228.6 15.3 %collective-permute-start.38 = (bf16[128,768]{1,0:T(8,128)(2,1)S(1)}, bf16[128,768]{1,0:T(8,128)(2,1)S(1)}, u32[]{:S(2)}, u32[]{:S(2)}) collective-permute-start(bf16[128,768]{1,0:T(8,128)(2,1)S(1)} %copy-done.28), channel_id=1, source_target_pairs={{0,2},{1,3},{2,4},{3,5},{4,6},{5,7},{6,0},{7,1},{8,10},{9,11},{10,... | collective-permute-start | bytes 589832 | tf_op jit(solution)/shard_map/ppermute | solution.py:239
  230.8 16.5 %all-to-all-start.1 = ((bf16[4,64,576]{2,1,0:T(8,128)(2,1)}), bf16[4,64,576]{2,1,0:T(8,128)(2,1)S(1)}, u32[]{:S(2)}, u32[]{:S(2)}) async-start(bf16[4,64,576]{2,1,0:T(8,128)(2,1)} %add_convert_fusion.2), calls=%async_computation.2 | async-start | bytes 655360 | tf_op jit(solution)/shard_map/all_to_all | solution.py:1272
  (73 other events, 433.9 us)
Sparse Core Ops, SparseCore 0:
  10.3 45.1 all-gather.2
  57.7 45.7 all-gather.4
  162.7 43.5 reduce-scatter.1

commit v4 on v3

--- a/solution.py
+++ b/solution.py
@@ -571,6 +571,10 @@
     "assemble_joined": 0,
     "pick_widen": 0,
     "pack_widen": 0,
+    "cut_joined": 0,
+    "cut_wide": 0,
+    "assemble_output": 0,
+    "finish_tokens": 0,
     "split_joined": 3,
     "attend": 5,
     "attend_back": 8,
@@ -581,10 +585,10 @@
     "turn_first": 3,
     "wide_grads": 6,
     "output_grads": 3,
-    "tokens_parts": 4,
+    "tokens_parts": 0,
     "joined_grads": 4,
-    "finish_widen": 3,
-    "finish_joined": 2,
+    "finish_widen": 0,
+    "finish_joined": 0,
 }
 
 SMEM = pl.BlockSpec(memory_space=pltpu.SMEM)
@@ -740,6 +744,19 @@
         out_ref[:, cols:] = low_ref[...]
 
     return call(body, "pack_widen", [ids, near, got, low], [((2 * kb, cols + width), BF)])[0]
+
+
+def assemble_output(weights, kb):
+    width, cols = weights.shape
+    half = width // (2 * kb)
+
+    def body(all_ref, w_ref):
+        for y in range(2):
+            for c in range(half):
+                rows = slice((c * 2 + y) * kb, (c * 2 + y + 1) * kb)
+                w_ref[(y * half + c) * kb : (y * half + c + 1) * kb, :] = all_ref[rows, :]
+
+    return call(body, "assemble_output", [weights], [((width, cols), BF)])[0]
 
 
 def owner_order(value, kb):
@@ -1128,22 +1145,45 @@
     )
 
 
-def tokens_parts(ids, back, weight):
+def tokens_parts(ids, back, weight, low):
     count, cols = back.shape
     rows = count // GROUPS
     width = weight.shape[0]
-
-    def body(ids_ref, jb_ref, w_ref, *outs):
-        for k, ref in enumerate(outs):
-            part = dot_nt(jb_ref[piece_rows(ids_ref, k, rows, -1), :], w_ref[...])
-            ref[...] = part.astype(ref.dtype)
+    more = low.shape[1]
+
+    def body(jb_ref, w_ref, low_ref, out_ref):
+        for g in range(GROUPS):
+            part = dot_nt(jb_ref[g * rows : (g + 1) * rows, :], w_ref[...])
+            out_ref[g, :rows, :] = part.astype(BF)
+            out_ref[g, rows:, :] = low_ref[g]
 
     return call(
         body,
         "tokens_parts",
-        [ids, back, weight],
-        [((rows, width), F32)] + [((rows, width), BF)] * 3,
+        [back, weight, low],
+        [((GROUPS, rows + more, width), BF)],
         flops=2 * count * width * cols,
+    )[0]
+
+
+def finish_tokens(got, attn_back):
+    rows, width = attn_back.shape
+    more = got.shape[1] - rows
+
+    def body(got_ref, attn_ref, out_ref, sum_ref):
+        total = attn_ref[...]
+        rest = jnp.zeros((more, width), F32)
+        for g in range(GROUPS):
+            total = total + got_ref[g, :rows, :].astype(F32)
+            rest = rest + got_ref[g, rows:, :].astype(F32)
+        out_ref[...] = total
+        sum_ref[...] = rest.astype(BF)
+
+    return call(
+        body,
+        "finish_tokens",
+        [got, attn_back],
+        [((rows, width), F32), ((more, width), BF)],
     )
 
 
@@ -1182,19 +1222,34 @@
     )
 
 
-def finish_widen(ids, pieces, low, low_got):
-    kb, cols = pieces[0].shape
-    half, width = low.shape
+def cut_wide(ids, total, kb):
+    cols = total.shape[1] - 16 * kb
+    width = 16 * kb
+
+    def body(ids_ref, all_ref, side_ref, far_ref):
+        y = ids_ref[2]
+        side_ref[:, :cols] = all_ref[pl.ds(pl.multiple_of(y * kb, 16), kb), :cols]
+        for half in range(2):
+            side_ref[:, cols + half * width : cols + (half + 1) * width] = all_ref[half * kb : (half + 1) * kb, cols:]
+        far_ref[...] = all_ref[pl.ds(pl.multiple_of((1 - y) * kb, 16), kb), :cols]
+
+    return call(body, "cut_wide", [ids, total], [((kb, cols + 2 * width), BF), ((kb, cols), BF)])
+
+
+def finish_widen(ids, pieces):
+    kb, cols = pieces[2].shape
+    width = 16 * kb
+    half = 2 * kb
     quarter = cols // 2
     count = quarter // half
 
     def body(ids_ref, *refs):
-        low_ref, got_ref, out_ref, narrow_ref, all_ref = refs[4:]
+        out_ref, narrow_ref, all_ref = refs[4:]
         y, x = ids_ref[2], ids_ref[3]
         for k in range(4):
             row = y if k < 2 else 1 - y
             col = x if k % 2 == 0 else 1 - x
-            all_ref[row * 2 + col] = refs[k][...].astype(F32)
+            all_ref[row * 2 + col] = refs[k][:, :cols].astype(F32)
         for part in range(2):
             for row in range(2):
                 picks = []
@@ -1204,23 +1259,40 @@
                         picks.append(all_ref[row * 2 + col, :, at : at + half])
                 at = (part * 2 + row) * 2 * quarter
                 out_ref[:, at : at + 2 * quarter] = jnp.concatenate(picks, axis=1)
-        narrow_ref[pl.ds(pl.multiple_of(x * half, 16), half), :] = low_ref[...].astype(F32)
-        narrow_ref[pl.ds(pl.multiple_of((1 - x) * half, 16), half), :] = got_ref[...].astype(F32)
+        for k in range(2):
+            for line in range(2):
+                at = (x if k == 0 else 1 - x) * half + line * kb
+                rows = pl.ds(pl.multiple_of(at, 16), kb)
+                narrow_ref[rows, :] = refs[k][:, cols + line * width : cols + (line + 1) * width].astype(F32)
 
     return call(
         body,
         "finish_widen",
-        [ids] + list(pieces) + [low, low_got],
+        [ids] + list(pieces),
         [((kb, 8 * quarter), F32), ((2 * half, width), F32)],
         scratch=[pltpu.VMEM((4, kb, cols), F32)],
     )
 
 
-def finish_joined(got, kb):
-    wide = got.shape[2]
+def cut_joined(ids, own, got):
+    shape = own.shape[1:]
+
+    def body(ids_ref, own_ref, got_ref, *outs):
+        for k, ref in enumerate(outs):
+            turn = (ids_ref[0] + k) % GROUPS
+            ref[...] = (own_ref[turn].astype(F32) + got_ref[turn].astype(F32)).astype(BF)
+
+    return call(body, "cut_joined", [ids, own, got], [(shape, BF)] * GROUPS)
+
+
+def finish_joined(ids, pieces, kb):
+    lines, wide = pieces[0].shape
     cols = wide // 3
 
-    def body(got_ref, out_ref, small_ref):
+    def body(ids_ref, *refs):
+        out_ref, small_ref, got_ref = refs[GROUPS:]
+        for k in range(GROUPS):
+            got_ref[(ids_ref[0] + GROUPS - k) % GROUPS] = refs[k][...]
         for g in range(GROUPS):
             for part in range(3):
                 at = (part * GROUPS + g) * cols
@@ -1230,7 +1302,13 @@
             small = small + got_ref[g, kb:, :].astype(F32)
         small_ref[...] = small
 
-    return call(body, "finish_joined", [got], [((kb, GROUPS * wide), F32), ((16, wide), F32)])
+    return call(
+        body,
+        "finish_joined",
+        [ids] + list(pieces),
+        [((kb, GROUPS * wide), F32), ((16, wide), F32)],
+        scratch=[pltpu.VMEM((GROUPS, lines, wide), BF)],
+    )
 
 
 def fast_device(
@@ -1275,7 +1353,6 @@
         far = at.swap(value, "seq")
         return (value, far, at.partner(value), at.partner(far))
 
-    w_output = lax.all_gather(output_weight, ("seq", "ctx"), tiled=True)
     packed = pack_joined(
         ids,
         joined_weight,
@@ -1292,6 +1369,13 @@
         widen_bias,
         cols,
     )
+    output_far = after(at.swap(output_weight, "seq"), packed[0])
+    output_pair = jnp.where(
+        at.seq == 0,
+        jnp.concatenate([output_weight, output_far], axis=0),
+        jnp.concatenate([output_far, output_weight], axis=0),
+    )
+    output_got = lax.all_gather(output_pair, "ctx", tiled=True)
     joined_rel = [packed[0]] + [at.shift(packed[k], k) for k in range(1, GROUPS)]
     x_cut = jnp.broadcast_to(after(inputs, *joined_rel)[None], (GROUPS, rows, width))
     x_four = across(x_cut).reshape(-1, width)
@@ -1299,8 +1383,9 @@
     joined_parts = spread_out(joined_got)
     w_joined, vec, near, wide = assemble_joined(ids, joined_parts, kb)
     widen_near, widen_far, narrow_low = pick_widen(after(ids, packed[3]), widen_weight, narrow_weight)
-    widen_got = at.swap(after(widen_far, joined_parts[1]), "seq")
-    w_wide = lax.all_gather(pack_widen(ids, widen_near, widen_got, narrow_low), "ctx", tiled=True)
+    widen_got = at.swap(after(widen_far, *joined_rel), "seq")
+    widen_all = pack_widen(ids, after(widen_near, w_joined), widen_got, narrow_low)
+    w_wide = lax.all_gather(widen_all, "ctx", tiled=True)
 
     queries, kv_own = split_joined(x_four, w_joined, near, scale)
     kv_other = at.partner(kv_own)
@@ -1325,6 +1410,8 @@
     mixed_near, inv = attended[:2]
     mixed_send = attended[2:]
     mixed_rel = [mixed_send[0]] + [at.shift(mixed_send[k], k) for k in range(1, GROUPS)]
+    w_output = assemble_output(output_got, kb)
+
     first, first_low, first_unit, first_root = close_attention(
         ids, inputs, mixed_rel, w_output, vec, kb
     )
@@ -1363,28 +1450,24 @@
     kv_got = at.partner(kv_give)
 
     output_sum = (output_keep[0] + output_got[0].astype(F32) + output_far.astype(F32)).astype(BF)
-    output_both = (output_sum.astype(F32) + at.swap(output_sum, "rep").astype(F32)).astype(BF)
     joined_keep, joined_give, joined_back = joined_grads(ids, x_four, query_back, kv_keep, kv_got, kb)
     joined_got = at.partner(joined_give)
-    own, s1, s2, s3 = tokens_parts(ids, joined_back, w_joined)
-    received = [at.shift(s1, -1), at.shift(s2, -2), at.shift(s3, -3)]
-    joined_far = at.swap(seq_send(joined_keep[1], joined_got[1]), "seq")
+    parts = tokens_parts(ids, joined_back, w_joined, output_sum)
+    tokens_got = across(parts)
+    joined_far = at.swap(seq_send(joined_keep[1], after(joined_got, parts)[1]), "seq")
     joined_sum = (joined_keep[0] + joined_got[0].astype(F32) + joined_far.astype(F32)).astype(BF)
     wide_sum = after(wide_sum, joined_got)
-    low_sum = wide_sum[:, 2 * quarter :]
-    row_own = lax.dynamic_slice_in_dim(wide_sum, at.seq * kb, kb, 0)[:, : 2 * quarter]
-    row_far = lax.dynamic_slice_in_dim(wide_sum, (1 - at.seq) * kb, kb, 0)[:, : 2 * quarter]
-    joined_both = (joined_sum.astype(F32) + at.swap(joined_sum, "rep").astype(F32)).astype(BF)
-    widen_pieces = [row_own, at.plane(row_own, 1), at.plane(row_far, 2), at.plane(row_far, 3)]
-    low_got = at.plane(low_sum, 1)
-    joined_mine = after(joined_both, low_got, *widen_pieces)
-    widen_total, narrow_total = finish_widen(ids, widen_pieces, low_sum, low_got)
-    output_all = across(after(output_both, joined_far))
-    output_total = jnp.sum(after(output_all, joined_mine).astype(F32), axis=0)
-    joined_total, pair = finish_joined(across(joined_mine), kb)
-    tokens_grad = after(attn_back, joined_mine) + own
-    for item in received:
-        tokens_grad = tokens_grad + item.astype(F32)
+    side, far = cut_wide(ids, wide_sum, kb)
+    widen_pieces = [side, at.plane(side, 1), at.plane(far, 2), at.plane(far, 3)]
+    joined_mine = cut_joined(after(ids, *widen_pieces[1:]), joined_sum, at.swap(joined_sum, "rep"))
+    widen_total, narrow_total = finish_widen(ids, widen_pieces)
+    joined_total, pair = finish_joined(
+        ids,
+        [joined_mine[0]] + [at.shift(joined_mine[k], k) for k in range(1, GROUPS)],
+        kb,
+    )
+    tokens_grad, output_mine = finish_tokens(tokens_got, after(attn_back, joined_mine[0]))
+    output_total = output_mine.astype(F32) + at.swap(output_mine, "rep").astype(F32)
     last = output_total[kb:, :kb]
     return (
         result[None],

time: 259 us -> 251 us (0.969)
  waiting for transfers between devices: 83.5 us -> 71.1 us
  Pallas kernels: 68.1 us -> 76.9 us
  starting transfers between devices: 62.1 us -> 58.9 us
    ppermute x17, waiting for transfers between devices: 44.1 us -> 32.7 us  [swap(): return lax.ppermute(value, axis, [(0, 1), (1, 0)])]
    pallas_call x18 -> x22, Pallas kernels: 68.1 us -> 76.9 us  [call(): pl.pallas_call(body, grid=grid, in_specs=in_specs, out_specs=out_specs, o...]
    all_gather x2, waiting for transfers between devices: 9.73 us -> 2.51 us  [the longest x1 2.51 us: fast_device(): w_wide = lax.all_gather(widen_all, 'ctx', tiled=True)]
    ppermute x12, waiting for transfers between devices: 22.4 us -> 15.5 us  [shift(): lax.ppermute(value, 'ctx', [(i, (i + steps * r) % n) for i in range(n)])]
    ppermute x5, waiting for transfers between devices: 0.01 us -> 6.27 us  [plane(): return lax.ppermute(value, ('rep', 'seq'), [(i, 3 - i) for i in range(4)])]
    reduce_scatter x1, waiting for transfers between devices: 0.01 us -> 5.74 us  [fast_device(): wide_sum = lax.psum_scatter(wide_grad, 'ctx', tiled=True)]
    all_to_all x3 -> x2, starting transfers between devices: 14.2 us -> 10.4 us  [across(): lax.all_to_all(value, 'ctx', 0, 0, axis_index_groups=columns, tiled=True)]
    unnamed x103 -> x93, local copies, waits for them, and re-layouts: 10.4 us -> 11.2 us
  transfers between devices with their start and end apart: 46 -> 45, of which waited for: 25 -> 23; matrix products, arithmetic and copies ran while one was open for 7% -> 5% of each run, Pallas kernels for 17% -> 22%
where the time goes in v4:
time: 251 us; the launch traced here: 250 us
  Pallas kernels  76.9 us (31%)
  waiting for transfers between devices  71.1 us (28%)
  starting transfers between devices  58.9 us (23%)
  local copies, waits for them, and re-layouts  19.4 us (8%)
  between operations  14.1 us (6%)
  other arithmetic  9.92 us (4%)
    pallas_call x22, Pallas kernels, call(): pl.pallas_call(body, grid=grid, in_specs=in_specs, out_specs=out_specs, o...  76.9 us
    ppermute x17, waiting for transfers between devices, swap(): return lax.ppermute(value, axis, [(0, 1), (1, 0)])  32.7 us
    ppermute x12, starting transfers between devices, shift(): lax.ppermute(value, 'ctx', [(i, (i + steps * r) % n) for i in range(n)])  23.4 us
    ppermute x17, starting transfers between devices, swap(): return lax.ppermute(value, axis, [(0, 1), (1, 0)])  19 us
    ppermute x12, waiting for transfers between devices, shift(): lax.ppermute(value, 'ctx', [(i, (i + steps * r) % n) for i in range(n)])  15.5 us
    unnamed x93, local copies, waits for them, and re-layouts  11.2 us
    all_to_all x2, starting transfers between devices, across(): lax.all_to_all(value, 'ctx', 0, 0, axis_index_groups=columns, tiled=True)  10.4 us
    ppermute x5, waiting for transfers between devices, plane(): return lax.ppermute(value, ('rep', 'seq'), [(i, 3 - i) for i in range(4)])  6.27 us
  transfers between devices with their start and end apart: 45, of which 23 were waited for; matrix products, arithmetic and copies ran while one was open for 5% of the time, Pallas kernels for 22%

profile of v4, /device:TPU:0, one launch (start us, length us, event | category | flops | bytes accessed | tf_op | source)
XLA Modules:
  0.0 250.4 jit_solution(2147178155507101865)
XLA Ops:
  27.6 5.0 %all-to-all-start = ((bf16[4,128,768]{2,1,0:T(8,128)(2,1)}), bf16[4,128,768]{2,1,0:T(8,128)(2,1)S(1)}, u32[]{:S(2)}, u32[]{:S(2)}) async-start(bf16[4,128,768]{2,1,0:T(8,128)(2,1)} %broadcast_in_dim.52), calls=%async_computation | async-start | bytes 1572864 | tf_op jit(solution)/shard_map/all_to_all | solution.py:1350
  35.0 5.0 %collective-permute-done.3.b_ref = bf16[4,64,576]{2,1,0:T(8,128)(2,1)S(1)} collective-permute-done((bf16[4,64,576]{2,1,0:T(8,128)(2,1)S(1)}, bf16[4,64,576]{2,1,0:T(8,128)(2,1)S(1)}, u32[]{:S(2)}, u32[]{:S(2)}) %collective-permute-start.3) | collective-permute-done | bytes 294944 | tf_op jit(solution)/shard_map/ppermute | solution.py:242
  50.5 3.9 %all-to-all-done = bf16[4,128,768]{2,1,0:T(8,128)(2,1)S(1)} async-done(((bf16[4,128,768]{2,1,0:T(8,128)(2,1)}), bf16[4,128,768]{2,1,0:T(8,128)(2,1)S(1)}, u32[]{:S(2)}, u32[]{:S(2)}) %all-to-all-start) | async-done | bytes 786464 | tf_op jit(solution)/shard_map/all_to_all | solution.py:1350
  55.3 3.1 %split_joined.1 = (bf16[512,192]{1,0:T(8,128)(2,1)}, bf16[512,384]{1,0:T(8,128)(2,1)}) custom-call(bf16[512,768]{1,0:T(8,128)(2,1)} %bitcast.62, bf16[768,576]{1,0:T(8,128)(2,1)} %get-tuple-element.101.w_ref, f32[16,192]{1,0:T(8,128)} %get-tuple-element.102.near_ref), custom_call_target="tpu_custom_call" | custom-call | flops 15000000512 | tf_op jit(solution)/shard_map/split_joined/pallas_call | solution.py:604
  61.1 4.7 %attend.1 = (f32[512,192]{1,0:T(8,128)}, f32[3,8,512]{2,1,0:T(8,128)}, bf16[128,192]{1,0:T(8,128)(2,1)}, bf16[128,192]{1,0:T(8,128)(2,1)}, bf16[128,192]{1,0:T(8,128)(2,1)}, /*index=5*/bf16[128,192]{1,0:T(8,128)(2,1)}) custom-call(s32[4]{0:T(128)} %pad_add_fusion.refs_0_.ids_ref, f32[3]{0:T(128)} %power_multiply_fusion.slope_ref, ...), custom_call_target="tpu_custom_call" | custom-call | flops 24999999488 | tf_op jit(solution)/shard_map/attend/pallas_call | solution.py:604
  74.2 4.3 %collective-permute-done.8.c_ref.refs_2_ = bf16[128,192]{1,0:T(8,128)(2,1)S(1)} collective-permute-done((bf16[128,192]{1,0:T(8,128)(2,1)}, bf16[128,192]{1,0:T(8,128)(2,1)S(1)}, u32[]{:S(2)}, u32[]{:S(2)}) %collective-permute-start.8) | collective-permute-done | bytes 49184 | tf_op jit(solution)/shard_map/ppermute | solution.py:239
  85.7 4.5 %collective-permute-done.11.refs_1_ = bf16[128,768]{1,0:T(8,128)(2,1)S(1)} collective-permute-done((bf16[128,768]{1,0:T(8,128)(2,1)}, bf16[128,768]{1,0:T(8,128)(2,1)S(1)}, u32[]{:S(2)}, u32[]{:S(2)}) %collective-permute-start.11) | collective-permute-done | bytes 196640 | tf_op jit(solution)/shard_map/ppermute | solution.py:242
  90.2 3.7 %collective-permute-done.12.refs_2_ = bf16[128,768]{1,0:T(8,128)(2,1)S(1)} collective-permute-done((bf16[128,768]{1,0:T(8,128)(2,1)}, bf16[128,768]{1,0:T(8,128)(2,1)S(1)}, u32[]{:S(2)}, u32[]{:S(2)}) %collective-permute-start.12) | collective-permute-done | bytes 196640 | tf_op jit(solution)/shard_map/ppermute | solution.py:242
  96.4 5.7 %widen_narrow.1 = (f32[128,768]{1,0:T(8,128)}, bf16[128,768]{1,0:T(8,128)(2,1)}, bf16[128,768]{1,0:T(8,128)(2,1)}, bf16[128,768]{1,0:T(8,128)(2,1)}, bf16[512,76...) custom-call(bf16[128,768]{1,0:T(8,128)(2,1)} %get-tuple-element.111.refs_0_, bf16[128,768]{1,0:T(8,128)(2,1)} %copy-done.25, ...), custom_call_target="tpu_custom_call" | custom-call | flops 30000001024 | tf_op jit(solution)/shard_map/widen_narrow/pallas_call | solution.py:604
  105.6 4.5 %collective-permute-done.15.a_ref = bf16[128,768]{1,0:T(8,128)(2,1)S(1)} collective-permute-done((bf16[128,768]{1,0:T(8,128)(2,1)}, bf16[128,768]{1,0:T(8,128)(2,1)S(1)}, u32[]{:S(2)}, u32[]{:S(2)}) %collective-permute-start.15) | collective-permute-done | bytes 196640 | tf_op jit(solution)/shard_map/ppermute | solution.py:242
  110.1 4.7 %collective-permute-done.16.b_ref = bf16[128,768]{1,0:T(8,128)(2,1)S(1)} collective-permute-done((bf16[128,768]{1,0:T(8,128)(2,1)}, bf16[128,768]{1,0:T(8,128)(2,1)S(1)}, u32[]{:S(2)}, u32[]{:S(2)}) %collective-permute-start.16) | collective-permute-done | bytes 196640 | tf_op jit(solution)/shard_map/ppermute | solution.py:242
  126.4 3.5 %collective-permute-done.19.refs_2_.refs_6_ = bf16[128,768]{1,0:T(8,128)(2,1)S(1)} collective-permute-done((bf16[128,768]{1,0:T(8,128)(2,1)}, bf16[128,768]{1,0:T(8,128)(2,1)S(1)}, u32[]{:S(2)}, u32[]{:S(2)}) %collective-permute-start.19) | collective-permute-done | bytes 196640 | tf_op jit(solution)/shard_map/ppermute | solution.py:242
  130.5 6.9 %widen_narrow_back.1 = (f32[128,768]{1,0:T(8,128)}, bf16[128,768]{1,0:T(8,128)(2,1)}, bf16[128,768]{1,0:T(8,128)(2,1)}, bf16[128,768]{1,0:T(8,128)(2,1)}, bf16[5...) custom-call(bf16[128,768]{1,0:T(8,128)(2,1)} %get-tuple-element.125.refs_0_.refs_4_, bf16[128,768]{1,0:T(8,128)(2,1)} %copy-done.28, ...), custom_call_target="tpu_custom_call" | custom-call | flops 35000000512 | tf_op jit(solution)/shard_map/widen_narrow_back/pallas_call | solution.py:604
  140.9 6.0 %wide_grads.1 = (bf16[768,2304]{1,0:T(8,128)(2,1)}, f32[1,768]{1,0:T(1,128)}, f32[1,768]{1,0:T(1,128)}) custom-call(bf16[128,768]{1,0:T(8,128)(2,1)} %get-tuple-element.111.refs_0_, bf16[128,768]{1,0:T(8,128)(2,1)} %copy-done.25, bf16[128,768]{1,0:T(8,128)(2,1)} %copy-done.26, bf16[128,768]{1,0:T(8,128)(2,1)} %copy-done.27, ...), custom_call_target="tpu_custom_call" | custom-call | flops 30000001024 | tf_op jit(solution)/shard_map/wide_grads/pallas_call | solution.py:604
  147.8 3.4 %turn_first.1 = (f32[128,768]{1,0:T(8,128)}, bf16[128,768]{1,0:T(8,128)(2,1)}, f32[8,768]{1,0:T(8,128)}, bf16[128,192]{1,0:T(8,128)(2,1)}, bf16[128,192]{1,0:T(8...) custom-call(s32[4]{0:T(128)} %pad_add_fusion.refs_0_.ids_ref, f32[128,768]{1,0:T(8,128)} %get-tuple-element.128.own_ref, ...), custom_call_target="tpu_custom_call" | custom-call | flops 15000000512 | tf_op jit(solution)/shard_map/turn_first/pallas_call | solution.py:604
  151.2 3.2 %output_grads.1 = (f32[2,4,64,768]{3,2,1,0:T(8,128)}, bf16[2,4,64,768]{3,2,1,0:T(8,128)(2,1)}) custom-call(s32[4]{0:T(128)} %pad_add_fusion.refs_0_.ids_ref, bf16[128,192]{1,0:T(8,128)(2,1)} %get-tuple-element.105.a_ref.refs_0_, bf16[128,192]{1,0:T(8,128)(2,1)} %copy-done.37, bf16[128,192]{1,0:T(8,128)(2,1)} %copy-done.38, bf16[128,192]{1,0:T(8,128)(2,1)} %copy-done.39, ...), custom_call_target="tpu_custom_call" | custom-call | flops 15000000512 | tf_op jit(solution)/shard_map/output_grads/pallas_call | solution.py:604
  157.2 3.2 %collective-permute-start.26 = (bf16[128,192]{1,0:T(8,128)(2,1)S(1)}, bf16[128,192]{1,0:T(8,128)(2,1)S(1)}, u32[]{:S(2)}, u32[]{:S(2)}) collective-permute-start(bf16[128,192]{1,0:T(8,128)(2,1)S(1)} %copy-done.40), channel_id=1, source_target_pairs={{0,6},{1,7},{2,0},{3,1},{4,2},{5,3},{6,4},{7,5},{8,14},{9,15},{10,... | collective-permute-start | bytes 147464 | tf_op jit(solution)/shard_map/ppermute | solution.py:239
  166.9 8.0 %attend_back.1 = (bf16[512,192]{1,0:T(8,128)(2,1)}, f32[512,384]{1,0:T(8,128)}, bf16[512,384]{1,0:T(8,128)(2,1)}) custom-call(s32[4]{0:T(128)} %pad_add_fusion.refs_0_.ids_ref, f32[3]{0:T(128)} %power_multiply_fusion.slope_ref, bf16[512,192]{1,0:T(8,128)(2,1)} %get-tuple-element.103.q_ref, bf16[128,192]{1,0:T(8,128)(2,1)} %get-tuple-element.135.refs_0_, ...), custom_call_target="tpu_custom_call" | custom-call | flops 40000000000 | tf_op jit(solution)/shard_map/attend_back/pallas_call | solution.py:604
  177.7 4.2 %joined_grads.1 = (f32[2,4,64,576]{3,2,1,0:T(8,128)}, bf16[2,4,64,576]{3,2,1,0:T(8,128)(2,1)}, bf16[512,576]{1,0:T(8,128)(2,1)}) custom-call(s32[4]{0:T(128)} %pad_add_fusion.refs_0_.ids_ref, bf16[512,768]{1,0:T(8,128)(2,1)} %bitcast.63, bf16[512,192]{1,0:T(8,128)(2,1)} %get-tuple-element.141.q_ref, f32[512,384]{1,0:T(8,128)} %get-tuple-element.142.kv_ref, ...), custom_call_target="tpu_custom_call" | custom-call | flops 20000000000 | tf_op jit(solution)/shard_map/joined_grads/pallas_call | solution.py:604
  183.9 3.9 %tokens_parts.1 = bf16[4,192,768]{2,1,0:T(8,128)(2,1)} custom-call(bf16[512,576]{1,0:T(8,128)(2,1)} %get-tuple-element.155.jb_ref, bf16[768,576]{1,0:T(8,128)(2,1)} %get-tuple-element.101.w_ref, bf16[4,64,768]{2,1,0:T(8,128)(2,1)} %fusion.5.low_ref), custom_call_target="tpu_custom_call" | custom-call | tf_op jit(solution)/shard_map/tokens_parts/pallas_call | solution.py:604
  187.8 5.4 %all-to-all-start.1 = ((bf16[4,192,768]{2,1,0:T(8,128)(2,1)}), bf16[4,192,768]{2,1,0:T(8,128)(2,1)S(1)}, u32[]{:S(2)}, u32[]{:S(2)}) async-start(bf16[4,192,768]{2,1,0:T(8,128)(2,1)} %tokens_parts.1), calls=%async_computation.1 | async-start | bytes 2359296 | tf_op jit(solution)/shard_map/all_to_all | solution.py:1350
  194.1 5.7 %reduce-scatter.2.cloned.1.call-done.all_ref = bf16[96,2304]{1,0:T(8,128)(2,1)} async-done(((bf16[768,2304]{1,0:T(8,128)(2,1)}), bf16[96,2304]{1,0:T(8,128)(2,1)}) %reduce-scatter.2.cloned.1.call-update) | async-done | bytes 442384 | tf_op jit(solution)/shard_map/reduce_scatter | solution.py:1430
  210.2 6.3 %collective-permute-done.33.refs_3_ = bf16[48,1536]{1,0:T(8,128)(2,1)S(1)} collective-permute-done((bf16[48,1536]{1,0:T(8,128)(2,1)S(1)}, bf16[48,1536]{1,0:T(8,128)(2,1)S(1)}, u32[]{:S(2)}, u32[]{:S(2)}) %collective-permute-start.33) | collective-permute-done | bytes 147488 | tf_op jit(solution)/shard_map/ppermute | solution.py:246
  219.1 8.4 %collective-permute-start.37 = (bf16[64,576]{1,0:T(8,128)(2,1)}, bf16[64,576]{1,0:T(8,128)(2,1)S(1)}, u32[]{:S(2)}, u32[]{:S(2)}) collective-permute-start(bf16[64,576]{1,0:T(8,128)(2,1)} %get-tuple-element.170), channel_id=1, source_target_pairs={{0,4},{1,5},{2,6},{3,7},{4,0},{5,1},{6,2},{7,3},{8,12},{9,13},{10,... | collective-permute-start | bytes 221192 | tf_op jit(solution)/shard_map/ppermute | solution.py:239
  (212 shorter events, 119.1 us)
Async XLA Ops:
  7.2 62.5 %all-gather.3.cloned.1.call-start = ((), (), s32[]{:S(2)}) async-start(), calls=%async_computation.3 | async-start | bytes 1327104 | tf_op jit(solution)/shard_map/all_gather | solution.py:1378
  27.6 26.9 %all-to-all-start = ((bf16[4,128,768]{2,1,0:T(8,128)(2,1)}), bf16[4,128,768]{2,1,0:T(8,128)(2,1)S(1)}, u32[]{:S(2)}, u32[]{:S(2)}) async-start(bf16[4,128,768]{2,1,0:T(8,128)(2,1)} %broadcast_in_dim.52), calls=%async_computation | async-start | bytes 1572864 | tf_op jit(solution)/shard_map/all_to_all | solution.py:1350
  32.5 63.8 %all-gather.5.cloned.1.call-start = ((), (), s32[]{:S(2)}) async-start(), calls=%async_computation.4 | async-start | bytes 3981312 | tf_op jit(solution)/shard_map/all_gather | solution.py:1388
  49.0 150.9 %reduce-scatter.2.cloned.1.call-start = ((), (), s32[]{:S(2)}) async-start(), calls=%async_computation.5 | async-start | bytes 3981312 | tf_op jit(solution)/shard_map/reduce_scatter | solution.py:1430
  65.9 12.7 %collective-permute-start.8 = (bf16[128,192]{1,0:T(8,128)(2,1)}, bf16[128,192]{1,0:T(8,128)(2,1)S(1)}, u32[]{:S(2)}, u32[]{:S(2)}) collective-permute-start(bf16[128,192]{1,0:T(8,128)(2,1)} %get-tuple-element.107), channel_id=1, source_target_pairs={{0,4},{1,5},{2,6},{3,7},{4,0},{5,1},{6,2},{7,3},{8,12},{9,13},{10,... | collective-permute-start | bytes 147464 | tf_op jit(solution)/shard_map/ppermute | solution.py:239
  68.4 10.1 %collective-permute-start.9 = (bf16[128,192]{1,0:T(8,128)(2,1)}, bf16[128,192]{1,0:T(8,128)(2,1)S(1)}, u32[]{:S(2)}, u32[]{:S(2)}) collective-permute-start(bf16[128,192]{1,0:T(8,128)(2,1)} %get-tuple-element.108), channel_id=1, source_target_pairs={{0,6},{1,7},{2,0},{3,1},{4,2},{5,3},{6,4},{7,5},{8,14},{9,15},{10,... | collective-permute-start | bytes 147464 | tf_op jit(solution)/shard_map/ppermute | solution.py:239
  83.6 10.2 %collective-permute-start.12 = (bf16[128,768]{1,0:T(8,128)(2,1)}, bf16[128,768]{1,0:T(8,128)(2,1)S(1)}, u32[]{:S(2)}, u32[]{:S(2)}) collective-permute-start(bf16[128,768]{1,0:T(8,128)(2,1)} %get-tuple-element.111.refs_0_), channel_id=1, source_target_pairs={{0,8},{8,0},{1,9},{9,1},{2,10},{10,2},{3,11},{11,3},{4,12},{12,4},... | collective-permute-start | bytes 589832 | tf_op jit(solution)/shard_map/ppermute | solution.py:242
  103.6 11.2 %collective-permute-start.16 = (bf16[128,768]{1,0:T(8,128)(2,1)}, bf16[128,768]{1,0:T(8,128)(2,1)S(1)}, u32[]{:S(2)}, u32[]{:S(2)}) collective-permute-start(bf16[128,768]{1,0:T(8,128)(2,1)} %get-tuple-element.121), channel_id=1, source_target_pairs={{0,8},{8,0},{1,9},{9,1},{2,10},{10,2},{3,11},{11,3},{4,12},{12,4},... | collective-permute-start | bytes 589832 | tf_op jit(solution)/shard_map/ppermute | solution.py:242
  105.1 9.7 %collective-permute-start.17 = (bf16[128,768]{1,0:T(8,128)(2,1)}, bf16[128,768]{1,0:T(8,128)(2,1)S(1)}, u32[]{:S(2)}, u32[]{:S(2)}) collective-permute-start(bf16[128,768]{1,0:T(8,128)(2,1)} %get-tuple-element.122), channel_id=1, source_target_pairs={{0,24},{8,16},{16,8},{24,0},{1,25},{9,17},{17,9},{25,1},{2,26},{10... | collective-permute-start | bytes 589832 | tf_op jit(solution)/shard_map/ppermute | solution.py:246
  119.5 10.3 %collective-permute-start.19 = (bf16[128,768]{1,0:T(8,128)(2,1)}, bf16[128,768]{1,0:T(8,128)(2,1)S(1)}, u32[]{:S(2)}, u32[]{:S(2)}) collective-permute-start(bf16[128,768]{1,0:T(8,128)(2,1)} %get-tuple-element.125.refs_0_.refs_4_), channel_id=1, source_target_pairs={{0,8},{8,0},{1,9},{9,1},{2,10},{10,2},{3,11},{11,3},{4,12},{12,4},... | collective-permute-start | bytes 589832 | tf_op jit(solution)/shard_map/ppermute | solution.py:242
  120.4 9.4 %collective-permute-start.20 = (bf16[128,768]{1,0:T(8,128)(2,1)}, bf16[128,768]{1,0:T(8,128)(2,1)}, u32[]{:S(2)}, u32[]{:S(2)}) collective-permute-start(bf16[128,768]{1,0:T(8,128)(2,1)} %get-tuple-element.125.refs_0_.refs_4_), channel_id=1, source_target_pairs={{0,24},{8,16},{16,8},{24,0},{1,25},{9,17},{17,9},{25,1},{2,26},{10... | collective-permute-start | bytes 589832 | tf_op jit(solution)/shard_map/ppermute | solution.py:246
  137.4 9.5 %collective-permute-start.21 = (bf16[128,768]{1,0:T(8,128)(2,1)}, bf16[128,768]{1,0:T(8,128)(2,1)S(1)}, u32[]{:S(2)}, u32[]{:S(2)}) collective-permute-start(bf16[128,768]{1,0:T(8,128)(2,1)} %get-tuple-element.129), channel_id=1, source_target_pairs={{0,16},{16,0},{1,17},{17,1},{2,18},{18,2},{3,19},{19,3},{4,20},{20... | collective-permute-start | bytes 589832 | tf_op jit(solution)/shard_map/ppermute | solution.py:242
  156.3 9.9 %collective-permute-start.25 = (bf16[128,192]{1,0:T(8,128)(2,1)S(1)}, bf16[128,192]{1,0:T(8,128)(2,1)S(1)}, u32[]{:S(2)}, u32[]{:S(2)}) collective-permute-start(bf16[128,192]{1,0:T(8,128)(2,1)S(1)} %copy-done.41), channel_id=1, source_target_pairs={{0,4},{1,5},{2,6},{3,7},{4,0},{5,1},{6,2},{7,3},{8,12},{9,13},{10,... | collective-permute-start | bytes 147464 | tf_op jit(solution)/shard_map/ppermute | solution.py:239
  157.2 9.0 %collective-permute-start.26 = (bf16[128,192]{1,0:T(8,128)(2,1)S(1)}, bf16[128,192]{1,0:T(8,128)(2,1)S(1)}, u32[]{:S(2)}, u32[]{:S(2)}) collective-permute-start(bf16[128,192]{1,0:T(8,128)(2,1)S(1)} %copy-done.40), channel_id=1, source_target_pairs={{0,6},{1,7},{2,0},{3,1},{4,2},{5,3},{6,4},{7,5},{8,14},{9,15},{10,... | collective-permute-start | bytes 147464 | tf_op jit(solution)/shard_map/ppermute | solution.py:239
  160.5 14.4 %collective-permute-start.28 = (bf16[4,64,768]{2,1,0:T(8,128)(2,1)S(1)}, bf16[4,64,768]{2,1,0:T(8,128)(2,1)S(1)}, u32[]{:S(2)}, u32[]{:S(2)}) collective-permute-start(bf16[4,64,768]{2,1,0:T(8,128)(2,1)S(1)} %fusion.7), channel_id=1, source_target_pairs={{0,8},{8,0},{1,9},{9,1},{2,10},{10,2},{3,11},{11,3},{4,12},{12,4},... | collective-permute-start | bytes 1179656 | tf_op jit(solution)/shard_map/ppermute | solution.py:242
  182.0 11.3 %collective-permute-start.30 = (bf16[2,4,64,576]{3,2,1,0:T(8,128)(2,1)}, bf16[2,4,64,576]{3,2,1,0:T(8,128)(2,1)S(1)}, u32[]{:S(2)}, u32[]{:S(2)}) collective-permute-start(bf16[2,4,64,576]{3,2,1,0:T(8,128)(2,1)} %get-tuple-element.159), channel_id=1, source_target_pairs={{0,1},{1,0},{2,3},{3,2},{4,5},{5,4},{6,7},{7,6},{8,9},{9,8},{10,11... | collective-permute-start | bytes 1769480 | tf_op jit(solution)/shard_map/ppermute | solution.py:279
  187.8 41.1 %all-to-all-start.1 = ((bf16[4,192,768]{2,1,0:T(8,128)(2,1)}), bf16[4,192,768]{2,1,0:T(8,128)(2,1)S(1)}, u32[]{:S(2)}, u32[]{:S(2)}) async-start(bf16[4,192,768]{2,1,0:T(8,128)(2,1)} %tokens_parts.1), calls=%async_computation.1 | async-start | bytes 2359296 | tf_op jit(solution)/shard_map/all_to_all | solution.py:1350
  193.3 9.9 %collective-permute-start.34 = (bf16[4,64,576]{2,1,0:T(8,128)(2,1)S(1)}, bf16[4,64,576]{2,1,0:T(8,128)(2,1)}, u32[]{:S(2)}, u32[]{:S(2)}) collective-permute-start(bf16[4,64,576]{2,1,0:T(8,128)(2,1)S(1)} %fusion.8), channel_id=1, source_target_pairs={{0,8},{8,0},{1,9},{9,1},{2,10},{10,2},{3,11},{11,3},{4,12},{12,4},... | collective-permute-start | bytes 884744 | tf_op jit(solution)/shard_map/ppermute | solution.py:242
  201.7 14.7 %collective-permute-start.31 = (bf16[48,3072]{1,0:T(8,128)(2,1)}, bf16[48,3072]{1,0:T(8,128)(2,1)}, u32[]{:S(2)}, u32[]{:S(2)}) collective-permute-start(bf16[48,3072]{1,0:T(8,128)(2,1)} %get-tuple-element.161.refs_0_), channel_id=1, source_target_pairs={{0,16},{16,0},{1,17},{17,1},{2,18},{18,2},{3,19},{19,3},{4,20},{20... | collective-permute-start | bytes 884744 | tf_op jit(solution)/shard_map/ppermute | solution.py:242
  204.3 12.1 %collective-permute-start.35 = (bf16[4,64,576]{2,1,0:T(8,128)(2,1)S(1)}, bf16[4,64,576]{2,1,0:T(8,128)(2,1)S(1)}, u32[]{:S(2)}, u32[]{:S(2)}) collective-permute-start(bf16[4,64,576]{2,1,0:T(8,128)(2,1)S(1)} %fusion.6.own_ref), channel_id=1, source_target_pairs={{0,16},{16,0},{1,17},{17,1},{2,18},{18,2},{3,19},{19,3},{4,20},{20... | collective-permute-start | bytes 884744 | tf_op jit(solution)/shard_map/ppermute | solution.py:242
  205.9 10.5 %collective-permute-start.33 = (bf16[48,1536]{1,0:T(8,128)(2,1)S(1)}, bf16[48,1536]{1,0:T(8,128)(2,1)S(1)}, u32[]{:S(2)}, u32[]{:S(2)}) collective-permute-start(bf16[48,1536]{1,0:T(8,128)(2,1)S(1)} %copy-done.36), channel_id=1, source_target_pairs={{0,24},{8,16},{16,8},{24,0},{1,25},{9,17},{17,9},{25,1},{2,26},{10... | collective-permute-start | bytes 442376 | tf_op jit(solution)/shard_map/ppermute | solution.py:246
  219.1 17.5 %collective-permute-start.36 = (bf16[64,576]{1,0:T(8,128)(2,1)}, bf16[64,576]{1,0:T(8,128)(2,1)S(1)}, u32[]{:S(2)}, u32[]{:S(2)}) collective-permute-start(bf16[64,576]{1,0:T(8,128)(2,1)} %get-tuple-element.169), channel_id=1, source_target_pairs={{0,2},{1,3},{2,4},{3,5},{4,6},{5,7},{6,0},{7,1},{8,10},{9,11},{10,... | collective-permute-start | bytes 221192 | tf_op jit(solution)/shard_map/ppermute | solution.py:239
  219.1 17.5 %collective-permute-start.37 = (bf16[64,576]{1,0:T(8,128)(2,1)}, bf16[64,576]{1,0:T(8,128)(2,1)S(1)}, u32[]{:S(2)}, u32[]{:S(2)}) collective-permute-start(bf16[64,576]{1,0:T(8,128)(2,1)} %get-tuple-element.170), channel_id=1, source_target_pairs={{0,4},{1,5},{2,6},{3,7},{4,0},{5,1},{6,2},{7,3},{8,12},{9,13},{10,... | collective-permute-start | bytes 221192 | tf_op jit(solution)/shard_map/ppermute | solution.py:239
  227.4 9.2 %collective-permute-start.38 = (bf16[64,576]{1,0:T(8,128)(2,1)}, bf16[64,576]{1,0:T(8,128)(2,1)S(1)}, u32[]{:S(2)}, u32[]{:S(2)}) collective-permute-start(bf16[64,576]{1,0:T(8,128)(2,1)} %get-tuple-element.171), channel_id=1, source_target_pairs={{0,6},{1,7},{2,0},{3,1},{4,2},{5,3},{6,4},{7,5},{8,14},{9,15},{10,... | collective-permute-start | bytes 221192 | tf_op jit(solution)/shard_map/ppermute | solution.py:239
  (67 other events, 319.4 us)
Sparse Core Ops, SparseCore 0:
  15.8 29.3 all-gather.2
  49.1 47.1 all-gather.4
  155.6 44.2 reduce-scatter.1

commit v5 on v4

--- a/solution.py
+++ b/solution.py
@@ -1111,57 +1111,53 @@
     cols = mixed_rel[0].shape[1]
 
     def body(ids_ref, *refs):
-        back_ref, fs_ref, ls_ref, gs_ref, us_ref, keep_ref, give_ref, full_ref = refs[GROUPS:]
+        back_ref, fs_ref, ls_ref, gs_ref, us_ref, keep_ref, give_ref, small_ref, full_ref = refs[GROUPS:]
         for k, ref in enumerate(refs[:GROUPS]):
             full_ref[piece_rows(ids_ref, k, cols, -1), :] = dot_tn(ref[...], back_ref[...])
         split_rows(ids_ref, full_ref, keep_ref, give_ref, kb)
         y, x = ids_ref[2], ids_ref[3]
         sums = jnp.concatenate([fs_ref[0:3, :], ls_ref[0:3, :]], axis=0)
         wide = (gs_ref[...], us_ref[...])
-        blocks = []
-        for row in range(2):
-            blocks.append([])
-            for g in range(GROUPS):
-                blocks[-1].append([])
-                for member in range(2):
-                    b = row * 8 + g * 2 + member
-                    lines = []
-                    for i in range(8):
-                        at = ((b % 4) * 4 + (i // 4) * 2 + i % 2) * kb
-                        mine = (y == (b % 8) // 4) & (x == (i % 4) // 2)
-                        lines.append(jnp.where(mine, wide[b // 8][:, at : at + kb], 0.0))
-                    lines = [sums[:, b * kb : (b + 1) * kb]] + lines + [jnp.zeros((2, kb), F32)]
-                    blocks[-1][-1].append(jnp.concatenate(lines, axis=0))
-        place_small(ids_ref, blocks, keep_ref, give_ref, kb)
-
-    shape = (2, GROUPS, kb + 16, width)
+        for owner in range(16):
+            lines = []
+            for i in range(8):
+                at = ((owner % 4) * 4 + (i // 4) * 2 + i % 2) * kb
+                mine = (y == (owner % 8) // 4) & (x == (i % 4) // 2)
+                lines.append(jnp.where(mine, wide[owner // 8][:, at : at + kb], 0.0))
+            lines = [sums[:, owner * kb : (owner + 1) * kb]] + lines + [jnp.zeros((2, kb), F32)]
+            small_ref[owner] = jnp.concatenate(lines, axis=0)
+
+    shape = (2, GROUPS, kb, width)
     return call(
         body,
         "output_grads",
         [ids] + list(mixed_rel) + [back, first_sums, final_sums, gate_sum, up_sum],
-        [(shape, F32), (shape, BF)],
+        [(shape, F32), (shape, BF), ((16, 16, kb), F32)],
         scratch=[pltpu.VMEM((width, width), F32)],
         flops=2 * rows * width * width,
     )
 
 
-def tokens_parts(ids, back, weight, low):
+def tokens_parts(ids, back, weight, keep, got, far):
     count, cols = back.shape
     rows = count // GROUPS
     width = weight.shape[0]
-    more = low.shape[1]
-
-    def body(jb_ref, w_ref, low_ref, out_ref):
+    more = far.shape[1]
+    first = pl.BlockSpec((1, GROUPS, more, width), lambda i: (0, 0, 0, 0))
+
+    def body(jb_ref, w_ref, keep_ref, got_ref, far_ref, out_ref):
         for g in range(GROUPS):
             part = dot_nt(jb_ref[g * rows : (g + 1) * rows, :], w_ref[...])
             out_ref[g, :rows, :] = part.astype(BF)
-            out_ref[g, rows:, :] = low_ref[g]
+            low = keep_ref[0, g] + got_ref[0, g].astype(F32) + far_ref[g].astype(F32)
+            out_ref[g, rows:, :] = low.astype(BF)
 
     return call(
         body,
         "tokens_parts",
-        [back, weight, low],
+        [back, weight, keep, got, far],
         [((GROUPS, rows + more, width), BF)],
+        in_specs=[vmem(back.shape), vmem(weight.shape), first, first, vmem(far.shape)],
         flops=2 * count * width * cols,
     )[0]
 
@@ -1187,19 +1183,19 @@
     )
 
 
-def joined_grads(ids, x_four, query_back, keep, got, kb):
+def joined_grads(ids, x_four, query_back, keep, got, small, kb):
     count, width = x_four.shape
     cols = query_back.shape[1]
     wide = 3 * cols
 
-    def body(ids_ref, x_ref, q_ref, kv_ref, got_ref, keep_ref, give_ref, back_ref, full_ref):
+    def body(ids_ref, x_ref, q_ref, kv_ref, got_ref, small_ref, keep_ref, give_ref, back_ref, full_ref):
         back_ref[:, :cols] = q_ref[...]
         back_ref[:, cols:] = (kv_ref[...] + got_ref[...].astype(F32)).astype(BF)
         full_ref[...] = dot_tn(x_ref[...], back_ref[...])
         split_rows(ids_ref, full_ref, keep_ref, give_ref, kb)
         g_own = ids_ref[0]
         sums = jnp.sum(back_ref[...].astype(F32), axis=0, keepdims=True)
-        pair = jnp.concatenate([sums[:, :cols], sums[:, 2 * cols :], jnp.zeros((14, cols), F32)], axis=0)
+        pair = jnp.concatenate([jnp.zeros((14, cols), F32), sums[:, :cols], sums[:, 2 * cols :]], axis=0)
         blocks = []
         for row in range(2):
             blocks.append([])
@@ -1208,14 +1204,14 @@
                 for member in range(2):
                     b = row * 8 + g * 2 + member
                     part = pair[:, (b % GROUPS) * kb : (b % GROUPS + 1) * kb]
-                    blocks[-1][-1].append(jnp.where(g_own == b // GROUPS, part, 0.0))
+                    blocks[-1][-1].append(small_ref[b] + jnp.where(g_own == b // GROUPS, part, 0.0))
         place_small(ids_ref, blocks, keep_ref, give_ref, kb)
 
     shape = (2, GROUPS, kb + 16, wide)
     return call(
         body,
         "joined_grads",
-        [ids, x_four, query_back, keep, got],
+        [ids, x_four, query_back, keep, got, small],
         [(shape, F32), (shape, BF), ((count, wide), BF)],
         scratch=[pltpu.VMEM((width, wide), F32)],
         flops=2 * count * width * wide,
@@ -1433,7 +1429,7 @@
     back_send = turned[3:]
     back_near = [back_send[0]] + [at.shift(back_send[k], k) for k in range(1, GROUPS)]
 
-    output_keep, output_give = output_grads(
+    output_keep, output_give, small = output_grads(
         ids, mixed_rel, output_back, first_sums, final_sums, gate_sum, up_sum, kb
     )
 
@@ -1445,14 +1441,12 @@
     query_back, kv_keep, kv_give = attend_back(
         ids, slopes, queries, back_near, mixed_near, inv, kv_own, kv_other, q_row, k_col, scale
     )
-    output_far = at.swap(seq_send(output_keep[1], output_got[1]), "seq")
-    kv_give, output_far = lax.optimization_barrier((kv_give, output_far))
+    output_far = at.swap(seq_send(output_keep[1], after(output_got, query_back)[1]), "seq")
     kv_got = at.partner(kv_give)
 
-    output_sum = (output_keep[0] + output_got[0].astype(F32) + output_far.astype(F32)).astype(BF)
-    joined_keep, joined_give, joined_back = joined_grads(ids, x_four, query_back, kv_keep, kv_got, kb)
+    joined_keep, joined_give, joined_back = joined_grads(ids, x_four, query_back, kv_keep, kv_got, small, kb)
     joined_got = at.partner(joined_give)
-    parts = tokens_parts(ids, joined_back, w_joined, output_sum)
+    parts = tokens_parts(ids, joined_back, w_joined, output_keep, output_got, output_far)
     tokens_got = across(parts)
     joined_far = at.swap(seq_send(joined_keep[1], after(joined_got, parts)[1]), "seq")
     joined_sum = (joined_keep[0] + joined_got[0].astype(F32) + joined_far.astype(F32)).astype(BF)
@@ -1468,14 +1462,14 @@
     )
     tokens_grad, output_mine = finish_tokens(tokens_got, after(attn_back, joined_mine[0]))
     output_total = output_mine.astype(F32) + at.swap(output_mine, "rep").astype(F32)
-    last = output_total[kb:, :kb]
+    last = pair[:, :kb]
     return (
         result[None],
         tokens_grad[None],
         joined_total,
-        pair[0, :kb],
-        pair[1, :kb],
-        output_total[:kb],
+        last[14],
+        last[15],
+        output_total,
         last[0],
         last[1],
         last[2],

time: 251 us -> 242 us (0.964)
  starting transfers between devices: 58.9 us -> 54.9 us
  waiting for transfers between devices: 71.1 us -> 67.1 us
    reduce_scatter x1, waiting for transfers between devices: 5.74 us -> 0.55 us  [fast_device(): wide_sum = lax.psum_scatter(wide_grad, 'ctx', tiled=True)]
    ppermute x17, waiting for transfers between devices: 32.7 us -> 37.2 us  [swap(): return lax.ppermute(value, axis, [(0, 1), (1, 0)])]
    ppermute x12, starting transfers between devices: 23.4 us -> 18.8 us  [shift(): lax.ppermute(value, 'ctx', [(i, (i + steps * r) % n) for i in range(n)])]
    unnamed x93 -> x89, local copies, waits for them, and re-layouts: 11.2 us -> 11 us
  transfers between devices with their start and end apart: 45 -> 45, of which waited for: 23 -> 25; matrix products, arithmetic and copies ran while one was open for 5% -> 6% of each run, Pallas kernels for 22% -> 26%
where the time goes in v5:
time: 242 us; the launch traced here: 241 us
  Pallas kernels  77.1 us (32%)
  waiting for transfers between devices  67.1 us (28%)
  starting transfers between devices  54.9 us (23%)
  local copies, waits for them, and re-layouts  18.8 us (8%)
  between operations  14.1 us (6%)
  other arithmetic  8.69 us (4%)
    pallas_call x22, Pallas kernels, call(): pl.pallas_call(body, grid=grid, in_specs=in_specs, out_specs=out_specs, o...  77.1 us
    ppermute x17, waiting for transfers between devices, swap(): return lax.ppermute(value, axis, [(0, 1), (1, 0)])  37.2 us
    ppermute x17, starting transfers between devices, swap(): return lax.ppermute(value, axis, [(0, 1), (1, 0)])  21.1 us
    ppermute x12, starting transfers between devices, shift(): lax.ppermute(value, 'ctx', [(i, (i + steps * r) % n) for i in range(n)])  18.8 us
    ppermute x12, waiting for transfers between devices, shift(): lax.ppermute(value, 'ctx', [(i, (i + steps * r) % n) for i in range(n)])  13.8 us
    unnamed x89, local copies, waits for them, and re-layouts  11 us
    all_to_all x2, starting transfers between devices, across(): lax.all_to_all(value, 'ctx', 0, 0, axis_index_groups=columns, tiled=True)  9.35 us
    ppermute x5, waiting for transfers between devices, plane(): return lax.ppermute(value, ('rep', 'seq'), [(i, 3 - i) for i in range(4)])  5.71 us
  transfers between devices with their start and end apart: 45, of which 25 were waited for; matrix products, arithmetic and copies ran while one was open for 6% of the time, Pallas kernels for 26%

profile of v5, /device:TPU:0, one launch (start us, length us, event | category | flops | bytes accessed | tf_op | source)
XLA Modules:
  0.0 240.6 jit_solution(12962817916291530149)
XLA Ops:
  7.2 3.1 %collective-permute-start.10 = (bf16[48,768]{1,0:T(8,128)(2,1)}, bf16[48,768]{1,0:T(8,128)(2,1)S(1)}, u32[]{:S(2)}, u32[]{:S(2)}) collective-permute-start(bf16[48,768]{1,0:T(8,128)(2,1)} %param.21), channel_id=1, source_target_pairs={{0,8},{8,0},{1,9},{9,1},{2,10},{10,2},{3,11},{11,3},{4,12},{12,4},... | collective-permute-start | bytes 221192 | tf_op jit(solution)/shard_map/ppermute | solution.py:242
  27.6 5.0 %all-to-all-start = ((bf16[4,128,768]{2,1,0:T(8,128)(2,1)}), bf16[4,128,768]{2,1,0:T(8,128)(2,1)S(1)}, u32[]{:S(2)}, u32[]{:S(2)}) async-start(bf16[4,128,768]{2,1,0:T(8,128)(2,1)} %broadcast_in_dim.52), calls=%async_computation | async-start | bytes 1572864 | tf_op jit(solution)/shard_map/all_to_all | solution.py:1346
  35.0 5.0 %collective-permute-done.3.b_ref = bf16[4,64,576]{2,1,0:T(8,128)(2,1)S(1)} collective-permute-done((bf16[4,64,576]{2,1,0:T(8,128)(2,1)S(1)}, bf16[4,64,576]{2,1,0:T(8,128)(2,1)S(1)}, u32[]{:S(2)}, u32[]{:S(2)}) %collective-permute-start.3) | collective-permute-done | bytes 294944 | tf_op jit(solution)/shard_map/ppermute | solution.py:242
  50.5 3.9 %all-to-all-done = bf16[4,128,768]{2,1,0:T(8,128)(2,1)S(1)} async-done(((bf16[4,128,768]{2,1,0:T(8,128)(2,1)}), bf16[4,128,768]{2,1,0:T(8,128)(2,1)S(1)}, u32[]{:S(2)}, u32[]{:S(2)}) %all-to-all-start) | async-done | bytes 786464 | tf_op jit(solution)/shard_map/all_to_all | solution.py:1346
  55.3 3.1 %split_joined.1 = (bf16[512,192]{1,0:T(8,128)(2,1)}, bf16[512,384]{1,0:T(8,128)(2,1)}) custom-call(bf16[512,768]{1,0:T(8,128)(2,1)} %bitcast.58, bf16[768,576]{1,0:T(8,128)(2,1)} %get-tuple-element.101.w_ref, f32[16,192]{1,0:T(8,128)} %get-tuple-element.102.near_ref), custom_call_target="tpu_custom_call" | custom-call | flops 15000000512 | tf_op jit(solution)/shard_map/split_joined/pallas_call | solution.py:604
  61.1 4.7 %attend.1 = (f32[512,192]{1,0:T(8,128)}, f32[3,8,512]{2,1,0:T(8,128)}, bf16[128,192]{1,0:T(8,128)(2,1)}, bf16[128,192]{1,0:T(8,128)(2,1)}, bf16[128,192]{1,0:T(8,128)(2,1)}, /*index=5*/bf16[128,192]{1,0:T(8,128)(2,1)}) custom-call(s32[4]{0:T(128)} %pad_add_fusion.refs_0_.ids_ref, f32[3]{0:T(128)} %power_multiply_fusion.slope_ref, ...), custom_call_target="tpu_custom_call" | custom-call | flops 24999999488 | tf_op jit(solution)/shard_map/attend/pallas_call | solution.py:604
  74.2 4.3 %collective-permute-done.8.c_ref.refs_2_ = bf16[128,192]{1,0:T(8,128)(2,1)S(1)} collective-permute-done((bf16[128,192]{1,0:T(8,128)(2,1)}, bf16[128,192]{1,0:T(8,128)(2,1)S(1)}, u32[]{:S(2)}, u32[]{:S(2)}) %collective-permute-start.8) | collective-permute-done | bytes 49184 | tf_op jit(solution)/shard_map/ppermute | solution.py:239
  85.5 4.5 %collective-permute-done.11.refs_1_ = bf16[128,768]{1,0:T(8,128)(2,1)S(1)} collective-permute-done((bf16[128,768]{1,0:T(8,128)(2,1)}, bf16[128,768]{1,0:T(8,128)(2,1)S(1)}, u32[]{:S(2)}, u32[]{:S(2)}) %collective-permute-start.11) | collective-permute-done | bytes 196640 | tf_op jit(solution)/shard_map/ppermute | solution.py:242
  90.0 3.7 %collective-permute-done.12.refs_2_ = bf16[128,768]{1,0:T(8,128)(2,1)S(1)} collective-permute-done((bf16[128,768]{1,0:T(8,128)(2,1)}, bf16[128,768]{1,0:T(8,128)(2,1)S(1)}, u32[]{:S(2)}, u32[]{:S(2)}) %collective-permute-start.12) | collective-permute-done | bytes 196640 | tf_op jit(solution)/shard_map/ppermute | solution.py:242
  96.4 5.7 %widen_narrow.1 = (f32[128,768]{1,0:T(8,128)}, bf16[128,768]{1,0:T(8,128)(2,1)}, bf16[128,768]{1,0:T(8,128)(2,1)}, bf16[128,768]{1,0:T(8,128)(2,1)}, bf16[512,76...) custom-call(bf16[128,768]{1,0:T(8,128)(2,1)} %get-tuple-element.111.refs_0_, bf16[128,768]{1,0:T(8,128)(2,1)} %copy-done.26, ...), custom_call_target="tpu_custom_call" | custom-call | flops 30000001024 | tf_op jit(solution)/shard_map/widen_narrow/pallas_call | solution.py:604
  106.7 3.4 %collective-permute-done.15.a_ref = bf16[128,768]{1,0:T(8,128)(2,1)S(1)} collective-permute-done((bf16[128,768]{1,0:T(8,128)(2,1)}, bf16[128,768]{1,0:T(8,128)(2,1)S(1)}, u32[]{:S(2)}, u32[]{:S(2)}) %collective-permute-start.15) | collective-permute-done | bytes 196640 | tf_op jit(solution)/shard_map/ppermute | solution.py:242
  110.1 4.7 %collective-permute-done.16.b_ref = bf16[128,768]{1,0:T(8,128)(2,1)S(1)} collective-permute-done((bf16[128,768]{1,0:T(8,128)(2,1)}, bf16[128,768]{1,0:T(8,128)(2,1)S(1)}, u32[]{:S(2)}, u32[]{:S(2)}) %collective-permute-start.16) | collective-permute-done | bytes 196640 | tf_op jit(solution)/shard_map/ppermute | solution.py:242
  126.4 3.5 %collective-permute-done.19.refs_2_.refs_6_ = bf16[128,768]{1,0:T(8,128)(2,1)S(1)} collective-permute-done((bf16[128,768]{1,0:T(8,128)(2,1)}, bf16[128,768]{1,0:T(8,128)(2,1)S(1)}, u32[]{:S(2)}, u32[]{:S(2)}) %collective-permute-start.19) | collective-permute-done | bytes 196640 | tf_op jit(solution)/shard_map/ppermute | solution.py:242
  130.5 6.9 %widen_narrow_back.1 = (f32[128,768]{1,0:T(8,128)}, bf16[128,768]{1,0:T(8,128)(2,1)}, bf16[128,768]{1,0:T(8,128)(2,1)}, bf16[128,768]{1,0:T(8,128)(2,1)}, bf16[5...) custom-call(bf16[128,768]{1,0:T(8,128)(2,1)} %get-tuple-element.125.refs_0_.refs_4_, bf16[128,768]{1,0:T(8,128)(2,1)} %copy-done.31, ...), custom_call_target="tpu_custom_call" | custom-call | flops 35000000512 | tf_op jit(solution)/shard_map/widen_narrow_back/pallas_call | solution.py:604
  140.9 6.0 %wide_grads.1 = (bf16[768,2304]{1,0:T(8,128)(2,1)}, f32[1,768]{1,0:T(1,128)}, f32[1,768]{1,0:T(1,128)}) custom-call(bf16[128,768]{1,0:T(8,128)(2,1)} %get-tuple-element.111.refs_0_, bf16[128,768]{1,0:T(8,128)(2,1)} %copy-done.26, bf16[128,768]{1,0:T(8,128)(2,1)} %copy-done.27, bf16[128,768]{1,0:T(8,128)(2,1)} %copy-done.28, ...), custom_call_target="tpu_custom_call" | custom-call | flops 30000001024 | tf_op jit(solution)/shard_map/wide_grads/pallas_call | solution.py:604
  147.8 3.4 %turn_first.1 = (f32[128,768]{1,0:T(8,128)}, bf16[128,768]{1,0:T(8,128)(2,1)}, f32[8,768]{1,0:T(8,128)}, bf16[128,192]{1,0:T(8,128)(2,1)}, bf16[128,192]{1,0:T(8...) custom-call(s32[4]{0:T(128)} %pad_add_fusion.refs_0_.ids_ref, f32[128,768]{1,0:T(8,128)} %get-tuple-element.128.own_ref, ...), custom_call_target="tpu_custom_call" | custom-call | flops 15000000512 | tf_op jit(solution)/shard_map/turn_first/pallas_call | solution.py:604
  155.0 3.1 %output_grads.1 = (f32[2,4,48,768]{3,2,1,0:T(8,128)}, bf16[2,4,48,768]{3,2,1,0:T(8,128)(2,1)}, f32[16,16,48]{2,1,0:T(8,128)}) custom-call(s32[4]{0:T(128)} %pad_add_fusion.refs_0_.ids_ref, bf16[128,192]{1,0:T(8,128)(2,1)} %get-tuple-element.105.a_ref.refs_0_, bf16[128,192]{1,0:T(8,128)(2,1)} %copy-done.38, bf16[128,192]{1,0:T(8,128)(2,1)} %copy-done.39, ...), custom_call_target="tpu_custom_call" | custom-call | flops 15000000512 | tf_op jit(solution)/shard_map/output_grads/pallas_call | solution.py:604
  161.6 8.1 %attend_back.1 = (bf16[512,192]{1,0:T(8,128)(2,1)}, f32[512,384]{1,0:T(8,128)}, bf16[512,384]{1,0:T(8,128)(2,1)}) custom-call(s32[4]{0:T(128)} %pad_add_fusion.refs_0_.ids_ref, f32[3]{0:T(128)} %power_multiply_fusion.slope_ref, bf16[512,192]{1,0:T(8,128)(2,1)} %get-tuple-element.103.q_ref, bf16[128,192]{1,0:T(8,128)(2,1)} %get-tuple-element.135.refs_0_, ...), custom_call_target="tpu_custom_call" | custom-call | flops 40000000000 | tf_op jit(solution)/shard_map/attend_back/pallas_call | solution.py:604
  172.4 4.4 %joined_grads.1 = (f32[2,4,64,576]{3,2,1,0:T(8,128)}, bf16[2,4,64,576]{3,2,1,0:T(8,128)(2,1)}, bf16[512,576]{1,0:T(8,128)(2,1)}) custom-call(s32[4]{0:T(128)} %pad_add_fusion.refs_0_.ids_ref, bf16[512,768]{1,0:T(8,128)(2,1)} %bitcast.59, bf16[512,192]{1,0:T(8,128)(2,1)} %get-tuple-element.141.q_ref, f32[512,384]{1,0:T(8,128)} %get-tuple-element.142.kv_ref, ...), custom_call_target="tpu_custom_call" | custom-call | flops 20000000000 | tf_op jit(solution)/shard_map/joined_grads/pallas_call | solution.py:604
  179.9 4.1 %tokens_parts.1 = bf16[4,176,768]{2,1,0:T(8,128)(2,1)} custom-call(bf16[512,576]{1,0:T(8,128)(2,1)} %get-tuple-element.153.jb_ref, bf16[768,576]{1,0:T(8,128)(2,1)} %get-tuple-element.101.w_ref, f32[2,4,48,768]{3,2,1,0:T(8,128)} %get-tuple-element.154.keep_ref, bf16[2,4,48,768]{3,2,1,0:T(8,128)(2,1)} %copy-done.4, bf16[4,48,768]{2,1,0:T(8,128)(2,1)} %copy-done.13), custom_call_target="tpu_custom_call" | custom-call | tf_op jit(solution)/shard_map/tokens_parts/pallas_call | solution.py:604
  184.0 4.4 %all-to-all-start.1 = ((bf16[4,176,768]{2,1,0:T(8,128)(2,1)}), bf16[4,176,768]{2,1,0:T(8,128)(2,1)S(1)}, u32[]{:S(2)}, u32[]{:S(2)}) async-start(bf16[4,176,768]{2,1,0:T(8,128)(2,1)} %tokens_parts.1), calls=%async_computation.1 | async-start | bytes 2162688 | tf_op jit(solution)/shard_map/all_to_all | solution.py:1346
  193.6 4.1 %collective-permute-done.34 = bf16[4,64,576]{2,1,0:T(8,128)(2,1)} collective-permute-done((bf16[4,64,576]{2,1,0:T(8,128)(2,1)S(1)}, bf16[4,64,576]{2,1,0:T(8,128)(2,1)}, u32[]{:S(2)}, u32[]{:S(2)}) %collective-permute-start.34) | collective-permute-done | bytes 294944 | tf_op jit(solution)/shard_map/ppermute | solution.py:242
  205.0 5.7 %collective-permute-done.33.refs_3_ = bf16[48,1536]{1,0:T(8,128)(2,1)S(1)} collective-permute-done((bf16[48,1536]{1,0:T(8,128)(2,1)S(1)}, bf16[48,1536]{1,0:T(8,128)(2,1)S(1)}, u32[]{:S(2)}, u32[]{:S(2)}) %collective-permute-start.33) | collective-permute-done | bytes 147488 | tf_op jit(solution)/shard_map/ppermute | solution.py:246
  223.6 3.0 %finish_widen.1 = (f32[48,6144]{1,0:T(8,128)}, f32[192,768]{1,0:T(8,128)}) custom-call(s32[4]{0:T(128)} %pad_add_fusion.refs_0_.ids_ref, bf16[48,3072]{1,0:T(8,128)(2,1)} %get-tuple-element.161.refs_0_, bf16[48,3072]{1,0:T(8,128)(2,1)} %collective-permute-done.31.refs_1_, bf16[48,1536]{1,0:T(8,128)(2,1)} %copy-done.14, bf16[48,1536]{1,0:T(8,128)(2,1)} %copy-done.15), custom_call_target="tpu_custom_call" | custom-call | tf_op jit(solution)/shard_map/finish_widen/pallas_call | solution.py:604
  (205 shorter events, 118.9 us)
Async XLA Ops:
  7.2 62.4 %all-gather.3.cloned.1.call-start = ((), (), s32[]{:S(2)}) async-start(), calls=%async_computation.3 | async-start | bytes 1327104 | tf_op jit(solution)/shard_map/all_gather | solution.py:1374
  27.6 26.9 %all-to-all-start = ((bf16[4,128,768]{2,1,0:T(8,128)(2,1)}), bf16[4,128,768]{2,1,0:T(8,128)(2,1)S(1)}, u32[]{:S(2)}, u32[]{:S(2)}) async-start(bf16[4,128,768]{2,1,0:T(8,128)(2,1)} %broadcast_in_dim.52), calls=%async_computation | async-start | bytes 1572864 | tf_op jit(solution)/shard_map/all_to_all | solution.py:1346
  32.5 63.8 %all-gather.5.cloned.1.call-start = ((), (), s32[]{:S(2)}) async-start(), calls=%async_computation.4 | async-start | bytes 3981312 | tf_op jit(solution)/shard_map/all_gather | solution.py:1384
  49.0 141.1 %reduce-scatter.2.cloned.1.call-start = ((), (), s32[]{:S(2)}) async-start(), calls=%async_computation.5 | async-start | bytes 3981312 | tf_op jit(solution)/shard_map/reduce_scatter | solution.py:1426
  65.8 12.6 %collective-permute-start.8 = (bf16[128,192]{1,0:T(8,128)(2,1)}, bf16[128,192]{1,0:T(8,128)(2,1)S(1)}, u32[]{:S(2)}, u32[]{:S(2)}) collective-permute-start(bf16[128,192]{1,0:T(8,128)(2,1)} %get-tuple-element.107), channel_id=1, source_target_pairs={{0,4},{1,5},{2,6},{3,7},{4,0},{5,1},{6,2},{7,3},{8,12},{9,13},{10,... | collective-permute-start | bytes 147464 | tf_op jit(solution)/shard_map/ppermute | solution.py:239
  68.3 10.1 %collective-permute-start.9 = (bf16[128,192]{1,0:T(8,128)(2,1)}, bf16[128,192]{1,0:T(8,128)(2,1)S(1)}, u32[]{:S(2)}, u32[]{:S(2)}) collective-permute-start(bf16[128,192]{1,0:T(8,128)(2,1)} %get-tuple-element.108), channel_id=1, source_target_pairs={{0,6},{1,7},{2,0},{3,1},{4,2},{5,3},{6,4},{7,5},{8,14},{9,15},{10,... | collective-permute-start | bytes 147464 | tf_op jit(solution)/shard_map/ppermute | solution.py:239
  83.5 10.3 %collective-permute-start.12 = (bf16[128,768]{1,0:T(8,128)(2,1)}, bf16[128,768]{1,0:T(8,128)(2,1)S(1)}, u32[]{:S(2)}, u32[]{:S(2)}) collective-permute-start(bf16[128,768]{1,0:T(8,128)(2,1)} %get-tuple-element.111.refs_0_), channel_id=1, source_target_pairs={{0,8},{8,0},{1,9},{9,1},{2,10},{10,2},{3,11},{11,3},{4,12},{12,4},... | collective-permute-start | bytes 589832 | tf_op jit(solution)/shard_map/ppermute | solution.py:242
  103.6 11.2 %collective-permute-start.16 = (bf16[128,768]{1,0:T(8,128)(2,1)}, bf16[128,768]{1,0:T(8,128)(2,1)S(1)}, u32[]{:S(2)}, u32[]{:S(2)}) collective-permute-start(bf16[128,768]{1,0:T(8,128)(2,1)} %get-tuple-element.121), channel_id=1, source_target_pairs={{0,8},{8,0},{1,9},{9,1},{2,10},{10,2},{3,11},{11,3},{4,12},{12,4},... | collective-permute-start | bytes 589832 | tf_op jit(solution)/shard_map/ppermute | solution.py:242
  105.1 9.7 %collective-permute-start.17 = (bf16[128,768]{1,0:T(8,128)(2,1)}, bf16[128,768]{1,0:T(8,128)(2,1)S(1)}, u32[]{:S(2)}, u32[]{:S(2)}) collective-permute-start(bf16[128,768]{1,0:T(8,128)(2,1)} %get-tuple-element.122), channel_id=1, source_target_pairs={{0,24},{8,16},{16,8},{24,0},{1,25},{9,17},{17,9},{25,1},{2,26},{10... | collective-permute-start | bytes 589832 | tf_op jit(solution)/shard_map/ppermute | solution.py:246
  119.5 10.3 %collective-permute-start.19 = (bf16[128,768]{1,0:T(8,128)(2,1)}, bf16[128,768]{1,0:T(8,128)(2,1)S(1)}, u32[]{:S(2)}, u32[]{:S(2)}) collective-permute-start(bf16[128,768]{1,0:T(8,128)(2,1)} %get-tuple-element.125.refs_0_.refs_4_), channel_id=1, source_target_pairs={{0,8},{8,0},{1,9},{9,1},{2,10},{10,2},{3,11},{11,3},{4,12},{12,4},... | collective-permute-start | bytes 589832 | tf_op jit(solution)/shard_map/ppermute | solution.py:242
  120.4 9.4 %collective-permute-start.20 = (bf16[128,768]{1,0:T(8,128)(2,1)}, bf16[128,768]{1,0:T(8,128)(2,1)}, u32[]{:S(2)}, u32[]{:S(2)}) collective-permute-start(bf16[128,768]{1,0:T(8,128)(2,1)} %get-tuple-element.125.refs_0_.refs_4_), channel_id=1, source_target_pairs={{0,24},{8,16},{16,8},{24,0},{1,25},{9,17},{17,9},{25,1},{2,26},{10... | collective-permute-start | bytes 589832 | tf_op jit(solution)/shard_map/ppermute | solution.py:246
  137.4 9.6 %collective-permute-start.21 = (bf16[128,768]{1,0:T(8,128)(2,1)}, bf16[128,768]{1,0:T(8,128)(2,1)S(1)}, u32[]{:S(2)}, u32[]{:S(2)}) collective-permute-start(bf16[128,768]{1,0:T(8,128)(2,1)} %get-tuple-element.129), channel_id=1, source_target_pairs={{0,16},{16,0},{1,17},{17,1},{2,18},{18,2},{3,19},{19,3},{4,20},{20... | collective-permute-start | bytes 589832 | tf_op jit(solution)/shard_map/ppermute | solution.py:242
  158.1 11.6 %collective-permute-start.28 = (bf16[2,4,48,768]{3,2,1,0:T(8,128)(2,1)}, bf16[2,4,48,768]{3,2,1,0:T(8,128)(2,1)S(1)}, u32[]{:S(2)}, u32[]{:S(2)}) collective-permute-start(bf16[2,4,48,768]{3,2,1,0:T(8,128)(2,1)} %get-tuple-element.155), channel_id=1, source_target_pairs={{0,1},{1,0},{2,3},{3,2},{4,5},{5,4},{6,7},{7,6},{8,9},{9,8},{10,11... | collective-permute-start | bytes 1769480 | tf_op jit(solution)/shard_map/ppermute | solution.py:279
  169.7 9.5 %collective-permute-start.29 = (bf16[4,48,768]{2,1,0:T(8,128)(2,1)S(1)}, bf16[4,48,768]{2,1,0:T(8,128)(2,1)S(1)}, u32[]{:S(2)}, u32[]{:S(2)}) collective-permute-start(bf16[4,48,768]{2,1,0:T(8,128)(2,1)S(1)} %fusion.7), channel_id=1, source_target_pairs={{0,8},{8,0},{1,9},{9,1},{2,10},{10,2},{3,11},{11,3},{4,12},{12,4},... | collective-permute-start | bytes 884744 | tf_op jit(solution)/shard_map/ppermute | solution.py:242
  176.8 11.6 %collective-permute-start.30 = (bf16[2,4,64,576]{3,2,1,0:T(8,128)(2,1)}, bf16[2,4,64,576]{3,2,1,0:T(8,128)(2,1)S(1)}, u32[]{:S(2)}, u32[]{:S(2)}) collective-permute-start(bf16[2,4,64,576]{3,2,1,0:T(8,128)(2,1)} %get-tuple-element.159), channel_id=1, source_target_pairs={{0,1},{1,0},{2,3},{3,2},{4,5},{5,4},{6,7},{7,6},{8,9},{9,8},{10,11... | collective-permute-start | bytes 1769480 | tf_op jit(solution)/shard_map/ppermute | solution.py:279
  184.0 34.9 %all-to-all-start.1 = ((bf16[4,176,768]{2,1,0:T(8,128)(2,1)}), bf16[4,176,768]{2,1,0:T(8,128)(2,1)S(1)}, u32[]{:S(2)}, u32[]{:S(2)}) async-start(bf16[4,176,768]{2,1,0:T(8,128)(2,1)} %tokens_parts.1), calls=%async_computation.1 | async-start | bytes 2162688 | tf_op jit(solution)/shard_map/all_to_all | solution.py:1346
  188.5 9.2 %collective-permute-start.34 = (bf16[4,64,576]{2,1,0:T(8,128)(2,1)S(1)}, bf16[4,64,576]{2,1,0:T(8,128)(2,1)}, u32[]{:S(2)}, u32[]{:S(2)}) collective-permute-start(bf16[4,64,576]{2,1,0:T(8,128)(2,1)S(1)} %fusion.6), channel_id=1, source_target_pairs={{0,8},{8,0},{1,9},{9,1},{2,10},{10,2},{3,11},{11,3},{4,12},{12,4},... | collective-permute-start | bytes 884744 | tf_op jit(solution)/shard_map/ppermute | solution.py:242
  191.9 18.8 %collective-permute-start.31 = (bf16[48,3072]{1,0:T(8,128)(2,1)}, bf16[48,3072]{1,0:T(8,128)(2,1)}, u32[]{:S(2)}, u32[]{:S(2)}) collective-permute-start(bf16[48,3072]{1,0:T(8,128)(2,1)} %get-tuple-element.161.refs_0_), channel_id=1, source_target_pairs={{0,16},{16,0},{1,17},{17,1},{2,18},{18,2},{3,19},{19,3},{4,20},{20... | collective-permute-start | bytes 884744 | tf_op jit(solution)/shard_map/ppermute | solution.py:242
  198.8 11.9 %collective-permute-start.35 = (bf16[4,64,576]{2,1,0:T(8,128)(2,1)S(1)}, bf16[4,64,576]{2,1,0:T(8,128)(2,1)S(1)}, u32[]{:S(2)}, u32[]{:S(2)}) collective-permute-start(bf16[4,64,576]{2,1,0:T(8,128)(2,1)S(1)} %fusion.5.own_ref), channel_id=1, source_target_pairs={{0,16},{16,0},{1,17},{17,1},{2,18},{18,2},{3,19},{19,3},{4,20},{20... | collective-permute-start | bytes 884744 | tf_op jit(solution)/shard_map/ppermute | solution.py:242
  201.0 9.7 %collective-permute-start.33 = (bf16[48,1536]{1,0:T(8,128)(2,1)S(1)}, bf16[48,1536]{1,0:T(8,128)(2,1)S(1)}, u32[]{:S(2)}, u32[]{:S(2)}) collective-permute-start(bf16[48,1536]{1,0:T(8,128)(2,1)S(1)} %copy-done.37), channel_id=1, source_target_pairs={{0,24},{8,16},{16,8},{24,0},{1,25},{9,17},{17,9},{25,1},{2,26},{10... | collective-permute-start | bytes 442376 | tf_op jit(solution)/shard_map/ppermute | solution.py:246
  213.3 13.3 %collective-permute-start.36 = (bf16[64,576]{1,0:T(8,128)(2,1)}, bf16[64,576]{1,0:T(8,128)(2,1)S(1)}, u32[]{:S(2)}, u32[]{:S(2)}) collective-permute-start(bf16[64,576]{1,0:T(8,128)(2,1)} %get-tuple-element.169), channel_id=1, source_target_pairs={{0,2},{1,3},{2,4},{3,5},{4,6},{5,7},{6,0},{7,1},{8,10},{9,11},{10,... | collective-permute-start | bytes 221192 | tf_op jit(solution)/shard_map/ppermute | solution.py:239
  215.9 10.6 %collective-permute-start.37 = (bf16[64,576]{1,0:T(8,128)(2,1)}, bf16[64,576]{1,0:T(8,128)(2,1)S(1)}, u32[]{:S(2)}, u32[]{:S(2)}) collective-permute-start(bf16[64,576]{1,0:T(8,128)(2,1)} %get-tuple-element.170), channel_id=1, source_target_pairs={{0,4},{1,5},{2,6},{3,7},{4,0},{5,1},{6,2},{7,3},{8,12},{9,13},{10,... | collective-permute-start | bytes 221192 | tf_op jit(solution)/shard_map/ppermute | solution.py:239
  217.1 9.5 %collective-permute-start.38 = (bf16[64,576]{1,0:T(8,128)(2,1)}, bf16[64,576]{1,0:T(8,128)(2,1)S(1)}, u32[]{:S(2)}, u32[]{:S(2)}) collective-permute-start(bf16[64,576]{1,0:T(8,128)(2,1)} %get-tuple-element.171), channel_id=1, source_target_pairs={{0,6},{1,7},{2,0},{3,1},{4,2},{5,3},{6,4},{7,5},{8,14},{9,15},{10,... | collective-permute-start | bytes 221192 | tf_op jit(solution)/shard_map/ppermute | solution.py:239
  222.1 10.5 %collective-permute-start.39 = (bf16[48,768]{1,0:T(8,128)(2,1)}, bf16[48,768]{1,0:T(8,128)(2,1)S(1)}, u32[]{:S(2)}, u32[]{:S(2)}) collective-permute-start(bf16[48,768]{1,0:T(8,128)(2,1)} %get-tuple-element.174), channel_id=1, source_target_pairs={{0,16},{16,0},{1,17},{17,1},{2,18},{18,2},{3,19},{19,3},{4,20},{20... | collective-permute-start | bytes 221192 | tf_op jit(solution)/shard_map/ppermute | solution.py:242
  (65 other events, 323.1 us)
Sparse Core Ops, SparseCore 0:
  15.8 29.3 all-gather.2
  49.1 47.1 all-gather.4
  147.1 42.9 reduce-scatter.1

commit v6 on v5

--- a/solution.py
+++ b/solution.py
@@ -613,14 +613,16 @@
     )(*inputs)
 
 
-def pack_joined(ids, weight, vectors, widen_bias, cols):
+def pack_joined(ids, weight, vectors, widen_bias, tokens, cols):
     kb = weight.shape[0]
     vectors = [item[None] for item in vectors]
     shape = (kb + 16, 3 * cols)
 
     def body(*refs):
         ids_ref, w_ref, wide_ref = refs[0], refs[1], refs[10]
-        all_ref = refs[15]
+        all_ref = refs[17]
+        for g in range(GROUPS):
+            refs[16][g] = refs[11][...]
         rows = [ref[...].astype(F32) for ref in refs[2:10]]
         wide = wide_ref[...].astype(F32)
         rows += [wide[:, k * kb : (k + 1) * kb] for k in range(8)]
@@ -632,14 +634,14 @@
             all_ref[g, kb:, :] = jnp.zeros((16, 3 * cols), BF)
             all_ref[g, kb:, :kb] = small
         for k in range(GROUPS):
-            refs[11 + k][...] = all_ref[(ids_ref[0] + k) % GROUPS]
-
-    inputs = [ids, weight] + vectors + [widen_bias[None]]
+            refs[12 + k][...] = all_ref[(ids_ref[0] + k) % GROUPS]
+
+    inputs = [ids, weight] + vectors + [widen_bias[None], tokens]
     return call(
         body,
         "pack_joined",
         inputs,
-        [(shape, BF)] * GROUPS,
+        [(shape, BF)] * GROUPS + [((GROUPS,) + tokens.shape, BF)],
         scratch=[pltpu.VMEM((GROUPS,) + shape, BF)],
     )
 
@@ -1363,6 +1365,7 @@
             final_shift,
         ],
         widen_bias,
+        inputs,
         cols,
     )
     output_far = after(at.swap(output_weight, "seq"), packed[0])
@@ -1373,7 +1376,7 @@
     )
     output_got = lax.all_gather(output_pair, "ctx", tiled=True)
     joined_rel = [packed[0]] + [at.shift(packed[k], k) for k in range(1, GROUPS)]
-    x_cut = jnp.broadcast_to(after(inputs, *joined_rel)[None], (GROUPS, rows, width))
+    x_cut = after(packed[4], *joined_rel)
     x_four = across(x_cut).reshape(-1, width)
     joined_got = jnp.stack(joined_rel)
     joined_parts = spread_out(joined_got)

time: 242 us -> 241 us (level)
  transfers between devices with their start and end apart: 45 -> 45, of which waited for: 25 -> 25; matrix products, arithmetic and copies ran while one was open for 6% -> 5% of each run, Pallas kernels for 26% -> 26%
where the time goes in v6:
time: 241 us; the launch traced here: 240 us
  Pallas kernels  77.5 us (32%)
  waiting for transfers between devices  66.8 us (28%)
  starting transfers between devices  56.1 us (23%)
  local copies, waits for them, and re-layouts  16.9 us (7%)
  between operations  14.1 us (6%)
  other arithmetic  8.69 us (4%)
    pallas_call x22, Pallas kernels, call(): pl.pallas_call(body, grid=grid, in_specs=in_specs, out_specs=out_specs, o...  77.5 us
    ppermute x17, waiting for transfers between devices, swap(): return lax.ppermute(value, axis, [(0, 1), (1, 0)])  37.2 us
    ppermute x17, starting transfers between devices, swap(): return lax.ppermute(value, axis, [(0, 1), (1, 0)])  20.7 us
    ppermute x12, starting transfers between devices, shift(): lax.ppermute(value, 'ctx', [(i, (i + steps * r) % n) for i in range(n)])  18.8 us
    ppermute x12, waiting for transfers between devices, shift(): lax.ppermute(value, 'ctx', [(i, (i + steps * r) % n) for i in range(n)])  13.6 us
    unnamed x89, local copies, waits for them, and re-layouts  11 us
    all_to_all x2, starting transfers between devices, across(): lax.all_to_all(value, 'ctx', 0, 0, axis_index_groups=columns, tiled=True)  11 us
    ppermute x5, waiting for transfers between devices, plane(): return lax.ppermute(value, ('rep', 'seq'), [(i, 3 - i) for i in range(4)])  5.74 us
  transfers between devices with their start and end apart: 45, of which 25 were waited for; matrix products, arithmetic and copies ran while one was open for 5% of the time, Pallas kernels for 26%

profile of v6, /device:TPU:0, one launch (start us, length us, event | category | flops | bytes accessed | tf_op | source)
XLA Modules:
  0.0 240.1 jit_solution(5695987287956063086)
XLA Ops:
  7.2 3.1 %collective-permute-start.10 = (bf16[48,768]{1,0:T(8,128)(2,1)}, bf16[48,768]{1,0:T(8,128)(2,1)S(1)}, u32[]{:S(2)}, u32[]{:S(2)}) collective-permute-start(bf16[48,768]{1,0:T(8,128)(2,1)} %param.21), channel_id=1, source_target_pairs={{0,8},{8,0},{1,9},{9,1},{2,10},{10,2},{3,11},{11,3},{4,12},{12,4},... | collective-permute-start | bytes 221192 | tf_op jit(solution)/shard_map/ppermute | solution.py:242
  26.1 6.6 %all-to-all-start = ((bf16[4,128,768]{2,1,0:T(8,128)(2,1)}), bf16[4,128,768]{2,1,0:T(8,128)(2,1)S(1)}, u32[]{:S(2)}, u32[]{:S(2)}) async-start(bf16[4,128,768]{2,1,0:T(8,128)(2,1)} %get-tuple-element.102), calls=%async_computation | async-start | bytes 1572864 | tf_op jit(solution)/shard_map/all_to_all | solution.py:1348
  35.1 4.8 %collective-permute-done.3.b_ref = bf16[4,64,576]{2,1,0:T(8,128)(2,1)S(1)} collective-permute-done((bf16[4,64,576]{2,1,0:T(8,128)(2,1)S(1)}, bf16[4,64,576]{2,1,0:T(8,128)(2,1)S(1)}, u32[]{:S(2)}, u32[]{:S(2)}) %collective-permute-start.3) | collective-permute-done | bytes 294944 | tf_op jit(solution)/shard_map/ppermute | solution.py:242
  50.4 4.1 %all-to-all-done = bf16[4,128,768]{2,1,0:T(8,128)(2,1)S(1)} async-done(((bf16[4,128,768]{2,1,0:T(8,128)(2,1)}), bf16[4,128,768]{2,1,0:T(8,128)(2,1)S(1)}, u32[]{:S(2)}, u32[]{:S(2)}) %all-to-all-start) | async-done | bytes 786464 | tf_op jit(solution)/shard_map/all_to_all | solution.py:1348
  55.4 3.1 %split_joined.1 = (bf16[512,192]{1,0:T(8,128)(2,1)}, bf16[512,384]{1,0:T(8,128)(2,1)}) custom-call(bf16[512,768]{1,0:T(8,128)(2,1)} %bitcast.58, bf16[768,576]{1,0:T(8,128)(2,1)} %get-tuple-element.103.w_ref, f32[16,192]{1,0:T(8,128)} %get-tuple-element.104.near_ref), custom_call_target="tpu_custom_call" | custom-call | flops 15000000512 | tf_op jit(solution)/shard_map/split_joined/pallas_call | solution.py:604
  61.2 4.7 %attend.1 = (f32[512,192]{1,0:T(8,128)}, f32[3,8,512]{2,1,0:T(8,128)}, bf16[128,192]{1,0:T(8,128)(2,1)}, bf16[128,192]{1,0:T(8,128)(2,1)}, bf16[128,192]{1,0:T(8,128)(2,1)}, /*index=5*/bf16[128,192]{1,0:T(8,128)(2,1)}) custom-call(s32[4]{0:T(128)} %pad_add_fusion.refs_0_.ids_ref, f32[3]{0:T(128)} %power_multiply_fusion.slope_ref, ...), custom_call_target="tpu_custom_call" | custom-call | flops 24999999488 | tf_op jit(solution)/shard_map/attend/pallas_call | solution.py:604
  74.3 4.1 %collective-permute-done.8.c_ref.refs_2_ = bf16[128,192]{1,0:T(8,128)(2,1)S(1)} collective-permute-done((bf16[128,192]{1,0:T(8,128)(2,1)}, bf16[128,192]{1,0:T(8,128)(2,1)S(1)}, u32[]{:S(2)}, u32[]{:S(2)}) %collective-permute-start.8) | collective-permute-done | bytes 49184 | tf_op jit(solution)/shard_map/ppermute | solution.py:239
  85.4 4.5 %collective-permute-done.11.refs_1_ = bf16[128,768]{1,0:T(8,128)(2,1)S(1)} collective-permute-done((bf16[128,768]{1,0:T(8,128)(2,1)}, bf16[128,768]{1,0:T(8,128)(2,1)S(1)}, u32[]{:S(2)}, u32[]{:S(2)}) %collective-permute-start.11) | collective-permute-done | bytes 196640 | tf_op jit(solution)/shard_map/ppermute | solution.py:242
  89.9 3.9 %collective-permute-done.12.refs_2_ = bf16[128,768]{1,0:T(8,128)(2,1)S(1)} collective-permute-done((bf16[128,768]{1,0:T(8,128)(2,1)}, bf16[128,768]{1,0:T(8,128)(2,1)S(1)}, u32[]{:S(2)}, u32[]{:S(2)}) %collective-permute-start.12) | collective-permute-done | bytes 196640 | tf_op jit(solution)/shard_map/ppermute | solution.py:242
  95.9 5.8 %widen_narrow.1 = (f32[128,768]{1,0:T(8,128)}, bf16[128,768]{1,0:T(8,128)(2,1)}, bf16[128,768]{1,0:T(8,128)(2,1)}, bf16[128,768]{1,0:T(8,128)(2,1)}, bf16[512,76...) custom-call(bf16[128,768]{1,0:T(8,128)(2,1)} %get-tuple-element.113.refs_0_, bf16[128,768]{1,0:T(8,128)(2,1)} %copy-done.26, ...), custom_call_target="tpu_custom_call" | custom-call | flops 30000001024 | tf_op jit(solution)/shard_map/widen_narrow/pallas_call | solution.py:604
  106.1 3.4 %collective-permute-done.15.a_ref = bf16[128,768]{1,0:T(8,128)(2,1)S(1)} collective-permute-done((bf16[128,768]{1,0:T(8,128)(2,1)}, bf16[128,768]{1,0:T(8,128)(2,1)S(1)}, u32[]{:S(2)}, u32[]{:S(2)}) %collective-permute-start.15) | collective-permute-done | bytes 196640 | tf_op jit(solution)/shard_map/ppermute | solution.py:242
  109.6 4.7 %collective-permute-done.16.b_ref = bf16[128,768]{1,0:T(8,128)(2,1)S(1)} collective-permute-done((bf16[128,768]{1,0:T(8,128)(2,1)}, bf16[128,768]{1,0:T(8,128)(2,1)S(1)}, u32[]{:S(2)}, u32[]{:S(2)}) %collective-permute-start.16) | collective-permute-done | bytes 196640 | tf_op jit(solution)/shard_map/ppermute | solution.py:242
  125.8 3.5 %collective-permute-done.19.refs_2_.refs_6_ = bf16[128,768]{1,0:T(8,128)(2,1)S(1)} collective-permute-done((bf16[128,768]{1,0:T(8,128)(2,1)}, bf16[128,768]{1,0:T(8,128)(2,1)S(1)}, u32[]{:S(2)}, u32[]{:S(2)}) %collective-permute-start.19) | collective-permute-done | bytes 196640 | tf_op jit(solution)/shard_map/ppermute | solution.py:242
  130.0 6.9 %widen_narrow_back.1 = (f32[128,768]{1,0:T(8,128)}, bf16[128,768]{1,0:T(8,128)(2,1)}, bf16[128,768]{1,0:T(8,128)(2,1)}, bf16[128,768]{1,0:T(8,128)(2,1)}, bf16[5...) custom-call(bf16[128,768]{1,0:T(8,128)(2,1)} %get-tuple-element.127.refs_0_.refs_4_, bf16[128,768]{1,0:T(8,128)(2,1)} %copy-done.31, ...), custom_call_target="tpu_custom_call" | custom-call | flops 35000000512 | tf_op jit(solution)/shard_map/widen_narrow_back/pallas_call | solution.py:604
  140.4 6.0 %wide_grads.1 = (bf16[768,2304]{1,0:T(8,128)(2,1)}, f32[1,768]{1,0:T(1,128)}, f32[1,768]{1,0:T(1,128)}) custom-call(bf16[128,768]{1,0:T(8,128)(2,1)} %get-tuple-element.113.refs_0_, bf16[128,768]{1,0:T(8,128)(2,1)} %copy-done.26, bf16[128,768]{1,0:T(8,128)(2,1)} %copy-done.27, bf16[128,768]{1,0:T(8,128)(2,1)} %copy-done.28, ...), custom_call_target="tpu_custom_call" | custom-call | flops 30000001024 | tf_op jit(solution)/shard_map/wide_grads/pallas_call | solution.py:604
  147.3 3.4 %turn_first.1 = (f32[128,768]{1,0:T(8,128)}, bf16[128,768]{1,0:T(8,128)(2,1)}, f32[8,768]{1,0:T(8,128)}, bf16[128,192]{1,0:T(8,128)(2,1)}, bf16[128,192]{1,0:T(8...) custom-call(s32[4]{0:T(128)} %pad_add_fusion.refs_0_.ids_ref, f32[128,768]{1,0:T(8,128)} %get-tuple-element.130.own_ref, ...), custom_call_target="tpu_custom_call" | custom-call | flops 15000000512 | tf_op jit(solution)/shard_map/turn_first/pallas_call | solution.py:604
  151.5 3.0 %collective-permute-start.26 = (bf16[128,192]{1,0:T(8,128)(2,1)}, bf16[128,192]{1,0:T(8,128)(2,1)S(1)}, u32[]{:S(2)}, u32[]{:S(2)}) collective-permute-start(bf16[128,192]{1,0:T(8,128)(2,1)} %get-tuple-element.140), channel_id=1, source_target_pairs={{0,6},{1,7},{2,0},{3,1},{4,2},{5,3},{6,4},{7,5},{8,14},{9,15},{10,... | collective-permute-start | bytes 147464 | tf_op jit(solution)/shard_map/ppermute | solution.py:239
  154.5 3.1 %output_grads.1 = (f32[2,4,48,768]{3,2,1,0:T(8,128)}, bf16[2,4,48,768]{3,2,1,0:T(8,128)(2,1)}, f32[16,16,48]{2,1,0:T(8,128)}) custom-call(s32[4]{0:T(128)} %pad_add_fusion.refs_0_.ids_ref, bf16[128,192]{1,0:T(8,128)(2,1)} %get-tuple-element.107.a_ref.refs_0_, bf16[128,192]{1,0:T(8,128)(2,1)} %copy-done.38, bf16[128,192]{1,0:T(8,128)(2,1)} %copy-done.39, ...), custom_call_target="tpu_custom_call" | custom-call | flops 15000000512 | tf_op jit(solution)/shard_map/output_grads/pallas_call | solution.py:604
  161.0 8.0 %attend_back.1 = (bf16[512,192]{1,0:T(8,128)(2,1)}, f32[512,384]{1,0:T(8,128)}, bf16[512,384]{1,0:T(8,128)(2,1)}) custom-call(s32[4]{0:T(128)} %pad_add_fusion.refs_0_.ids_ref, f32[3]{0:T(128)} %power_multiply_fusion.slope_ref, bf16[512,192]{1,0:T(8,128)(2,1)} %get-tuple-element.105.q_ref, bf16[128,192]{1,0:T(8,128)(2,1)} %get-tuple-element.137.refs_0_, ...), custom_call_target="tpu_custom_call" | custom-call | flops 40000000000 | tf_op jit(solution)/shard_map/attend_back/pallas_call | solution.py:604
  171.9 4.4 %joined_grads.1 = (f32[2,4,64,576]{3,2,1,0:T(8,128)}, bf16[2,4,64,576]{3,2,1,0:T(8,128)(2,1)}, bf16[512,576]{1,0:T(8,128)(2,1)}) custom-call(s32[4]{0:T(128)} %pad_add_fusion.refs_0_.ids_ref, bf16[512,768]{1,0:T(8,128)(2,1)} %bitcast.59, bf16[512,192]{1,0:T(8,128)(2,1)} %get-tuple-element.143.q_ref, f32[512,384]{1,0:T(8,128)} %get-tuple-element.144.kv_ref, ...), custom_call_target="tpu_custom_call" | custom-call | flops 20000000000 | tf_op jit(solution)/shard_map/joined_grads/pallas_call | solution.py:604
  179.4 4.1 %tokens_parts.1 = bf16[4,176,768]{2,1,0:T(8,128)(2,1)} custom-call(bf16[512,576]{1,0:T(8,128)(2,1)} %get-tuple-element.155.jb_ref, bf16[768,576]{1,0:T(8,128)(2,1)} %get-tuple-element.103.w_ref, f32[2,4,48,768]{3,2,1,0:T(8,128)} %get-tuple-element.156.keep_ref, bf16[2,4,48,768]{3,2,1,0:T(8,128)(2,1)} %copy-done.4, bf16[4,48,768]{2,1,0:T(8,128)(2,1)} %copy-done.13), custom_call_target="tpu_custom_call" | custom-call | tf_op jit(solution)/shard_map/tokens_parts/pallas_call | solution.py:604
  183.5 4.4 %all-to-all-start.1 = ((bf16[4,176,768]{2,1,0:T(8,128)(2,1)}), bf16[4,176,768]{2,1,0:T(8,128)(2,1)S(1)}, u32[]{:S(2)}, u32[]{:S(2)}) async-start(bf16[4,176,768]{2,1,0:T(8,128)(2,1)} %tokens_parts.1), calls=%async_computation.1 | async-start | bytes 2162688 | tf_op jit(solution)/shard_map/all_to_all | solution.py:1348
  193.1 4.1 %collective-permute-done.34 = bf16[4,64,576]{2,1,0:T(8,128)(2,1)} collective-permute-done((bf16[4,64,576]{2,1,0:T(8,128)(2,1)S(1)}, bf16[4,64,576]{2,1,0:T(8,128)(2,1)}, u32[]{:S(2)}, u32[]{:S(2)}) %collective-permute-start.34) | collective-permute-done | bytes 294944 | tf_op jit(solution)/shard_map/ppermute | solution.py:242
  204.4 5.7 %collective-permute-done.33.refs_3_ = bf16[48,1536]{1,0:T(8,128)(2,1)S(1)} collective-permute-done((bf16[48,1536]{1,0:T(8,128)(2,1)S(1)}, bf16[48,1536]{1,0:T(8,128)(2,1)S(1)}, u32[]{:S(2)}, u32[]{:S(2)}) %collective-permute-start.33) | collective-permute-done | bytes 147488 | tf_op jit(solution)/shard_map/ppermute | solution.py:246
  (204 shorter events, 116.7 us)
Async XLA Ops:
  7.2 62.6 %all-gather.3.cloned.1.call-start = ((), (), s32[]{:S(2)}) async-start(), calls=%async_computation.3 | async-start | bytes 1327104 | tf_op jit(solution)/shard_map/all_gather | solution.py:1377
  26.1 28.5 %all-to-all-start = ((bf16[4,128,768]{2,1,0:T(8,128)(2,1)}), bf16[4,128,768]{2,1,0:T(8,128)(2,1)S(1)}, u32[]{:S(2)}, u32[]{:S(2)}) async-start(bf16[4,128,768]{2,1,0:T(8,128)(2,1)} %get-tuple-element.102), calls=%async_computation | async-start | bytes 1572864 | tf_op jit(solution)/shard_map/all_to_all | solution.py:1348
  32.7 63.2 %all-gather.5.cloned.1.call-start = ((), (), s32[]{:S(2)}) async-start(), calls=%async_computation.4 | async-start | bytes 3981312 | tf_op jit(solution)/shard_map/all_gather | solution.py:1387
  48.9 140.6 %reduce-scatter.2.cloned.1.call-start = ((), (), s32[]{:S(2)}) async-start(), calls=%async_computation.5 | async-start | bytes 3981312 | tf_op jit(solution)/shard_map/reduce_scatter | solution.py:1429
  65.9 12.4 %collective-permute-start.8 = (bf16[128,192]{1,0:T(8,128)(2,1)}, bf16[128,192]{1,0:T(8,128)(2,1)S(1)}, u32[]{:S(2)}, u32[]{:S(2)}) collective-permute-start(bf16[128,192]{1,0:T(8,128)(2,1)} %get-tuple-element.109), channel_id=1, source_target_pairs={{0,4},{1,5},{2,6},{3,7},{4,0},{5,1},{6,2},{7,3},{8,12},{9,13},{10,... | collective-permute-start | bytes 147464 | tf_op jit(solution)/shard_map/ppermute | solution.py:239
  68.1 10.3 %collective-permute-start.9 = (bf16[128,192]{1,0:T(8,128)(2,1)}, bf16[128,192]{1,0:T(8,128)(2,1)S(1)}, u32[]{:S(2)}, u32[]{:S(2)}) collective-permute-start(bf16[128,192]{1,0:T(8,128)(2,1)} %get-tuple-element.110), channel_id=1, source_target_pairs={{0,6},{1,7},{2,0},{3,1},{4,2},{5,3},{6,4},{7,5},{8,14},{9,15},{10,... | collective-permute-start | bytes 147464 | tf_op jit(solution)/shard_map/ppermute | solution.py:239
  83.3 10.5 %collective-permute-start.12 = (bf16[128,768]{1,0:T(8,128)(2,1)}, bf16[128,768]{1,0:T(8,128)(2,1)S(1)}, u32[]{:S(2)}, u32[]{:S(2)}) collective-permute-start(bf16[128,768]{1,0:T(8,128)(2,1)} %get-tuple-element.113.refs_0_), channel_id=1, source_target_pairs={{0,8},{8,0},{1,9},{9,1},{2,10},{10,2},{3,11},{11,3},{4,12},{12,4},... | collective-permute-start | bytes 589832 | tf_op jit(solution)/shard_map/ppermute | solution.py:242
  103.1 11.2 %collective-permute-start.16 = (bf16[128,768]{1,0:T(8,128)(2,1)}, bf16[128,768]{1,0:T(8,128)(2,1)S(1)}, u32[]{:S(2)}, u32[]{:S(2)}) collective-permute-start(bf16[128,768]{1,0:T(8,128)(2,1)} %get-tuple-element.123), channel_id=1, source_target_pairs={{0,8},{8,0},{1,9},{9,1},{2,10},{10,2},{3,11},{11,3},{4,12},{12,4},... | collective-permute-start | bytes 589832 | tf_op jit(solution)/shard_map/ppermute | solution.py:242
  104.6 9.7 %collective-permute-start.17 = (bf16[128,768]{1,0:T(8,128)(2,1)}, bf16[128,768]{1,0:T(8,128)(2,1)S(1)}, u32[]{:S(2)}, u32[]{:S(2)}) collective-permute-start(bf16[128,768]{1,0:T(8,128)(2,1)} %get-tuple-element.124), channel_id=1, source_target_pairs={{0,24},{8,16},{16,8},{24,0},{1,25},{9,17},{17,9},{25,1},{2,26},{10... | collective-permute-start | bytes 589832 | tf_op jit(solution)/shard_map/ppermute | solution.py:246
  119.0 10.3 %collective-permute-start.19 = (bf16[128,768]{1,0:T(8,128)(2,1)}, bf16[128,768]{1,0:T(8,128)(2,1)S(1)}, u32[]{:S(2)}, u32[]{:S(2)}) collective-permute-start(bf16[128,768]{1,0:T(8,128)(2,1)} %get-tuple-element.127.refs_0_.refs_4_), channel_id=1, source_target_pairs={{0,8},{8,0},{1,9},{9,1},{2,10},{10,2},{3,11},{11,3},{4,12},{12,4},... | collective-permute-start | bytes 589832 | tf_op jit(solution)/shard_map/ppermute | solution.py:242
  119.9 9.4 %collective-permute-start.20 = (bf16[128,768]{1,0:T(8,128)(2,1)}, bf16[128,768]{1,0:T(8,128)(2,1)}, u32[]{:S(2)}, u32[]{:S(2)}) collective-permute-start(bf16[128,768]{1,0:T(8,128)(2,1)} %get-tuple-element.127.refs_0_.refs_4_), channel_id=1, source_target_pairs={{0,24},{8,16},{16,8},{24,0},{1,25},{9,17},{17,9},{25,1},{2,26},{10... | collective-permute-start | bytes 589832 | tf_op jit(solution)/shard_map/ppermute | solution.py:246
  136.9 9.6 %collective-permute-start.21 = (bf16[128,768]{1,0:T(8,128)(2,1)}, bf16[128,768]{1,0:T(8,128)(2,1)S(1)}, u32[]{:S(2)}, u32[]{:S(2)}) collective-permute-start(bf16[128,768]{1,0:T(8,128)(2,1)} %get-tuple-element.131), channel_id=1, source_target_pairs={{0,16},{16,0},{1,17},{17,1},{2,18},{18,2},{3,19},{19,3},{4,20},{20... | collective-permute-start | bytes 589832 | tf_op jit(solution)/shard_map/ppermute | solution.py:242
  157.5 11.6 %collective-permute-start.28 = (bf16[2,4,48,768]{3,2,1,0:T(8,128)(2,1)}, bf16[2,4,48,768]{3,2,1,0:T(8,128)(2,1)S(1)}, u32[]{:S(2)}, u32[]{:S(2)}) collective-permute-start(bf16[2,4,48,768]{3,2,1,0:T(8,128)(2,1)} %get-tuple-element.157), channel_id=1, source_target_pairs={{0,1},{1,0},{2,3},{3,2},{4,5},{5,4},{6,7},{7,6},{8,9},{9,8},{10,11... | collective-permute-start | bytes 1769480 | tf_op jit(solution)/shard_map/ppermute | solution.py:279
  169.2 9.5 %collective-permute-start.29 = (bf16[4,48,768]{2,1,0:T(8,128)(2,1)S(1)}, bf16[4,48,768]{2,1,0:T(8,128)(2,1)S(1)}, u32[]{:S(2)}, u32[]{:S(2)}) collective-permute-start(bf16[4,48,768]{2,1,0:T(8,128)(2,1)S(1)} %fusion.7), channel_id=1, source_target_pairs={{0,8},{8,0},{1,9},{9,1},{2,10},{10,2},{3,11},{11,3},{4,12},{12,4},... | collective-permute-start | bytes 884744 | tf_op jit(solution)/shard_map/ppermute | solution.py:242
  176.3 11.6 %collective-permute-start.30 = (bf16[2,4,64,576]{3,2,1,0:T(8,128)(2,1)}, bf16[2,4,64,576]{3,2,1,0:T(8,128)(2,1)S(1)}, u32[]{:S(2)}, u32[]{:S(2)}) collective-permute-start(bf16[2,4,64,576]{3,2,1,0:T(8,128)(2,1)} %get-tuple-element.161), channel_id=1, source_target_pairs={{0,1},{1,0},{2,3},{3,2},{4,5},{5,4},{6,7},{7,6},{8,9},{9,8},{10,11... | collective-permute-start | bytes 1769480 | tf_op jit(solution)/shard_map/ppermute | solution.py:279
  183.5 34.9 %all-to-all-start.1 = ((bf16[4,176,768]{2,1,0:T(8,128)(2,1)}), bf16[4,176,768]{2,1,0:T(8,128)(2,1)S(1)}, u32[]{:S(2)}, u32[]{:S(2)}) async-start(bf16[4,176,768]{2,1,0:T(8,128)(2,1)} %tokens_parts.1), calls=%async_computation.1 | async-start | bytes 2162688 | tf_op jit(solution)/shard_map/all_to_all | solution.py:1348
  187.9 9.2 %collective-permute-start.34 = (bf16[4,64,576]{2,1,0:T(8,128)(2,1)S(1)}, bf16[4,64,576]{2,1,0:T(8,128)(2,1)}, u32[]{:S(2)}, u32[]{:S(2)}) collective-permute-start(bf16[4,64,576]{2,1,0:T(8,128)(2,1)S(1)} %fusion.6), channel_id=1, source_target_pairs={{0,8},{8,0},{1,9},{9,1},{2,10},{10,2},{3,11},{11,3},{4,12},{12,4},... | collective-permute-start | bytes 884744 | tf_op jit(solution)/shard_map/ppermute | solution.py:242
  191.4 18.8 %collective-permute-start.31 = (bf16[48,3072]{1,0:T(8,128)(2,1)}, bf16[48,3072]{1,0:T(8,128)(2,1)}, u32[]{:S(2)}, u32[]{:S(2)}) collective-permute-start(bf16[48,3072]{1,0:T(8,128)(2,1)} %get-tuple-element.163.refs_0_), channel_id=1, source_target_pairs={{0,16},{16,0},{1,17},{17,1},{2,18},{18,2},{3,19},{19,3},{4,20},{20... | collective-permute-start | bytes 884744 | tf_op jit(solution)/shard_map/ppermute | solution.py:242
  198.3 11.9 %collective-permute-start.35 = (bf16[4,64,576]{2,1,0:T(8,128)(2,1)S(1)}, bf16[4,64,576]{2,1,0:T(8,128)(2,1)S(1)}, u32[]{:S(2)}, u32[]{:S(2)}) collective-permute-start(bf16[4,64,576]{2,1,0:T(8,128)(2,1)S(1)} %fusion.5.own_ref), channel_id=1, source_target_pairs={{0,16},{16,0},{1,17},{17,1},{2,18},{18,2},{3,19},{19,3},{4,20},{20... | collective-permute-start | bytes 884744 | tf_op jit(solution)/shard_map/ppermute | solution.py:242
  200.4 9.7 %collective-permute-start.33 = (bf16[48,1536]{1,0:T(8,128)(2,1)S(1)}, bf16[48,1536]{1,0:T(8,128)(2,1)S(1)}, u32[]{:S(2)}, u32[]{:S(2)}) collective-permute-start(bf16[48,1536]{1,0:T(8,128)(2,1)S(1)} %copy-done.37), channel_id=1, source_target_pairs={{0,24},{8,16},{16,8},{24,0},{1,25},{9,17},{17,9},{25,1},{2,26},{10... | collective-permute-start | bytes 442376 | tf_op jit(solution)/shard_map/ppermute | solution.py:246
  212.8 13.2 %collective-permute-start.36 = (bf16[64,576]{1,0:T(8,128)(2,1)}, bf16[64,576]{1,0:T(8,128)(2,1)S(1)}, u32[]{:S(2)}, u32[]{:S(2)}) collective-permute-start(bf16[64,576]{1,0:T(8,128)(2,1)} %get-tuple-element.171), channel_id=1, source_target_pairs={{0,2},{1,3},{2,4},{3,5},{4,6},{5,7},{6,0},{7,1},{8,10},{9,11},{10,... | collective-permute-start | bytes 221192 | tf_op jit(solution)/shard_map/ppermute | solution.py:239
  215.4 10.6 %collective-permute-start.37 = (bf16[64,576]{1,0:T(8,128)(2,1)}, bf16[64,576]{1,0:T(8,128)(2,1)S(1)}, u32[]{:S(2)}, u32[]{:S(2)}) collective-permute-start(bf16[64,576]{1,0:T(8,128)(2,1)} %get-tuple-element.172), channel_id=1, source_target_pairs={{0,4},{1,5},{2,6},{3,7},{4,0},{5,1},{6,2},{7,3},{8,12},{9,13},{10,... | collective-permute-start | bytes 221192 | tf_op jit(solution)/shard_map/ppermute | solution.py:239
  216.6 9.4 %collective-permute-start.38 = (bf16[64,576]{1,0:T(8,128)(2,1)}, bf16[64,576]{1,0:T(8,128)(2,1)S(1)}, u32[]{:S(2)}, u32[]{:S(2)}) collective-permute-start(bf16[64,576]{1,0:T(8,128)(2,1)} %get-tuple-element.173), channel_id=1, source_target_pairs={{0,6},{1,7},{2,0},{3,1},{4,2},{5,3},{6,4},{7,5},{8,14},{9,15},{10,... | collective-permute-start | bytes 221192 | tf_op jit(solution)/shard_map/ppermute | solution.py:239
  221.5 10.5 %collective-permute-start.39 = (bf16[48,768]{1,0:T(8,128)(2,1)}, bf16[48,768]{1,0:T(8,128)(2,1)S(1)}, u32[]{:S(2)}, u32[]{:S(2)}) collective-permute-start(bf16[48,768]{1,0:T(8,128)(2,1)} %get-tuple-element.176), channel_id=1, source_target_pairs={{0,16},{16,0},{1,17},{17,1},{2,18},{18,2},{3,19},{19,3},{4,20},{20... | collective-permute-start | bytes 221192 | tf_op jit(solution)/shard_map/ppermute | solution.py:242
  (65 other events, 334.8 us)
Sparse Core Ops, SparseCore 0:
  16.2 29.6 all-gather.2
  49.0 46.7 all-gather.4
  146.6 42.9 reduce-scatter.1
